TPU v7x, 32 devices: a whole 2x2x4 slice. The times are simulated.
32 devices in a mesh: tm: 8 (over y, x, core), space: 4 (over z).
Axes of the slice: x: 2, y: 2, z: 4, core: 2. Of those that a mesh axis runs over, the one named last changes fastest.
Arguments:
- initial_state: float32 [192, 512], P('space'), may hold values from -6 to 6
- velocity: bfloat16 [192, 512], P('space'), may hold values from -0.5 to 0.5
- diffusion: bfloat16 [192, 512], P('space'), may hold values from 0.25 to 0.5
- forcing: bfloat16 [64, 192, 512], P('tm', 'space'), may hold values from -6 to 6
- implicit: float32 [512, 512], replicated, may hold values from 0 to 1
- coarse_implicit: float32 [512, 512], replicated, may hold values from 0 to 1
Outputs:
- solution: float32 [64, 192, 512], P('tm', 'space')
All inputs are finite; a program needn't handle non-finite values.
Results may differ from a plain program's by a relative error of at most 0.0003.
Values may be sent and summed in bfloat16 or wider, within the bound.
No kernel may reach another device: no remote copies, remote signals or barrier semaphores. Data moves between devices by JAX's collectives and lax.ppermute only.
A program may use at most 64 MiB of HBM per device.

v0:
```python
import jax
import jax.numpy as jnp
from jax import lax
from jax.sharding import PartitionSpec as P

CYCLES = 2


HIGHEST = lax.Precision.HIGHEST


def with_halo(cells, sides, width):
    for axis, dim in sides:
        count = lax.axis_size(axis)
        head = lax.slice_in_dim(cells, 0, width, axis=dim)
        tail = lax.slice_in_dim(cells, cells.shape[dim] - width, cells.shape[dim], axis=dim)
        cells = jnp.concatenate(
            [
                lax.ppermute(tail, axis, [(i, (i + 1) % count) for i in range(count)]),
                cells,
                lax.ppermute(head, axis, [((i + 1) % count, i) for i in range(count)]),
            ],
            axis=dim,
        )
    return cells


def from_behind(block, axis, distance):
    devices = range(lax.axis_size(axis))
    route = [(i - distance, i) for i in devices if i - distance in devices]
    return lax.ppermute(block, axis, route)


def stencil_weights(velocity, diffusion):
    moving = velocity.astype(jnp.float32)
    spread = diffusion.astype(jnp.float32)
    return (spread + 0.5 * moving, 1.0 - 2.0 * spread, spread - 0.5 * moving)


def apply_matrix(field, matrix):
    return jnp.dot(field, matrix, precision=HIGHEST, preferred_element_type=jnp.float32)


def per_device(initial_state, velocity, diffusion, forcing, implicit, coarse_implicit):
    slab_rows = initial_state.shape[0]
    block_steps = forcing.shape[0]
    first_block = lax.axis_index("tm") == 0
    stacked = jnp.concatenate([forcing, velocity[None], diffusion[None]], axis=0)
    sources = with_halo(stacked, (("space", 1),), block_steps)
    wide_weights = stencil_weights(sources[block_steps], sources[block_steps + 1])
    wide_forcing = sources[:block_steps]

    def relax_block(begin_state, step_count):
        values = []
        current = with_halo(begin_state, (("space", 0),), block_steps)
        width_all = current.shape[0]
        for offset in range(1, step_count + 1):
            upper_edge = width_all - offset
            summed = (
                wide_weights[1][offset:upper_edge] * current[1:-1]
                + wide_weights[2][offset:upper_edge] * current[2:]
                + wide_weights[0][offset:upper_edge] * current[:-2]
                + wide_forcing[offset - 1, offset:upper_edge].astype(jnp.float32)
            )
            current = apply_matrix(summed, implicit)
            values.append(current[block_steps - offset : block_steps - offset + slab_rows])
        return values

    def previous(end_values):
        arrived = from_behind(end_values, "tm", 1)
        return jnp.where(first_block, initial_state, arrived)

    end_values = jnp.zeros_like(initial_state)
    for repeat in range(CYCLES):
        if repeat == 0:
            begin_state = jnp.where(first_block, initial_state, jnp.zeros_like(initial_state))
        else:
            begin_state = previous(end_values)
        end_values = relax_block(begin_state, block_steps)[-1]
        residual = relax_block(previous(end_values), block_steps)[-1] - end_values
        gathered = lax.all_gather(
            residual[None].astype(jnp.bfloat16), "tm", axis=0, tiled=True
        ).astype(jnp.float32)

        def coarse_turn(source, carried):
            return apply_matrix(carried, coarse_implicit) + gathered[source]

        end_values = end_values + lax.fori_loop(
            1, lax.axis_index("tm") + 1, coarse_turn, gathered[0]
        )
    values = relax_block(previous(end_values), block_steps - 1)
    return jnp.stack(values + [end_values], axis=0)


def solution(mesh):
    in_specs = (
        P("space", None),
        P("space", None),
        P("space", None),
        P("tm", "space", None),
        P(),
        P(),
    )
    out_specs = P("tm", "space", None)
    return jax.shard_map(
        per_device, mesh=mesh, in_specs=in_specs, out_specs=out_specs, check_vma=False
    )
```

profile of v0, /device:TPU:6, one launch (start us, length us, event | category | flops | bytes accessed | tf_op | source)
XLA Modules:
  0.0 139.8 jit_solution(8762002623819105948)
XLA Ops:
  0.1 3.7 %collective-permute-start.3 = (f32[8,512]{1,0:T(8,128)S(1)}, f32[8,512]{1,0:T(8,128)S(1)}, u32[]{:S(2)}, u32[]{:S(2)}) collective-permute-start(f32[8,512]{1,0:T(8,128)S(1)} %get-tuple-element.102), channel_id=1, source_target_pairs={{1,0},{2,1},{3,2},{0,3},{5,4},{6,5},{7,6},{4,7},{9,8},{10,9},{11,1... | collective-permute-start | bytes 49160 | tf_op jit(solution)/shard_map/ppermute | solution.py:21
  4.7 3.9 %collective-permute-start.1 = (bf16[10,8,512]{2,1,0:T(8,128)(2,1)S(1)}, bf16[10,8,512]{2,1,0:T(8,128)(2,1)S(1)}, u32[]{:S(2)}, u32[]{:S(2)}) collective-permute-start(bf16[10,8,512]{2,1,0:T(8,128)(2,1)S(1)} %get-tuple-element.89), channel_id=1, source_target_pairs={{1,0},{2,1},{3,2},{0,3},{5,4},{6,5},{7,6},{4,7},{9,8},{10,9},{11,1... | collective-permute-start | bytes 245768 | tf_op jit(solution)/shard_map/ppermute | solution.py:21
  10.6 4.2 %collective-permute-done = bf16[10,8,512]{2,1,0:T(8,128)(2,1)S(1)} collective-permute-done((bf16[10,8,512]{2,1,0:T(8,128)(2,1)S(1)}, bf16[10,8,512]{2,1,0:T(8,128)(2,1)S(1)}, u32[]{:S(2)}, u32[]{:S(2)}) %collective-permute-start) | collective-permute-done | bytes 81952 | tf_op jit(solution)/shard_map/ppermute | solution.py:19
  22.2 1.9 %collective-permute-start.4 = (f32[48,512]{1,0:T(8,128)S(1)}, f32[48,512]{1,0:T(8,128)S(1)}, u32[]{:S(2)}, u32[]{:S(2)}) collective-permute-start(f32[48,512]{1,0:T(8,128)S(1)} %fusion.182), channel_id=1, source_target_pairs={{0,4},{4,8},{8,12},{12,16},{16,20},{20,24},{24,28},{1,5},{5,9},{9,... | collective-permute-start | bytes 294920 | tf_op jit(solution)/shard_map/ppermute | solution.py:31
  24.1 4.0 %collective-permute-done.4 = f32[48,512]{1,0:T(8,128)S(1)} collective-permute-done((f32[48,512]{1,0:T(8,128)S(1)}, f32[48,512]{1,0:T(8,128)S(1)}, u32[]{:S(2)}, u32[]{:S(2)}) %collective-permute-start.4) | collective-permute-done | bytes 98336 | tf_op jit(solution)/shard_map/ppermute | solution.py:31
  28.3 2.0 %collective-permute-start.5 = (f32[8,512]{1,0:T(8,128)S(1)}, f32[8,512]{1,0:T(8,128)S(1)}, u32[]{:S(2)}, u32[]{:S(2)}) collective-permute-start(f32[8,512]{1,0:T(8,128)S(1)} %get-tuple-element.99), channel_id=1, source_target_pairs={{0,1},{1,2},{2,3},{3,0},{4,5},{5,6},{6,7},{7,4},{8,9},{9,10},{10,1... | collective-permute-start | bytes 49160 | tf_op jit(solution)/shard_map/ppermute | solution.py:19
  30.2 1.7 %collective-permute-done.6 = f32[8,512]{1,0:T(8,128)S(1)} collective-permute-done((f32[8,512]{1,0:T(8,128)S(1)}, f32[8,512]{1,0:T(8,128)S(1)}, u32[]{:S(2)}, u32[]{:S(2)}) %collective-permute-start.6) | collective-permute-done | bytes 16416 | tf_op jit(solution)/shard_map/ppermute | solution.py:21
  31.9 1.9 %collective-permute-done.5 = f32[8,512]{1,0:T(8,128)S(1)} collective-permute-done((f32[8,512]{1,0:T(8,128)S(1)}, f32[8,512]{1,0:T(8,128)S(1)}, u32[]{:S(2)}, u32[]{:S(2)}) %collective-permute-start.5) | collective-permute-done | bytes 16416 | tf_op jit(solution)/shard_map/ppermute | solution.py:19
  40.3 9.8 %all-gather = bf16[384,512]{1,0:T(8,128)(2,1)S(1)} all-gather(bf16[48,512]{1,0:T(8,128)(2,1)S(1)} %fusion.1), channel_id=2, replica_groups=mesh['tm'=8,'space'=4] {'tm'}, dimensions={0}, use_global_device_ids=true | all-gather | bytes 442368 | tf_op jit(solution)/shard_map/all_gather | solution.py:81
  51.1 10.0 %while.20 = (s32[]{:T(128)}, f32[48,512]{1,0:T(8,128)S(1)}, s32[]{:T(128)}, f32[512,512]{1,0:T(8,128)S(1)}, f32[8,48,512]{2,1,0:T(8,128)}, /*index=5*/s32[]{:T(128)}, s32[]{:T(128)}, s32[]{:T(128)}) while((s32[]{:T(128)}, f32[48,512]{1,0:T(8,128)S(1)}, s32[]{:T(128)}, f32[512,512]{1,0:T(8,128)S(1)}, f32[8,48,512]{2,1,0:T(8,128)}, ...), condition=%wide.region_1.2_spmd, body=%wide.region_0.1_spmd.sunk | while | flops 151019520 | bytes 1540227 | solution.py:88
  51.2 1.6 %convolution_add_fusion.4 = f32[48,512]{1,0:T(8,128)S(1)} fusion(f32[48,512]{1,0:T(8,128)S(1)} %copy.28, f32[512,512]{1,0:T(8,128)S(1)} %get-tuple-element.190, f32[8,48,512]{2,1,0:T(8,128)} %get-tuple-element.191, s32[]{:T(128)S(6)} %select_n.48), kind=kOutput, calls=%fused_computation.clone.1 | convolution fusion | flops 151019520 | bytes 1343492 | tf_op jit(solution)/shard_map/while/body/dot_general | solution.py:41
  54.5 1.6 %convolution_add_fusion.4 = f32[48,512]{1,0:T(8,128)S(1)} fusion(f32[48,512]{1,0:T(8,128)S(1)} %copy.28, f32[512,512]{1,0:T(8,128)S(1)} %get-tuple-element.190, f32[8,48,512]{2,1,0:T(8,128)} %get-tuple-element.191, s32[]{:T(128)S(6)} %select_n.48), kind=kOutput, calls=%fused_computation.clone.1 | convolution fusion | flops 151019520 | bytes 1343492 | tf_op jit(solution)/shard_map/while/body/dot_general | solution.py:41
  59.5 1.6 %convolution_add_fusion.4 = f32[48,512]{1,0:T(8,128)S(1)} fusion(f32[48,512]{1,0:T(8,128)S(1)} %copy.28, f32[512,512]{1,0:T(8,128)S(1)} %get-tuple-element.190, f32[8,48,512]{2,1,0:T(8,128)} %get-tuple-element.191, s32[]{:T(128)S(6)} %select_n.48), kind=kOutput, calls=%fused_computation.clone.1 | convolution fusion | flops 151019520 | bytes 1343492 | tf_op jit(solution)/shard_map/while/body/dot_general | solution.py:41
  62.0 3.9 %collective-permute-start.7 = (f32[48,512]{1,0:T(8,128)S(1)}, f32[48,512]{1,0:T(8,128)S(1)}, u32[]{:S(2)}, u32[]{:S(2)}) collective-permute-start(f32[48,512]{1,0:T(8,128)S(1)} %add.433), channel_id=1, source_target_pairs={{0,4},{4,8},{8,12},{12,16},{16,20},{20,24},{24,28},{1,5},{5,9},{9,... | collective-permute-start | bytes 294920 | tf_op jit(solution)/shard_map/ppermute | solution.py:31
  66.0 2.0 %collective-permute-done.7 = f32[48,512]{1,0:T(8,128)S(1)} collective-permute-done((f32[48,512]{1,0:T(8,128)S(1)}, f32[48,512]{1,0:T(8,128)S(1)}, u32[]{:S(2)}, u32[]{:S(2)}) %collective-permute-start.7) | collective-permute-done | bytes 98336 | tf_op jit(solution)/shard_map/ppermute | solution.py:31
  68.1 2.0 %collective-permute-start.8 = (f32[8,512]{1,0:T(8,128)S(1)}, f32[8,512]{1,0:T(8,128)S(1)}, u32[]{:S(2)}, u32[]{:S(2)}) collective-permute-start(f32[8,512]{1,0:T(8,128)S(1)} %get-tuple-element.97), channel_id=1, source_target_pairs={{0,1},{1,2},{2,3},{3,0},{4,5},{5,6},{6,7},{7,4},{8,9},{9,10},{10,1... | collective-permute-start | bytes 49160 | tf_op jit(solution)/shard_map/ppermute | solution.py:19
  70.1 1.7 %collective-permute-done.9 = f32[8,512]{1,0:T(8,128)S(1)} collective-permute-done((f32[8,512]{1,0:T(8,128)S(1)}, f32[8,512]{1,0:T(8,128)S(1)}, u32[]{:S(2)}, u32[]{:S(2)}) %collective-permute-start.9) | collective-permute-done | bytes 16416 | tf_op jit(solution)/shard_map/ppermute | solution.py:21
  71.8 1.9 %collective-permute-done.8 = f32[8,512]{1,0:T(8,128)S(1)} collective-permute-done((f32[8,512]{1,0:T(8,128)S(1)}, f32[8,512]{1,0:T(8,128)S(1)}, u32[]{:S(2)}, u32[]{:S(2)}) %collective-permute-start.8) | collective-permute-done | bytes 16416 | tf_op jit(solution)/shard_map/ppermute | solution.py:19
  80.2 1.9 %collective-permute-start.10 = (f32[48,512]{1,0:T(8,128)S(1)}, f32[48,512]{1,0:T(8,128)S(1)}, u32[]{:S(2)}, u32[]{:S(2)}) collective-permute-start(f32[48,512]{1,0:T(8,128)S(1)} %fusion.183), channel_id=1, source_target_pairs={{0,4},{4,8},{8,12},{12,16},{16,20},{20,24},{24,28},{1,5},{5,9},{9,... | collective-permute-start | bytes 294920 | tf_op jit(solution)/shard_map/ppermute | solution.py:31
  82.1 4.0 %collective-permute-done.10 = f32[48,512]{1,0:T(8,128)S(1)} collective-permute-done((f32[48,512]{1,0:T(8,128)S(1)}, f32[48,512]{1,0:T(8,128)S(1)}, u32[]{:S(2)}, u32[]{:S(2)}) %collective-permute-start.10) | collective-permute-done | bytes 98336 | tf_op jit(solution)/shard_map/ppermute | solution.py:31
  87.5 2.0 %collective-permute-start.11 = (f32[8,512]{1,0:T(8,128)S(1)}, f32[8,512]{1,0:T(8,128)S(1)}, u32[]{:S(2)}, u32[]{:S(2)}) collective-permute-start(f32[8,512]{1,0:T(8,128)S(1)} %get-tuple-element.95), channel_id=1, source_target_pairs={{0,1},{1,2},{2,3},{3,0},{4,5},{5,6},{6,7},{7,4},{8,9},{9,10},{10,1... | collective-permute-start | bytes 49160 | tf_op jit(solution)/shard_map/ppermute | solution.py:19
  89.4 1.9 %collective-permute-done.12 = f32[8,512]{1,0:T(8,128)S(1)} collective-permute-done((f32[8,512]{1,0:T(8,128)}, f32[8,512]{1,0:T(8,128)S(1)}, u32[]{:S(2)}, u32[]{:S(2)}) %collective-permute-start.12) | collective-permute-done | bytes 16416 | tf_op jit(solution)/shard_map/ppermute | solution.py:21
  91.3 1.7 %collective-permute-done.11 = f32[8,512]{1,0:T(8,128)S(1)} collective-permute-done((f32[8,512]{1,0:T(8,128)S(1)}, f32[8,512]{1,0:T(8,128)S(1)}, u32[]{:S(2)}, u32[]{:S(2)}) %collective-permute-start.11) | collective-permute-done | bytes 16416 | tf_op jit(solution)/shard_map/ppermute | solution.py:19
  100.4 8.4 %all-gather.1 = bf16[384,512]{1,0:T(8,128)(2,1)S(1)} all-gather(bf16[48,512]{1,0:T(8,128)(2,1)S(1)} %fusion.2), channel_id=3, replica_groups=mesh['tm'=8,'space'=4] {'tm'}, dimensions={0}, use_global_device_ids=true | all-gather | bytes 442368 | tf_op jit(solution)/shard_map/all_gather | solution.py:81
  109.7 10.0 %while.21 = (s32[]{:T(128)}, f32[48,512]{1,0:T(8,128)S(1)}, s32[]{:T(128)}, f32[512,512]{1,0:T(8,128)S(1)}, f32[8,48,512]{2,1,0:T(8,128)}, /*index=5*/s32[]{:T(128)}, s32[]{:T(128)}, s32[]{:T(128)}) while((s32[]{:T(128)}, f32[48,512]{1,0:T(8,128)S(1)}, s32[]{:T(128)}, f32[512,512]{1,0:T(8,128)S(1)}, f32[8,48,512]{2,1,0:T(8,128)}, ...), condition=%wide.region_3.4_spmd, body=%wide.region_2.3_spmd.sunk | while | flops 151019520 | bytes 1540227 | solution.py:88
  113.1 1.6 %convolution_add_fusion.5 = f32[48,512]{1,0:T(8,128)S(1)} fusion(f32[48,512]{1,0:T(8,128)S(1)} %copy.29, f32[512,512]{1,0:T(8,128)S(1)} %get-tuple-element.214, f32[8,48,512]{2,1,0:T(8,128)} %get-tuple-element.215, s32[]{:T(128)S(6)} %select_n.49), kind=kOutput, calls=%fused_computation.1.clone.1 | convolution fusion | flops 151019520 | bytes 1343492 | tf_op jit(solution)/shard_map/while/body/dot_general | solution.py:41
  114.8 1.6 %convolution_add_fusion.5 = f32[48,512]{1,0:T(8,128)S(1)} fusion(f32[48,512]{1,0:T(8,128)S(1)} %copy.29, f32[512,512]{1,0:T(8,128)S(1)} %get-tuple-element.214, f32[8,48,512]{2,1,0:T(8,128)} %get-tuple-element.215, s32[]{:T(128)S(6)} %select_n.49), kind=kOutput, calls=%fused_computation.1.clone.1 | convolution fusion | flops 151019520 | bytes 1343492 | tf_op jit(solution)/shard_map/while/body/dot_general | solution.py:41
  119.7 3.9 %collective-permute-start.13 = (f32[48,512]{1,0:T(8,128)S(1)}, f32[48,512]{1,0:T(8,128)S(1)}, u32[]{:S(2)}, u32[]{:S(2)}) collective-permute-start(f32[48,512]{1,0:T(8,128)S(1)} %add.482), channel_id=1, source_target_pairs={{0,4},{4,8},{8,12},{12,16},{16,20},{20,24},{24,28},{1,5},{5,9},{9,... | collective-permute-start | bytes 294920 | tf_op jit(solution)/shard_map/ppermute | solution.py:31
  123.7 2.0 %collective-permute-done.13 = f32[48,512]{1,0:T(8,128)S(1)} collective-permute-done((f32[48,512]{1,0:T(8,128)S(1)}, f32[48,512]{1,0:T(8,128)S(1)}, u32[]{:S(2)}, u32[]{:S(2)}) %collective-permute-start.13) | collective-permute-done | bytes 98336 | tf_op jit(solution)/shard_map/ppermute | solution.py:31
  126.0 1.8 %collective-permute-start.14 = (f32[8,512]{1,0:T(8,128)S(1)}, f32[8,512]{1,0:T(8,128)S(1)}, u32[]{:S(2)}, u32[]{:S(2)}) collective-permute-start(f32[8,512]{1,0:T(8,128)S(1)} %get-tuple-element.93), channel_id=1, source_target_pairs={{0,1},{1,2},{2,3},{3,0},{4,5},{5,6},{6,7},{7,4},{8,9},{9,10},{10,1... | collective-permute-start | bytes 49160 | tf_op jit(solution)/shard_map/ppermute | solution.py:19
  127.8 1.7 %collective-permute-done.15 = f32[8,512]{1,0:T(8,128)S(1)} collective-permute-done((f32[8,512]{1,0:T(8,128)S(1)}, f32[8,512]{1,0:T(8,128)S(1)}, u32[]{:S(2)}, u32[]{:S(2)}) %collective-permute-start.15) | collective-permute-done | bytes 16416 | tf_op jit(solution)/shard_map/ppermute | solution.py:21
  129.5 2.0 %collective-permute-done.14 = f32[8,512]{1,0:T(8,128)S(1)} collective-permute-done((f32[8,512]{1,0:T(8,128)S(1)}, f32[8,512]{1,0:T(8,128)S(1)}, u32[]{:S(2)}, u32[]{:S(2)}) %collective-permute-start.14) | collective-permute-done | bytes 16416 | tf_op jit(solution)/shard_map/ppermute | solution.py:19
  (132 shorter events, 54.9 us)
Async XLA Ops:
  0.0 14.9 %copy-start = (f32[512,512]{1,0:T(8,128)S(1)}, f32[512,512]{1,0:T(8,128)}, u32[]{:S(2)}) copy-start(f32[512,512]{1,0:T(8,128)} %param.14) | copy-start | bytes 3145732
  0.0 3.7 %copy-start.4 = (bf16[48,512]{1,0:T(8,128)(2,1)S(1)}, bf16[48,512]{1,0:T(8,128)(2,1)}, u32[]{:S(2)}) copy-start(bf16[48,512]{1,0:T(8,128)(2,1)} %param.11) | copy-start | bytes 147460
  0.0 3.7 %copy-start.3 = (bf16[48,512]{1,0:T(8,128)(2,1)S(1)}, bf16[48,512]{1,0:T(8,128)(2,1)}, u32[]{:S(2)}) copy-start(bf16[48,512]{1,0:T(8,128)(2,1)} %param.12) | copy-start | bytes 147460
  0.1 8.5 %collective-permute-start.3 = (f32[8,512]{1,0:T(8,128)S(1)}, f32[8,512]{1,0:T(8,128)S(1)}, u32[]{:S(2)}, u32[]{:S(2)}) collective-permute-start(f32[8,512]{1,0:T(8,128)S(1)} %get-tuple-element.102), channel_id=1, source_target_pairs={{1,0},{2,1},{3,2},{0,3},{5,4},{6,5},{7,6},{4,7},{9,8},{10,9},{11,1... | collective-permute-start | bytes 49160 | tf_op jit(solution)/shard_map/ppermute | solution.py:21
  3.7 5.7 %collective-permute-start.2 = (f32[8,512]{1,0:T(8,128)S(1)}, f32[8,512]{1,0:T(8,128)S(1)}, u32[]{:S(2)}, u32[]{:S(2)}) collective-permute-start(f32[8,512]{1,0:T(8,128)S(1)} %get-tuple-element.101), channel_id=1, source_target_pairs={{0,1},{1,2},{2,3},{3,0},{4,5},{5,6},{6,7},{7,4},{8,9},{9,10},{10,1... | collective-permute-start | bytes 49160 | tf_op jit(solution)/shard_map/ppermute | solution.py:19
  3.7 11.1 %copy-start.2 = (bf16[8,48,512]{2,1,0:T(8,128)(2,1)S(1)}, bf16[8,48,512]{2,1,0:T(8,128)(2,1)}, u32[]{:S(2)}) copy-start(bf16[8,48,512]{2,1,0:T(8,128)(2,1)} %param.13) | copy-start | bytes 1179652
  4.7 5.9 %collective-permute-start.1 = (bf16[10,8,512]{2,1,0:T(8,128)(2,1)S(1)}, bf16[10,8,512]{2,1,0:T(8,128)(2,1)S(1)}, u32[]{:S(2)}, u32[]{:S(2)}) collective-permute-start(bf16[10,8,512]{2,1,0:T(8,128)(2,1)S(1)} %get-tuple-element.89), channel_id=1, source_target_pairs={{1,0},{2,1},{3,2},{0,3},{5,4},{6,5},{7,6},{4,7},{9,8},{10,9},{11,1... | collective-permute-start | bytes 245768 | tf_op jit(solution)/shard_map/ppermute | solution.py:21
  8.5 6.2 %collective-permute-start = (bf16[10,8,512]{2,1,0:T(8,128)(2,1)S(1)}, bf16[10,8,512]{2,1,0:T(8,128)(2,1)S(1)}, u32[]{:S(2)}, u32[]{:S(2)}) collective-permute-start(bf16[10,8,512]{2,1,0:T(8,128)(2,1)S(1)} %get-tuple-element.88), channel_id=1, source_target_pairs={{0,1},{1,2},{2,3},{3,0},{4,5},{5,6},{6,7},{7,4},{8,9},{9,10},{10,1... | collective-permute-start | bytes 245768 | tf_op jit(solution)/shard_map/ppermute | solution.py:19
  20.6 18.2 %copy-start.6 = (bf16[50,512]{1,0:T(8,128)(2,1)}, bf16[50,512]{1,0:T(8,128)(2,1)S(1)}, u32[]{:S(2)}) copy-start(bf16[50,512]{1,0:T(8,128)(2,1)S(1)} %get-tuple-element.84) | copy-start | bytes 153604
  21.4 6.7 %copy-start.5 = (f32[48,512]{1,0:T(8,128)S(1)}, f32[48,512]{1,0:T(8,128)}, u32[]{:S(2)}) copy-start(f32[48,512]{1,0:T(8,128)} %param.10) | copy-start | bytes 294916
  22.2 17.4 %copy-start.8 = (f32[48,512]{1,0:T(8,128)}, f32[48,512]{1,0:T(8,128)S(1)}, u32[]{:S(2)}) copy-start(f32[48,512]{1,0:T(8,128)S(1)} %fusion.182) | copy-start | bytes 294916
  22.2 5.9 %collective-permute-start.4 = (f32[48,512]{1,0:T(8,128)S(1)}, f32[48,512]{1,0:T(8,128)S(1)}, u32[]{:S(2)}, u32[]{:S(2)}) collective-permute-start(f32[48,512]{1,0:T(8,128)S(1)} %fusion.182), channel_id=1, source_target_pairs={{0,4},{4,8},{8,12},{12,16},{16,20},{20,24},{24,28},{1,5},{5,9},{9,... | collective-permute-start | bytes 294920 | tf_op jit(solution)/shard_map/ppermute | solution.py:31
  28.2 3.8 %collective-permute-start.6 = (f32[8,512]{1,0:T(8,128)S(1)}, f32[8,512]{1,0:T(8,128)S(1)}, u32[]{:S(2)}, u32[]{:S(2)}) collective-permute-start(f32[8,512]{1,0:T(8,128)S(1)} %get-tuple-element.100), channel_id=1, source_target_pairs={{1,0},{2,1},{3,2},{0,3},{5,4},{6,5},{7,6},{4,7},{9,8},{10,9},{11,1... | collective-permute-start | bytes 49160 | tf_op jit(solution)/shard_map/ppermute | solution.py:21
  28.3 5.5 %collective-permute-start.5 = (f32[8,512]{1,0:T(8,128)S(1)}, f32[8,512]{1,0:T(8,128)S(1)}, u32[]{:S(2)}, u32[]{:S(2)}) collective-permute-start(f32[8,512]{1,0:T(8,128)S(1)} %get-tuple-element.99), channel_id=1, source_target_pairs={{0,1},{1,2},{2,3},{3,0},{4,5},{5,6},{6,7},{7,4},{8,9},{9,10},{10,1... | collective-permute-start | bytes 49160 | tf_op jit(solution)/shard_map/ppermute | solution.py:19
  40.3 10.8 %copy-start.1 = (f32[512,512]{1,0:T(8,128)S(1)}, f32[512,512]{1,0:T(8,128)}, u32[]{:S(2)}) copy-start(f32[512,512]{1,0:T(8,128)} %param.15) | copy-start | bytes 3145732
  62.0 5.9 %collective-permute-start.7 = (f32[48,512]{1,0:T(8,128)S(1)}, f32[48,512]{1,0:T(8,128)S(1)}, u32[]{:S(2)}, u32[]{:S(2)}) collective-permute-start(f32[48,512]{1,0:T(8,128)S(1)} %add.433), channel_id=1, source_target_pairs={{0,4},{4,8},{8,12},{12,16},{16,20},{20,24},{24,28},{1,5},{5,9},{9,... | collective-permute-start | bytes 294920 | tf_op jit(solution)/shard_map/ppermute | solution.py:31
  68.0 3.8 %collective-permute-start.9 = (f32[8,512]{1,0:T(8,128)S(1)}, f32[8,512]{1,0:T(8,128)S(1)}, u32[]{:S(2)}, u32[]{:S(2)}) collective-permute-start(f32[8,512]{1,0:T(8,128)S(1)} %get-tuple-element.98), channel_id=1, source_target_pairs={{1,0},{2,1},{3,2},{0,3},{5,4},{6,5},{7,6},{4,7},{9,8},{10,9},{11,1... | collective-permute-start | bytes 49160 | tf_op jit(solution)/shard_map/ppermute | solution.py:21
  68.1 5.6 %collective-permute-start.8 = (f32[8,512]{1,0:T(8,128)S(1)}, f32[8,512]{1,0:T(8,128)S(1)}, u32[]{:S(2)}, u32[]{:S(2)}) collective-permute-start(f32[8,512]{1,0:T(8,128)S(1)} %get-tuple-element.97), channel_id=1, source_target_pairs={{0,1},{1,2},{2,3},{3,0},{4,5},{5,6},{6,7},{7,4},{8,9},{9,10},{10,1... | collective-permute-start | bytes 49160 | tf_op jit(solution)/shard_map/ppermute | solution.py:19
  77.8 0.8 copy-start.7
  80.2 5.9 %collective-permute-start.10 = (f32[48,512]{1,0:T(8,128)S(1)}, f32[48,512]{1,0:T(8,128)S(1)}, u32[]{:S(2)}, u32[]{:S(2)}) collective-permute-start(f32[48,512]{1,0:T(8,128)S(1)} %fusion.183), channel_id=1, source_target_pairs={{0,4},{4,8},{8,12},{12,16},{16,20},{20,24},{24,28},{1,5},{5,9},{9,... | collective-permute-start | bytes 294920 | tf_op jit(solution)/shard_map/ppermute | solution.py:31
  86.1 0.6 copy-start.9
  87.4 3.9 %collective-permute-start.12 = (f32[8,512]{1,0:T(8,128)}, f32[8,512]{1,0:T(8,128)S(1)}, u32[]{:S(2)}, u32[]{:S(2)}) collective-permute-start(f32[8,512]{1,0:T(8,128)} %get-tuple-element.96), channel_id=1, source_target_pairs={{1,0},{2,1},{3,2},{0,3},{5,4},{6,5},{7,6},{4,7},{9,8},{10,9},{11,1... | collective-permute-start | bytes 49160 | tf_op jit(solution)/shard_map/ppermute | solution.py:21
  87.5 5.5 %collective-permute-start.11 = (f32[8,512]{1,0:T(8,128)S(1)}, f32[8,512]{1,0:T(8,128)S(1)}, u32[]{:S(2)}, u32[]{:S(2)}) collective-permute-start(f32[8,512]{1,0:T(8,128)S(1)} %get-tuple-element.95), channel_id=1, source_target_pairs={{0,1},{1,2},{2,3},{3,0},{4,5},{5,6},{6,7},{7,4},{8,9},{9,10},{10,1... | collective-permute-start | bytes 49160 | tf_op jit(solution)/shard_map/ppermute | solution.py:19
  119.7 5.9 %collective-permute-start.13 = (f32[48,512]{1,0:T(8,128)S(1)}, f32[48,512]{1,0:T(8,128)S(1)}, u32[]{:S(2)}, u32[]{:S(2)}) collective-permute-start(f32[48,512]{1,0:T(8,128)S(1)} %add.482), channel_id=1, source_target_pairs={{0,4},{4,8},{8,12},{12,16},{16,20},{20,24},{24,28},{1,5},{5,9},{9,... | collective-permute-start | bytes 294920 | tf_op jit(solution)/shard_map/ppermute | solution.py:31
  125.7 3.8 %collective-permute-start.15 = (f32[8,512]{1,0:T(8,128)S(1)}, f32[8,512]{1,0:T(8,128)S(1)}, u32[]{:S(2)}, u32[]{:S(2)}) collective-permute-start(f32[8,512]{1,0:T(8,128)S(1)} %get-tuple-element.94), channel_id=1, source_target_pairs={{1,0},{2,1},{3,2},{0,3},{5,4},{6,5},{7,6},{4,7},{9,8},{10,9},{11,1... | collective-permute-start | bytes 49160 | tf_op jit(solution)/shard_map/ppermute | solution.py:21
  126.0 5.5 %collective-permute-start.14 = (f32[8,512]{1,0:T(8,128)S(1)}, f32[8,512]{1,0:T(8,128)S(1)}, u32[]{:S(2)}, u32[]{:S(2)}) collective-permute-start(f32[8,512]{1,0:T(8,128)S(1)} %get-tuple-element.93), channel_id=1, source_target_pairs={{0,1},{1,2},{2,3},{3,0},{4,5},{5,6},{6,7},{7,4},{8,9},{9,10},{10,1... | collective-permute-start | bytes 49160 | tf_op jit(solution)/shard_map/ppermute | solution.py:19
  136.6 0.9 copy-start.10
  138.3 0.9 copy-start.11
where the time goes:
time: 141 us; the launch traced here: 140 us
  matrix products  50.9 us (36%)
  waiting for transfers between devices  32.7 us (23%)
  starting transfers between devices  27.5 us (20%)
  blocking collectives  18.2 us (13%)
  other arithmetic  5.67 us (4%)
  local copies, waits for them, and re-layouts  3.93 us (3%)
    dot_general x51, matrix products, apply_matrix(): jnp.dot(field, matrix, precision=HIGHEST, preferred_element_type=jnp.floa...  50.9 us
    all_gather x2, blocking collectives, per_device(): lax.all_gather(residual[None].astype(jnp.bfloat16), 'tm', axis=0, tiled=T...  18.2 us
    ppermute x6, waiting for transfers between devices, with_halo(): lax.ppermute(tail, axis, [(i, (i + 1) % count) for i in range(count)])  12.5 us
    ppermute x4, waiting for transfers between devices, from_behind(): return lax.ppermute(block, axis, route)  12 us
    ppermute x4, starting transfers between devices, from_behind(): return lax.ppermute(block, axis, route)  11.7 us
    ppermute x6, waiting for transfers between devices, with_halo(): lax.ppermute(head, axis, [((i + 1) % count, i) for i in range(count)])  8.21 us
    ppermute x6, starting transfers between devices, with_halo(): lax.ppermute(head, axis, [((i + 1) % count, i) for i in range(count)])  8.03 us
    ppermute x6, starting transfers between devices, with_halo(): lax.ppermute(tail, axis, [(i, (i + 1) % count) for i in range(count)])  7.74 us
  transfers between devices with their start and end apart: 16, of which 15 were waited for; matrix products, arithmetic and copies ran while one was open for 1% of the time, Pallas kernels for 0%

commit v1 on v0

v1 whole, which is shorter than its diff:
```python
import functools

import jax
import jax.numpy as jnp
from jax import lax
from jax.experimental import pallas as pl
from jax.experimental.pallas import tpu as pltpu
from jax.sharding import PartitionSpec as P

F32 = jnp.float32
BF16 = jnp.bfloat16


def ring(count, distance):
    return [(i, (i + distance) % count) for i in range(count)]


def split(value):
    high = value.astype(BF16)
    return high, (value - high.astype(F32)).astype(BF16)


def product(left, right):
    return jnp.dot(left, right, preferred_element_type=F32)


def product3(value, high_matrix, low_matrix):
    rows = value.shape[0]
    high, low = split(value)
    both = product(jnp.concatenate([high, low], axis=0), high_matrix)
    return both[:rows] + (both[rows:] + product(high, low_matrix))


def stencil(value, weights):
    west, centre, east = weights
    return centre * value + east * jnp.roll(value, -1, 0) + west * jnp.roll(value, 1, 0)


def make_weights(low, own, high, rows):
    wide = low.shape[1]

    def extended(at):
        return jnp.concatenate(
            [low[at, wide - rows :].astype(F32), own[at].astype(F32), high[at, :rows].astype(F32)], axis=0
        )

    moving, spread = extended(0), extended(1)
    return (spread + 0.5 * moving, 1.0 - 2.0 * spread, spread - 0.5 * moving)


def call(kernel, out_shape, *operands, smem=()):
    in_specs = [
        pl.BlockSpec(memory_space=pltpu.SMEM if i in smem else pltpu.VMEM) for i in range(len(operands))
    ]
    single = not isinstance(out_shape, (list, tuple))
    out_specs = jax.tree.map(lambda _: pl.BlockSpec(memory_space=pltpu.VMEM), out_shape)
    return pl.pallas_call(
        kernel,
        out_shape=out_shape,
        in_specs=in_specs,
        out_specs=out_specs if not single else pl.BlockSpec(memory_space=pltpu.VMEM),
        name=getattr(kernel, "__name__", None) or kernel.func.__name__,
    )(*operands)


def extended_forcing(low, own, high, at):
    return jnp.concatenate([low[at].astype(F32), own[at].astype(F32), high[at].astype(F32)], axis=0)


def pack(steps, wide, velocity, diffusion, forcing, start, head, tail):
    own = start.shape[0]
    f_rows = steps * steps
    for out, lead in ((head, 0), (tail, own)):
        near = slice(0, steps) if lead == 0 else slice(own - steps, own)
        far = slice(0, wide) if lead == 0 else slice(own - wide, own)
        for step in range(steps):
            out[step * steps : (step + 1) * steps] = forcing[step, near]
        out[f_rows : f_rows + wide] = velocity[far]
        out[f_rows + wide : f_rows + 2 * wide] = diffusion[far]
        parts = split(start[near])
        for i in range(2):
            at = f_rows + 2 * wide + i * steps
            out[at : at + steps] = parts[i]


def split_matrices(implicit, coarse_implicit, high_m, low_m, coarse):
    high_m[...], low_m[...] = split(implicit[...])
    coarse[...] = coarse_implicit[...].astype(BF16)


def first_sweep(steps, place, flow, fhigh, chigh, uhigh, clow_, ulow, forcing, coef, start, high_m, low_m, out):
    lead = fhigh.shape[1]
    own = start.shape[0]
    weights = make_weights(clow_, coef, chigh, lead)
    current = jnp.concatenate(
        [
            ulow[0].astype(F32) + ulow[1].astype(F32),
            start[...],
            uhigh[0].astype(F32) + uhigh[1].astype(F32),
        ],
        axis=0,
    )
    current = jnp.where(place[0] == 0, current, 0.0)
    for step in range(steps):
        summed = stencil(current, weights) + extended_forcing(flow, forcing, fhigh, step)
        current = product3(summed, high_m[...], low_m[...])
    out[...] = current[lead : lead + own]


def second_sweep(steps, keep, alow, ahigh, clow, chigh, a, coef, high_m, low_m, rho_high, rho_low, a_near):
    wide = alow.shape[0]
    own = a.shape[0]
    weights = make_weights(clow, coef, chigh, wide)
    current = jnp.concatenate([alow[...], a[...], ahigh[...]], axis=0)
    a_near[...] = current[wide - steps : wide + own + steps]
    for _ in range(steps):
        current = product3(stencil(current, weights), high_m[...], low_m[...])
    current = current[wide - keep : wide + own + keep]
    high = current.astype(BF16)
    rho_high[...] = high
    near = slice(keep - steps, keep + own + steps)
    rho_low[...] = (current[near] - high[near].astype(F32)).astype(BF16)


def coarse_and_third(steps, place, rho, clow, chigh, coef, high_m, low_m, coarse, le_out, psi_out, err_scratch):
    own = coef.shape[1]
    keep = (rho.shape[1] - own) // 2
    at = place[0]
    weights = make_weights(clow, coef, chigh, keep)
    first = jnp.where(at >= 2, rho[0].astype(F32), 0.0)

    def turn(source, carried):
        return product(carried.astype(BF16), coarse[...]) + rho[source].astype(F32)

    error = lax.fori_loop(1, at - 1, turn, first)
    err_scratch[...] = error
    current = error
    for _ in range(steps):
        current = product3(stencil(current, weights), high_m[...], low_m[...])
    mid = slice(keep - steps, keep + own + steps)
    le_out[...] = current[mid]
    current = current - product(err_scratch[...].astype(BF16), coarse[...])
    for _ in range(steps):
        current = product(stencil(current, weights).astype(BF16), high_m[...])
    psi_out[...] = current[mid].astype(BF16)


def last_sweep(
    steps, place, psi, b_before, b, flow, fhigh, clow, chigh, uhigh, ulow, forcing, coef, start, high_m, low_m, coarse, out
):
    own = coef.shape[1]
    lead = (b_before.shape[0] - own) // 2
    at = place[0]
    weights = make_weights(clow, coef, chigh, lead)

    def turn(source, carried):
        return product(carried.astype(BF16), coarse[...]) + psi[source].astype(F32)

    error = lax.fori_loop(2, at - 1, turn, jnp.zeros(b_before.shape, F32))
    initial = jnp.concatenate(
        [
            ulow[0].astype(F32) + ulow[1].astype(F32),
            start[...],
            uhigh[0].astype(F32) + uhigh[1].astype(F32),
        ],
        axis=0,
    )
    current = jnp.where(at == 0, initial, b_before[...] + error)
    mid = slice(lead, lead + own)
    before = psi[jnp.maximum(at - 1, 0)].astype(F32)
    last = jnp.where(at >= 1, product(error.astype(BF16), coarse[...]) + before, 0.0)
    out[steps - 1] = b[mid] + last[mid]
    for step in range(steps - 1):
        summed = stencil(current, weights) + extended_forcing(flow, forcing, fhigh, step)
        current = product3(summed, high_m[...], low_m[...])
        out[step] = current[mid]


def per_device(initial_state, velocity, diffusion, forcing, implicit, coarse_implicit):
    own, columns = initial_state.shape
    steps = forcing.shape[0]
    blocks = lax.axis_size("tm")
    slabs = lax.axis_size("space")
    at = lax.axis_index("tm")
    place = at.astype(jnp.int32).reshape(1)
    keep = 3 * steps
    wide = 4 * steps

    coef = jnp.stack([velocity, diffusion])
    f_rows, c_rows = steps * steps, 2 * wide

    def unpack(packed):
        return (
            packed[:f_rows].reshape(steps, steps, columns),
            packed[f_rows : f_rows + c_rows].reshape(2, wide, columns),
            packed[f_rows + c_rows :].reshape(2, steps, columns),
        )

    packed_shape = jax.ShapeDtypeStruct((f_rows + c_rows + 2 * steps, columns), BF16)
    head, tail = call(
        functools.partial(pack, steps, wide), [packed_shape, packed_shape], velocity, diffusion, forcing, initial_state
    )
    flow, clow, ulow = unpack(lax.ppermute(tail, "space", ring(slabs, 1)))
    fhigh, chigh, uhigh = unpack(lax.ppermute(head, "space", ring(slabs, -1)))
    matrix_shape = jax.ShapeDtypeStruct(implicit.shape, BF16)
    high_m, low_m, coarse = call(split_matrices, [matrix_shape] * 3, implicit, coarse_implicit)

    def field(rows, dtype=F32):
        return jax.ShapeDtypeStruct((rows, columns), dtype)

    a = call(
        functools.partial(first_sweep, steps),
        field(own),
        place, flow, fhigh, chigh, uhigh, clow, ulow, forcing, coef, initial_state, high_m, low_m,
        smem=(0,),
    )
    alow = lax.ppermute(a[own - wide :], "space", ring(slabs, 1))
    ahigh = lax.ppermute(a[:wide], "space", ring(slabs, -1))
    near = own + 2 * steps
    rho, rho_low, a_near = call(
        functools.partial(second_sweep, steps, keep),
        [field(own + 2 * keep, BF16), field(near, BF16), field(near)],
        alow, ahigh, clow, chigh, a, coef, high_m, low_m,
    )
    rho_all = lax.all_gather(rho, "tm", axis=0)
    low_before = lax.ppermute(rho_low, "tm", ring(blocks, 1))
    le, psi = third(steps, own, keep, columns, place, rho_all, clow, chigh, coef, high_m, low_m, coarse)
    rho_before = rho_all[jnp.maximum(at - 1, 0)][keep - steps : keep + own + steps].astype(F32) + low_before.astype(F32)
    b = a_near + jnp.where(at == 0, 0.0, rho_before) + le
    b_before = lax.ppermute(b, "tm", ring(blocks, 1))
    psi_all = lax.all_gather(psi, "tm", axis=0)
    return call(
        functools.partial(last_sweep, steps),
        jax.ShapeDtypeStruct((steps, own, columns), F32),
        place, psi_all, b_before, b, flow, fhigh, clow, chigh, uhigh, ulow, forcing, coef, initial_state,
        high_m, low_m, coarse,
        smem=(0,),
    )


def third(steps, own, keep, columns, place, *operands):
    near = own + 2 * steps
    vmem = pl.BlockSpec(memory_space=pltpu.VMEM)
    return pl.pallas_call(
        functools.partial(coarse_and_third, steps),
        out_shape=[jax.ShapeDtypeStruct((near, columns), F32), jax.ShapeDtypeStruct((near, columns), BF16)],
        in_specs=[pl.BlockSpec(memory_space=pltpu.SMEM)] + [vmem] * len(operands),
        out_specs=[vmem, vmem],
        scratch_shapes=[pltpu.VMEM((own + 2 * keep, columns), F32)],
        name="coarse_and_third",
    )(place, *operands)


def solution(mesh):
    in_specs = (
        P("space", None),
        P("space", None),
        P("space", None),
        P("tm", "space", None),
        P(),
        P(),
    )
    out_specs = P("tm", "space", None)
    return jax.shard_map(per_device, mesh=mesh, in_specs=in_specs, out_specs=out_specs, check_vma=False)
```

time: 141 us -> 74.8 us (0.53)
  the two profiles are of different devices: /device:TPU:6 before, /device:TPU:0 now
where the time goes in v1:
time: 74.8 us; the launch traced here: 74.4 us
  Pallas kernels  26.3 us (35%)
  blocking collectives  24.6 us (33%)
  starting transfers between devices  9.12 us (12%)
  waiting for transfers between devices  7.97 us (11%)
  local copies, waits for them, and re-layouts  4.76 us (6%)
  other arithmetic  1.62 us (2%)
    pallas_call x5, Pallas kernels, call(): pl.pallas_call(kernel, out_shape=out_shape, in_specs=in_specs, out_specs=...  19.2 us
    all_gather x1, blocking collectives, per_device(): rho_all = lax.all_gather(rho, 'tm', axis=0)  13.2 us
    all_gather x1, blocking collectives, per_device(): psi_all = lax.all_gather(psi, 'tm', axis=0)  11.4 us
    pallas_call x1, Pallas kernels, third(): pl.pallas_call(functools.partial(coarse_and_third, steps), out_shape=[jax...  7.07 us
    ppermute x1, waiting for transfers between devices, per_device(): alow = lax.ppermute(a[own - wide:], 'space', ring(slabs, 1))  4.16 us
    ppermute x1, starting transfers between devices, per_device(): ahigh = lax.ppermute(a[:wide], 'space', ring(slabs, -1))  3.62 us
    ppermute x1, starting transfers between devices, per_device(): flow, clow, ulow = unpack(lax.ppermute(tail, 'space', ring(slabs, 1)))  3.05 us
    ppermute x1, starting transfers between devices, per_device(): fhigh, chigh, uhigh = unpack(lax.ppermute(head, 'space', ring(slabs, -1)))  2.03 us
  transfers between devices with their start and end apart: 6, of which 4 were waited for; matrix products, arithmetic and copies ran while one was open for 3% of the time, Pallas kernels for 13%

profile of v1, /device:TPU:0, one launch (start us, length us, event | category | flops | bytes accessed | tf_op | source)
XLA Modules:
  0.0 74.4 jit_solution(8034537969320671306)
XLA Ops:
  0.0 1.8 %pack.1 = (bf16[144,512]{1,0:T(8,128)(2,1)}, bf16[144,512]{1,0:T(8,128)(2,1)}) custom-call(bf16[48,512]{1,0:T(8,128)(2,1)} %velocity.1, bf16[48,512]{1,0:T(8,128)(2,1)} %diffusion.1, bf16[8,48,512]{2,1,0:T(8,128)(2,1)} %forcing.5, f32[48,512]{1,0:T(8,128)} %start.5), custom_call_target="tpu_custom_call" | custom-call | tf_op jit(solution)/shard_map/pack/pallas_call | solution.py:57
  1.8 3.1 %collective-permute-start = (bf16[144,512]{1,0:T(8,128)(2,1)}, bf16[144,512]{1,0:T(8,128)(2,1)S(1)}, u32[]{:S(2)}, u32[]{:S(2)}) collective-permute-start(bf16[144,512]{1,0:T(8,128)(2,1)} %get-tuple-element.15), channel_id=1, source_target_pairs={{0,1},{1,2},{2,3},{3,0},{4,5},{5,6},{6,7},{7,4},{8,9},{9,10},{10,1... | collective-permute-start | bytes 442376 | tf_op jit(solution)/shard_map/ppermute | solution.py:203
  4.8 2.0 %collective-permute-start.1 = (bf16[144,512]{1,0:T(8,128)(2,1)}, bf16[144,512]{1,0:T(8,128)(2,1)S(1)}, u32[]{:S(2)}, u32[]{:S(2)}) collective-permute-start(bf16[144,512]{1,0:T(8,128)(2,1)} %get-tuple-element.16), channel_id=1, source_target_pairs={{0,3},{1,0},{2,1},{3,2},{4,7},{5,4},{6,5},{7,6},{8,11},{9,8},{10,9... | collective-permute-start | bytes 442376 | tf_op jit(solution)/shard_map/ppermute | solution.py:204
  6.9 2.8 %split_matrices.1 = (bf16[512,512]{1,0:T(8,128)(2,1)}, bf16[512,512]{1,0:T(8,128)(2,1)}, bf16[512,512]{1,0:T(8,128)(2,1)}) custom-call(f32[512,512]{1,0:T(8,128)} %implicit.1, f32[512,512]{1,0:T(8,128)} %coarse_implicit.1), custom_call_target="tpu_custom_call" | custom-call | tf_op jit(solution)/shard_map/split_matrices/pallas_call | solution.py:57
  9.7 0.0 copy-done.1
  9.7 0.0 copy-done.2
  9.7 0.6 pad_maximum_fusion.coef
  10.4 1.5 %collective-permute-done = bf16[144,512]{1,0:T(8,128)(2,1)S(1)} collective-permute-done((bf16[144,512]{1,0:T(8,128)(2,1)}, bf16[144,512]{1,0:T(8,128)(2,1)S(1)}, u32[]{:S(2)}, u32[]{:S(2)}) %collective-permute-start) | collective-permute-done | bytes 147488 | tf_op jit(solution)/shard_map/ppermute | solution.py:203
  11.8 0.7 fusion.3
  12.5 0.6 slice_bitcast_fusion.2.ulow
  13.1 0.4 collective-permute-done.1
  13.5 0.6 slice_bitcast_fusion.3.uhigh
  14.1 0.7 fusion.4
  14.8 4.5 %first_sweep.1.a = f32[48,512]{1,0:T(8,128)} custom-call(s32[1]{0:T(128)} %bitcast.place, bf16[8,8,512]{2,1,0:T(8,128)(2,1)} %get-tuple-element.26.flow, bf16[8,8,512]{2,1,0:T(8,128)(2,1)} %get-tuple-element.28.fhigh, bf16[2,32,512]{2,1,0:T(8,128)(2,1)} %bitcast.27, bf16[2,8,512]{2,1,0:T(8,128)(2,1)} %slice_bitcast_fusion.3.uhigh, ...), custom_call_target="tpu_custom_call" | custom-call | tf_op jit(solution)/shard_map/first_sweep/pallas_call | solution.py:57
  19.3 0.9 %fusion.5 = (f32[32,512]{1,0:T(8,128)S(1)}, f32[32,512]{1,0:T(8,128)S(1)}) fusion(f32[48,512]{1,0:T(8,128)} %first_sweep.1.a), kind=kLoop, calls=%fused_computation.12 | loop fusion | bytes 262144 | tf_op jit(solution)/shard_map/slice | solution.py:218
  20.3 3.6 %collective-permute-start.3 = (f32[32,512]{1,0:T(8,128)S(1)}, f32[32,512]{1,0:T(8,128)S(1)}, u32[]{:S(2)}, u32[]{:S(2)}) collective-permute-start(f32[32,512]{1,0:T(8,128)S(1)} %get-tuple-element.29), channel_id=1, source_target_pairs={{0,3},{1,0},{2,1},{3,2},{4,7},{5,4},{6,5},{7,6},{8,11},{9,8},{10,9... | collective-permute-start | bytes 196616 | tf_op jit(solution)/shard_map/ppermute | solution.py:218
  23.9 0.0 collective-permute-start.2
  23.9 1.9 %collective-permute-done.3.ahigh = f32[32,512]{1,0:T(8,128)S(1)} collective-permute-done((f32[32,512]{1,0:T(8,128)S(1)}, f32[32,512]{1,0:T(8,128)S(1)}, u32[]{:S(2)}, u32[]{:S(2)}) %collective-permute-start.3) | collective-permute-done | bytes 65568 | tf_op jit(solution)/shard_map/ppermute | solution.py:218
  25.8 4.2 %collective-permute-done.2.alow = f32[32,512]{1,0:T(8,128)S(1)} collective-permute-done((f32[32,512]{1,0:T(8,128)S(1)}, f32[32,512]{1,0:T(8,128)S(1)}, u32[]{:S(2)}, u32[]{:S(2)}) %collective-permute-start.2) | collective-permute-done | bytes 65568 | tf_op jit(solution)/shard_map/ppermute | solution.py:217
  29.9 0.6 copy-done.6
  30.6 5.1 %second_sweep.1 = (bf16[96,512]{1,0:T(8,128)(2,1)}, bf16[64,512]{1,0:T(8,128)(2,1)}, f32[64,512]{1,0:T(8,128)}) custom-call(f32[32,512]{1,0:T(8,128)} %copy-done.6, f32[32,512]{1,0:T(8,128)} %copy-done.5, bf16[2,32,512]{2,1,0:T(8,128)(2,1)} %bitcast.24, bf16[2,32,512]{2,1,0:T(8,128)(2,1)} %bitcast.28, f32[48,512]{1,0:T(8,128)} %first_sweep.1.a, ...), custom_call_target="tpu_custom_call" | custom-call | tf_op jit(solution)/shard_map/second_sweep/pallas_call | solution.py:57
  35.6 0.0 collective-permute-start.4
  35.6 13.2 %all-gather = bf16[768,512]{1,0:T(8,128)(2,1)} all-gather(bf16[96,512]{1,0:T(8,128)(2,1)} %get-tuple-element.19), channel_id=2, replica_groups=mesh['tm'=8,'space'=4] {'tm'}, dimensions={0}, use_global_device_ids=true | all-gather | bytes 884736 | tf_op jit(solution)/shard_map/all_gather | solution.py:225
  48.8 7.1 %coarse_and_third.1 = (f32[64,512]{1,0:T(8,128)}, bf16[64,512]{1,0:T(8,128)(2,1)}) custom-call(s32[1]{0:T(128)} %bitcast.place, bf16[8,96,512]{2,1,0:T(8,128)(2,1)} %bitcast.20, bf16[2,32,512]{2,1,0:T(8,128)(2,1)} %bitcast.25, bf16[2,32,512]{2,1,0:T(8,128)(2,1)} %bitcast.29, bf16[2,48,512]{2,1,0:T(8,128)(2,1)} %pad_maximum_fusion.coef, ...), custom_call_target="tpu_custom_call" | custom-call | tf_op jit(solution)/shard_map/coarse_and_third/pallas_call | solution.py:244
  55.9 0.0 collective-permute-done.4
  55.9 1.0 %fusion.2.b = f32[64,512]{1,0:T(8,128)S(1)} fusion(f32[64,512]{1,0:T(8,128)} %get-tuple-element.24, f32[64,512]{1,0:T(8,128)S(1)} %copy-done.3, bf16[64,512]{1,0:T(8,128)(2,1)S(1)} %collective-permute-done.4, bf16[8,96,512]{2,1,0:T(8,128)(2,1)} %bitcast.21, s32[]{:T(128)S(6)} %max.3, s32[]{:T(128)S(6)} %add.14, pred[]{:T(512)S(6)} %eq.3), kind=kLoop, calls=%fused_computation.3 | loop fusion | flops 196608 | bytes 524297 | tf_op jit(solution)/shard_map/add | solution.py:229
  56.9 0.4 collective-permute-start.5
  57.3 0.0 copy-done.7
  57.3 11.4 %all-gather.1 = bf16[512,512]{1,0:T(8,128)(2,1)} all-gather(bf16[64,512]{1,0:T(8,128)(2,1)S(1)} %copy-done.7), channel_id=3, replica_groups=mesh['tm'=8,'space'=4] {'tm'}, dimensions={0}, use_global_device_ids=true | all-gather | bytes 589824 | tf_op jit(solution)/shard_map/all_gather | solution.py:231
  68.7 0.0 collective-permute-done.5.b_before
  68.7 0.7 copy-done.4
  69.4 5.0 %last_sweep.1 = f32[8,48,512]{2,1,0:T(8,128)} custom-call(s32[1]{0:T(128)} %bitcast.place, bf16[8,64,512]{2,1,0:T(8,128)(2,1)} %bitcast.22, f32[64,512]{1,0:T(8,128)} %copy-done.4, f32[64,512]{1,0:T(8,128)} %copy-done, bf16[8,8,512]{2,1,0:T(8,128)(2,1)} %get-tuple-element.26.flow, bf16[8,8,512]{2,1,0:T(8,128)(2,1)} %get-tuple-element.28.fhigh, ...), custom_call_target="tpu_custom_call" | custom-call | tf_op jit(solution)/shard_map/last_sweep/pallas_call | solution.py:57
  (11 shorter events, 0.0 us)
Async XLA Ops:
  1.8 10.0 %collective-permute-start = (bf16[144,512]{1,0:T(8,128)(2,1)}, bf16[144,512]{1,0:T(8,128)(2,1)S(1)}, u32[]{:S(2)}, u32[]{:S(2)}) collective-permute-start(bf16[144,512]{1,0:T(8,128)(2,1)} %get-tuple-element.15), channel_id=1, source_target_pairs={{0,1},{1,2},{2,3},{3,0},{4,5},{5,6},{6,7},{7,4},{8,9},{9,10},{10,1... | collective-permute-start | bytes 442376 | tf_op jit(solution)/shard_map/ppermute | solution.py:203
  4.8 8.7 %collective-permute-start.1 = (bf16[144,512]{1,0:T(8,128)(2,1)}, bf16[144,512]{1,0:T(8,128)(2,1)S(1)}, u32[]{:S(2)}, u32[]{:S(2)}) collective-permute-start(bf16[144,512]{1,0:T(8,128)(2,1)} %get-tuple-element.16), channel_id=1, source_target_pairs={{0,3},{1,0},{2,1},{3,2},{4,7},{5,4},{6,5},{7,6},{8,11},{9,8},{10,9... | collective-permute-start | bytes 442376 | tf_op jit(solution)/shard_map/ppermute | solution.py:204
  6.9 2.8 %copy-start.1 = (bf16[48,512]{1,0:T(8,128)(2,1)S(1)}, bf16[48,512]{1,0:T(8,128)(2,1)}, u32[]{:S(2)}) copy-start(bf16[48,512]{1,0:T(8,128)(2,1)} %velocity.1) | copy-start | bytes 147460
  6.9 2.8 %copy-start.2 = (bf16[48,512]{1,0:T(8,128)(2,1)S(1)}, bf16[48,512]{1,0:T(8,128)(2,1)}, u32[]{:S(2)}) copy-start(bf16[48,512]{1,0:T(8,128)(2,1)} %diffusion.1) | copy-start | bytes 147460
  20.3 5.5 %collective-permute-start.3 = (f32[32,512]{1,0:T(8,128)S(1)}, f32[32,512]{1,0:T(8,128)S(1)}, u32[]{:S(2)}, u32[]{:S(2)}) collective-permute-start(f32[32,512]{1,0:T(8,128)S(1)} %get-tuple-element.29), channel_id=1, source_target_pairs={{0,3},{1,0},{2,1},{3,2},{4,7},{5,4},{6,5},{7,6},{8,11},{9,8},{10,9... | collective-permute-start | bytes 196616 | tf_op jit(solution)/shard_map/ppermute | solution.py:218
  23.9 6.1 %collective-permute-start.2 = (f32[32,512]{1,0:T(8,128)S(1)}, f32[32,512]{1,0:T(8,128)S(1)}, u32[]{:S(2)}, u32[]{:S(2)}) collective-permute-start(f32[32,512]{1,0:T(8,128)S(1)} %get-tuple-element.30), channel_id=1, source_target_pairs={{0,1},{1,2},{2,3},{3,0},{4,5},{5,6},{6,7},{7,4},{8,9},{9,10},{10,1... | collective-permute-start | bytes 196616 | tf_op jit(solution)/shard_map/ppermute | solution.py:217
  25.8 4.2 %copy-start.5 = (f32[32,512]{1,0:T(8,128)}, f32[32,512]{1,0:T(8,128)S(1)}, u32[]{:S(2)}) copy-start(f32[32,512]{1,0:T(8,128)S(1)} %collective-permute-done.3.ahigh) | copy-start | bytes 196612
  29.9 0.6 copy-start.6
  35.6 20.2 %collective-permute-start.4 = (bf16[64,512]{1,0:T(8,128)(2,1)}, bf16[64,512]{1,0:T(8,128)(2,1)S(1)}, u32[]{:S(2)}, u32[]{:S(2)}) collective-permute-start(bf16[64,512]{1,0:T(8,128)(2,1)} %get-tuple-element.23), channel_id=1, source_target_pairs={{0,4},{4,8},{8,12},{12,16},{16,20},{20,24},{24,28},{28,0},{1,5},{5... | collective-permute-start | bytes 196616 | tf_op jit(solution)/shard_map/ppermute | solution.py:226
  48.8 7.1 %copy-start.3 = (f32[64,512]{1,0:T(8,128)S(1)}, f32[64,512]{1,0:T(8,128)}, u32[]{:S(2)}) copy-start(f32[64,512]{1,0:T(8,128)} %get-tuple-element.22) | copy-start | bytes 393220
  55.9 1.4 %copy-start.7 = (bf16[64,512]{1,0:T(8,128)(2,1)S(1)}, bf16[64,512]{1,0:T(8,128)(2,1)}, u32[]{:S(2)}) copy-start(bf16[64,512]{1,0:T(8,128)(2,1)} %get-tuple-element.21) | copy-start | bytes 196612
  56.9 11.9 %copy-start = (f32[64,512]{1,0:T(8,128)}, f32[64,512]{1,0:T(8,128)S(1)}, u32[]{:S(2)}) copy-start(f32[64,512]{1,0:T(8,128)S(1)} %fusion.2.b) | copy-start | bytes 393220
  56.9 11.9 %collective-permute-start.5 = (f32[64,512]{1,0:T(8,128)S(1)}, f32[64,512]{1,0:T(8,128)S(1)}, u32[]{:S(2)}, u32[]{:S(2)}) collective-permute-start(f32[64,512]{1,0:T(8,128)S(1)} %fusion.2.b), channel_id=1, source_target_pairs={{0,4},{4,8},{8,12},{12,16},{16,20},{20,24},{24,28},{28,0},{1,5},{5... | collective-permute-start | bytes 393224 | tf_op jit(solution)/shard_map/ppermute | solution.py:230
  68.7 0.7 copy-start.4

commit v2 on v0

v2 whole, which is shorter than its diff:
```python
import functools

import jax
import jax.numpy as jnp
from jax import lax
from jax.experimental import pallas as pl
from jax.experimental.pallas import tpu as pltpu
from jax.sharding import PartitionSpec as P

F32 = jnp.float32
BF16 = jnp.bfloat16


def ring(count, distance):
    return [(i, (i + distance) % count) for i in range(count)]


def split(value):
    high = value.astype(BF16)
    return high, (value - high.astype(F32)).astype(BF16)


def product(left, right):
    return jnp.dot(left, right, preferred_element_type=F32)


def product3(value, high_matrix, low_matrix):
    rows = value.shape[0]
    high, low = split(value)
    both = product(jnp.concatenate([high, low], axis=0), high_matrix)
    return both[:rows] + (both[rows:] + product(high, low_matrix))


def stencil(value, weights):
    west, centre, east = weights
    return centre * value + east * jnp.roll(value, -1, 0) + west * jnp.roll(value, 1, 0)


class Layout:
    def __init__(self, steps, own):
        self.steps = steps
        self.own = own
        self.wide = 5 * steps
        self.keep = 3 * steps
        self.fine = 2 * steps
        self.velocity = steps * self.wide
        self.diffusion = self.velocity + self.wide
        self.start = self.diffusion + self.wide
        self.start_low = self.start + self.wide
        self.rows = self.start_low + self.fine

    def centred(self, width, inside):
        return slice(width - inside, width + self.own + inside)


def pack(lay, velocity, diffusion, forcing, start, head, tail):
    for out, first in ((head, 0), (tail, lay.own - lay.wide)):
        near = slice(first, first + lay.wide)
        for step in range(lay.steps):
            out[step * lay.wide : (step + 1) * lay.wide] = forcing[step, near]
        out[lay.velocity : lay.diffusion] = velocity[near]
        out[lay.diffusion : lay.start] = diffusion[near]
        high, low = split(start[near])
        out[lay.start : lay.start_low] = high
        out[lay.start_low : lay.rows] = low[: lay.fine] if first == 0 else low[lay.wide - lay.fine :]


def split_matrices(implicit, coarse_implicit, high_m, low_m, coarse):
    high_m[...], low_m[...] = split(implicit[...])
    coarse[...] = coarse_implicit[...].astype(BF16)


def from_packs(lay, low, own, high, at, width):
    return jnp.concatenate(
        [
            low[at + lay.wide - width : at + lay.wide].astype(F32),
            own.astype(F32),
            high[at : at + width].astype(F32),
        ],
        axis=0,
    )


def start_from_packs(lay, low, own, high, width):
    value = from_packs(lay, low, own, high, lay.start, width)
    fine = min(width, lay.fine)
    low_tail = low[lay.start_low + lay.fine - fine : lay.rows].astype(F32)
    high_tail = high[lay.start_low : lay.start_low + fine].astype(F32)
    pieces = [
        value[: width - fine] if width > fine else None,
        value[width - fine : width] + low_tail,
        value[width : width + lay.own],
        value[width + lay.own : width + lay.own + fine] + high_tail,
        value[width + lay.own + fine :] if width > fine else None,
    ]
    return jnp.concatenate([piece for piece in pieces if piece is not None], axis=0)


def two_sweeps(lay, place, low, high, forcing, velocity, diffusion, start, high_m, low_m, rho, rho_low, a_near, weights):
    wide, steps = lay.wide, lay.steps
    moving = from_packs(lay, low, velocity[...], high, lay.velocity, wide)
    spread = from_packs(lay, low, diffusion[...], high, lay.diffusion, wide)
    weights[0] = spread + 0.5 * moving
    weights[1] = 1.0 - 2.0 * spread
    weights[2] = spread - 0.5 * moving
    current = start_from_packs(lay, low, start[...], high, wide)
    current = jnp.where(place[0] == 0, current, 0.0)
    for step in range(steps):
        summed = stencil(current, weights[...]) + from_packs(lay, low, forcing[step], high, step * wide, wide)
        current = product3(summed, high_m[...], low_m[...])
    a_near[...] = current[lay.centred(wide, steps)]
    width = wide - steps
    current = current[lay.centred(wide, width)]
    narrow = weights[:, lay.centred(wide, width)]
    for _ in range(steps):
        current = product3(stencil(current, narrow), high_m[...], low_m[...])
    high_part, low_part = split(current)
    rho[...] = high_part[lay.centred(width, lay.keep)]
    rho_low[...] = low_part[lay.centred(width, 0)]


def coarse_and_third(lay, place, rho, rho_low, a_near, weights, high_m, low_m, coarse, psi, passed, b_own, error_kept):
    keep, steps, own = lay.keep, lay.steps, lay.own
    at = place[0]
    narrow = weights[:, lay.centred(lay.wide, keep)]
    first = jnp.where(at >= 2, rho[0].astype(F32), 0.0)

    def turn(source, carried):
        return product(carried.astype(BF16), coarse[...]) + rho[source].astype(F32)

    current = lax.fori_loop(1, at - 1, turn, first)
    error_kept[...] = current
    for _ in range(steps):
        current = product3(stencil(current, narrow), high_m[...], low_m[...])
    near = lay.centred(keep, steps)
    before = rho[jnp.maximum(at - 1, 0)].astype(F32)[near]
    b = a_near[...] + jnp.where(at == 0, 0.0, before) + current[near]
    b_own[...] = b[lay.centred(steps, 0)]
    rows = own + 2 * steps
    passed[:rows], passed[rows : 2 * rows] = split(b)
    passed[2 * rows :] = rho_low[...]
    current = current - product(error_kept[...].astype(BF16), coarse[...])
    for _ in range(steps):
        current = product(stencil(current, narrow).astype(BF16), high_m[...])
    psi[...] = current[near].astype(BF16)


def last_sweep(lay, place, psi, passed, b_own, low, high, forcing, weights, start, high_m, low_m, coarse, out):
    steps, own = lay.steps, lay.own
    at = place[0]
    rows = own + 2 * steps
    narrow = weights[:, lay.centred(lay.wide, steps)]

    def turn(source, carried):
        return product(carried.astype(BF16), coarse[...]) + psi[source].astype(F32)

    error = lax.fori_loop(2, at - 1, turn, jnp.zeros((rows, start.shape[1]), F32))
    b_before = passed[:rows].astype(F32) + passed[rows : 2 * rows].astype(F32)
    initial = start_from_packs(lay, low, start[...], high, steps)
    current = jnp.where(at == 0, initial, b_before + error)
    mid = lay.centred(steps, 0)
    last = product(error[mid].astype(BF16), coarse[...]) + psi[jnp.maximum(at - 1, 0)].astype(F32)[mid]
    last = last + passed[2 * rows :].astype(F32)
    out[steps - 1] = b_own[...] + jnp.where(at == 0, 0.0, last)
    for step in range(steps - 1):
        summed = stencil(current, narrow) + from_packs(lay, low, forcing[step], high, step * lay.wide, steps)
        current = product3(summed, high_m[...], low_m[...])
        out[step] = current[mid]


def in_vmem(value):
    return pltpu.with_memory_space_constraint(value, pltpu.VMEM)


def call(kernel, lay, outs, *operands, scratch=()):
    spaces = [pltpu.SMEM if o.dtype == jnp.int32 else pltpu.VMEM for o in operands]
    return pl.pallas_call(
        kernel if lay is None else functools.partial(kernel, lay),
        out_shape=outs,
        in_specs=[pl.BlockSpec(memory_space=space) for space in spaces],
        out_specs=jax.tree.map(lambda _: pl.BlockSpec(memory_space=pltpu.VMEM), outs),
        scratch_shapes=scratch,
        compiler_params=pltpu.CompilerParams(vmem_limit_bytes=16 << 20),
        name=kernel.__name__,
    )(*operands)


def per_device(initial_state, velocity, diffusion, forcing, implicit, coarse_implicit):
    own, columns = initial_state.shape
    steps = forcing.shape[0]
    blocks = lax.axis_size("tm")
    slabs = lax.axis_size("space")
    place = lax.axis_index("tm").astype(jnp.int32).reshape(1)
    lay = Layout(steps, own)
    near = own + 2 * steps

    def kept(*shape, dtype=F32):
        return pltpu.VMEM(shape, dtype)

    head, tail = call(pack, lay, [kept(lay.rows, columns, dtype=BF16)] * 2, velocity, diffusion, forcing, initial_state)
    low = in_vmem(lax.ppermute(tail, "space", ring(slabs, 1)))
    high = in_vmem(lax.ppermute(head, "space", ring(slabs, -1)))
    high_m, low_m, coarse = call(
        split_matrices, None, [kept(*implicit.shape, dtype=BF16)] * 3, implicit, coarse_implicit
    )
    high_m, low_m, coarse = in_vmem(high_m), in_vmem(low_m), in_vmem(coarse)
    rho, rho_low, a_near, weights = call(
        two_sweeps,
        lay,
        [
            kept(own + 2 * lay.keep, columns, dtype=BF16),
            kept(own, columns, dtype=BF16),
            kept(near, columns),
            kept(3, own + 2 * lay.wide, columns),
        ],
        place, low, high, forcing, velocity, diffusion, initial_state, high_m, low_m,
    )
    weights = in_vmem(weights)
    rho_all = lax.all_gather(rho, "tm", axis=0)
    psi, passed, b_own = call(
        coarse_and_third,
        lay,
        [
            kept(near, columns, dtype=BF16),
            kept(2 * near + own, columns, dtype=BF16),
            kept(own, columns),
        ],
        place, rho_all, in_vmem(rho_low), in_vmem(a_near), weights, high_m, low_m, coarse,
        scratch=[pltpu.VMEM((own + 2 * lay.keep, columns), F32)],
    )
    passed = lax.ppermute(passed, "tm", ring(blocks, 1))
    psi_all = lax.all_gather(psi, "tm", axis=0)
    return call(
        last_sweep,
        lay,
        jax.ShapeDtypeStruct((steps, own, columns), F32),
        place, psi_all, in_vmem(passed), in_vmem(b_own), low, high, forcing, weights, initial_state, high_m, low_m, coarse,
    )


def solution(mesh):
    in_specs = (
        P("space", None),
        P("space", None),
        P("space", None),
        P("tm", "space", None),
        P(),
        P(),
    )
    out_specs = P("tm", "space", None)
    return jax.shard_map(per_device, mesh=mesh, in_specs=in_specs, out_specs=out_specs, check_vma=False)
```

time: 141 us -> 65.4 us (0.46)
  the two profiles are of different devices: /device:TPU:6 before, /device:TPU:0 now
where the time goes in v2:
time: 65.4 us; the launch traced here: 65 us
  blocking collectives  21.8 us (33%)
  waiting for transfers between devices  17.4 us (27%)
  Pallas kernels  14.2 us (22%)
  local copies, waits for them, and re-layouts  5.95 us (9%)
  starting transfers between devices  5.61 us (9%)
    pallas_call x5, Pallas kernels, call(): pl.pallas_call(kernel if lay is None else functools.partial(kernel, lay),...  14.2 us
    all_gather x1, blocking collectives, per_device(): psi_all = lax.all_gather(psi, 'tm', axis=0)  11.3 us
    all_gather x1, blocking collectives, per_device(): rho_all = lax.all_gather(rho, 'tm', axis=0)  10.4 us
    ppermute x1, waiting for transfers between devices, per_device(): low = in_vmem(lax.ppermute(tail, 'space', ring(slabs, 1)))  8.87 us
    ppermute x1, waiting for transfers between devices, per_device(): high = in_vmem(lax.ppermute(head, 'space', ring(slabs, -1)))  8.55 us
    unnamed x20, local copies, waits for them, and re-layouts  5.95 us
    ppermute x1, starting transfers between devices, per_device(): low = in_vmem(lax.ppermute(tail, 'space', ring(slabs, 1)))  3.1 us
    ppermute x1, starting transfers between devices, per_device(): high = in_vmem(lax.ppermute(head, 'space', ring(slabs, -1)))  2.09 us
  transfers between devices with their start and end apart: 3, of which 2 were waited for; matrix products, arithmetic and copies ran while one was open for 0% of the time, Pallas kernels for 0%

profile of v2, /device:TPU:0, one launch (start us, length us, event | category | flops | bytes accessed | tf_op | source)
XLA Modules:
  0.0 65.0 jit_solution(7665862442670958423)
XLA Ops:
  0.0 0.0 copy-start
  0.0 1.0 %copy-done = bf16[8,48,512]{2,1,0:T(8,128)(2,1)S(1)} copy-done((bf16[8,48,512]{2,1,0:T(8,128)(2,1)S(1)}, bf16[8,48,512]{2,1,0:T(8,128)(2,1)}, u32[]{:S(2)}) %copy-start) | copy-done | bytes 393240
  1.0 0.0 copy-start.4
  1.0 0.9 %copy-done.4 = f32[48,512]{1,0:T(8,128)S(1)} copy-done((f32[48,512]{1,0:T(8,128)S(1)}, f32[48,512]{1,0:T(8,128)}, u32[]{:S(2)}) %copy-start.4) | copy-done | bytes 98328
  1.9 0.0 copy-start.6
  1.9 0.8 %copy-done.6 = bf16[48,512]{1,0:T(8,128)(2,1)S(1)} copy-done((bf16[48,512]{1,0:T(8,128)(2,1)S(1)}, bf16[48,512]{1,0:T(8,128)(2,1)}, u32[]{:S(2)}) %copy-start.6) | copy-done | bytes 49176
  2.7 0.0 copy-start.8
  2.7 0.8 %copy-done.8 = bf16[48,512]{1,0:T(8,128)(2,1)S(1)} copy-done((bf16[48,512]{1,0:T(8,128)(2,1)S(1)}, bf16[48,512]{1,0:T(8,128)(2,1)}, u32[]{:S(2)}) %copy-start.8) | copy-done | bytes 49176
  3.5 0.1 pack.1
  3.6 3.1 %collective-permute-start = (bf16[456,512]{1,0:T(8,128)(2,1)S(1)}, bf16[456,512]{1,0:T(8,128)(2,1)S(1)}, u32[]{:S(2)}, u32[]{:S(2)}) collective-permute-start(bf16[456,512]{1,0:T(8,128)(2,1)S(1)} %get-tuple-element.17), channel_id=1, source_target_pairs={{0,1},{1,2},{2,3},{3,0},{4,5},{5,6},{6,7},{7,4},{8,9},{9,10},{10,1... | collective-permute-start | bytes 1400840 | tf_op jit(solution)/shard_map/ppermute | solution.py:201
  6.7 2.1 %collective-permute-start.1 = (bf16[456,512]{1,0:T(8,128)(2,1)S(1)}, bf16[456,512]{1,0:T(8,128)(2,1)S(1)}, u32[]{:S(2)}, u32[]{:S(2)}) collective-permute-start(bf16[456,512]{1,0:T(8,128)(2,1)S(1)} %get-tuple-element.18), channel_id=1, source_target_pairs={{0,3},{1,0},{2,1},{3,2},{4,7},{5,4},{6,5},{7,6},{8,11},{9,8},{10,9... | collective-permute-start | bytes 1400840 | tf_op jit(solution)/shard_map/ppermute | solution.py:202
  8.7 0.0 copy-start.2
  8.8 1.2 %copy-done.2 = f32[512,512]{1,0:T(8,128)S(1)} copy-done((f32[512,512]{1,0:T(8,128)S(1)}, f32[512,512]{1,0:T(8,128)}, u32[]{:S(2)}) %copy-start.2) | copy-done | bytes 1048600
  10.0 0.0 copy-start.3
  10.0 1.2 %copy-done.3 = f32[512,512]{1,0:T(8,128)S(1)} copy-done((f32[512,512]{1,0:T(8,128)S(1)}, f32[512,512]{1,0:T(8,128)}, u32[]{:S(2)}) %copy-start.3) | copy-done | bytes 1048600
  11.2 0.0 copy-start.1
  11.2 0.0 copy-start.5
  11.2 0.0 copy-start.7
  11.2 0.2 split_matrices.1
  11.4 8.9 %collective-permute-done.low = bf16[456,512]{1,0:T(8,128)(2,1)S(1)} collective-permute-done((bf16[456,512]{1,0:T(8,128)(2,1)S(1)}, bf16[456,512]{1,0:T(8,128)(2,1)S(1)}, u32[]{:S(2)}, u32[]{:S(2)}) %collective-permute-start) | collective-permute-done | bytes 466976 | tf_op jit(solution)/shard_map/ppermute | solution.py:201
  20.3 8.5 %collective-permute-done.1.high = bf16[456,512]{1,0:T(8,128)(2,1)S(1)} collective-permute-done((bf16[456,512]{1,0:T(8,128)(2,1)S(1)}, bf16[456,512]{1,0:T(8,128)(2,1)S(1)}, u32[]{:S(2)}, u32[]{:S(2)}) %collective-permute-start.1) | collective-permute-done | bytes 466976 | tf_op jit(solution)/shard_map/ppermute | solution.py:202
  28.8 0.0 copy-done.1
  28.8 0.0 copy-done.5
  28.8 0.0 copy-done.7
  28.8 0.0 copy-done.9
  28.8 6.0 %two_sweeps.1 = (bf16[96,512]{1,0:T(8,128)(2,1)S(1)}, bf16[48,512]{1,0:T(8,128)(2,1)S(1)}, f32[64,512]{1,0:T(8,128)S(1)}, f32[3,128,512]{2,1,0:T(8,128)S(1)}) custom-call(s32[1]{0:T(128)} %bitcast.place, bf16[456,512]{1,0:T(8,128)(2,1)S(1)} %collective-permute-done.low, bf16[456,512]{1,0:T(8,128)(2,1)S(1)} %collective-permute-done.1.high, ...), custom_call_target="tpu_custom_call" | custom-call | tf_op jit(solution)/shard_map/two_sweeps/pallas_call | solution.py:177
  34.8 10.4 %all-gather = bf16[768,512]{1,0:T(8,128)(2,1)S(1)} all-gather(bf16[96,512]{1,0:T(8,128)(2,1)S(1)} %get-tuple-element.21), channel_id=2, replica_groups=mesh['tm'=8,'space'=4] {'tm'}, dimensions={0}, use_global_device_ids=true | all-gather | bytes 884736 | tf_op jit(solution)/shard_map/all_gather | solution.py:219
  45.3 4.8 %coarse_and_third.1 = (bf16[64,512]{1,0:T(8,128)(2,1)S(1)}, bf16[176,512]{1,0:T(8,128)(2,1)S(1)}, f32[48,512]{1,0:T(8,128)S(1)}) custom-call(s32[1]{0:T(128)} %bitcast.place, bf16[8,96,512]{2,1,0:T(8,128)(2,1)S(1)} %bitcast.3, bf16[48,512]{1,0:T(8,128)(2,1)S(1)} %get-tuple-element.22.rho_low, f32[64,512]{1,0:T(8,128)S(1)} %get-tuple-element.23.a_near, ...), custom_call_target="tpu_custom_call" | custom-call | tf_op jit(solution)/shard_map/coarse_and_third/pallas_call | solution.py:177
  50.1 0.4 collective-permute-start.2
  50.5 11.3 %all-gather.1 = bf16[512,512]{1,0:T(8,128)(2,1)S(1)} all-gather(bf16[64,512]{1,0:T(8,128)(2,1)S(1)} %get-tuple-element.26), channel_id=3, replica_groups=mesh['tm'=8,'space'=4] {'tm'}, dimensions={0}, use_global_device_ids=true | all-gather | bytes 589824 | tf_op jit(solution)/shard_map/all_gather | solution.py:232
  61.9 0.0 collective-permute-done.2.passed
  61.9 3.1 %last_sweep.1 = f32[8,48,512]{2,1,0:T(8,128)} custom-call(s32[1]{0:T(128)} %bitcast.place, bf16[8,64,512]{2,1,0:T(8,128)(2,1)S(1)} %bitcast.4, bf16[176,512]{1,0:T(8,128)(2,1)S(1)} %collective-permute-done.2.passed, f32[48,512]{1,0:T(8,128)S(1)} %get-tuple-element.28.b_own, bf16[456,512]{1,0:T(8,128)(2,1)S(1)} %collective-permute-done.low, ...), custom_call_target="tpu_custom_call" | custom-call | tf_op jit(solution)/shard_map/last_sweep/pallas_call | solution.py:177
  (1 shorter events, 0.0 us)
Async XLA Ops:
  0.0 1.0 %copy-start = (bf16[8,48,512]{2,1,0:T(8,128)(2,1)S(1)}, bf16[8,48,512]{2,1,0:T(8,128)(2,1)}, u32[]{:S(2)}) copy-start(bf16[8,48,512]{2,1,0:T(8,128)(2,1)} %forcing.5) | copy-start | bytes 1179652
  1.0 0.9 %copy-start.4 = (f32[48,512]{1,0:T(8,128)S(1)}, f32[48,512]{1,0:T(8,128)}, u32[]{:S(2)}) copy-start(f32[48,512]{1,0:T(8,128)} %start.5) | copy-start | bytes 294916
  1.9 0.8 %copy-start.6 = (bf16[48,512]{1,0:T(8,128)(2,1)S(1)}, bf16[48,512]{1,0:T(8,128)(2,1)}, u32[]{:S(2)}) copy-start(bf16[48,512]{1,0:T(8,128)(2,1)} %velocity.3) | copy-start | bytes 147460
  2.7 0.8 %copy-start.8 = (bf16[48,512]{1,0:T(8,128)(2,1)S(1)}, bf16[48,512]{1,0:T(8,128)(2,1)}, u32[]{:S(2)}) copy-start(bf16[48,512]{1,0:T(8,128)(2,1)} %diffusion.3) | copy-start | bytes 147460
  3.6 16.7 %collective-permute-start = (bf16[456,512]{1,0:T(8,128)(2,1)S(1)}, bf16[456,512]{1,0:T(8,128)(2,1)S(1)}, u32[]{:S(2)}, u32[]{:S(2)}) collective-permute-start(bf16[456,512]{1,0:T(8,128)(2,1)S(1)} %get-tuple-element.17), channel_id=1, source_target_pairs={{0,1},{1,2},{2,3},{3,0},{4,5},{5,6},{6,7},{7,4},{8,9},{9,10},{10,1... | collective-permute-start | bytes 1400840 | tf_op jit(solution)/shard_map/ppermute | solution.py:201
  6.7 22.2 %collective-permute-start.1 = (bf16[456,512]{1,0:T(8,128)(2,1)S(1)}, bf16[456,512]{1,0:T(8,128)(2,1)S(1)}, u32[]{:S(2)}, u32[]{:S(2)}) collective-permute-start(bf16[456,512]{1,0:T(8,128)(2,1)S(1)} %get-tuple-element.18), channel_id=1, source_target_pairs={{0,3},{1,0},{2,1},{3,2},{4,7},{5,4},{6,5},{7,6},{8,11},{9,8},{10,9... | collective-permute-start | bytes 1400840 | tf_op jit(solution)/shard_map/ppermute | solution.py:202
  8.7 1.2 %copy-start.2 = (f32[512,512]{1,0:T(8,128)S(1)}, f32[512,512]{1,0:T(8,128)}, u32[]{:S(2)}) copy-start(f32[512,512]{1,0:T(8,128)} %implicit.1) | copy-start | bytes 3145732
  10.0 1.2 %copy-start.3 = (f32[512,512]{1,0:T(8,128)S(1)}, f32[512,512]{1,0:T(8,128)}, u32[]{:S(2)}) copy-start(f32[512,512]{1,0:T(8,128)} %coarse_implicit.1) | copy-start | bytes 3145732
  11.2 17.6 %copy-start.1 = (bf16[8,48,512]{2,1,0:T(8,128)(2,1)S(1)}, bf16[8,48,512]{2,1,0:T(8,128)(2,1)}, u32[]{:S(2)}) copy-start(bf16[8,48,512]{2,1,0:T(8,128)(2,1)} %forcing.5) | copy-start | bytes 1179652
  11.2 17.6 %copy-start.5 = (f32[48,512]{1,0:T(8,128)S(1)}, f32[48,512]{1,0:T(8,128)}, u32[]{:S(2)}) copy-start(f32[48,512]{1,0:T(8,128)} %start.5) | copy-start | bytes 294916
  11.2 17.6 %copy-start.7 = (bf16[48,512]{1,0:T(8,128)(2,1)S(1)}, bf16[48,512]{1,0:T(8,128)(2,1)}, u32[]{:S(2)}) copy-start(bf16[48,512]{1,0:T(8,128)(2,1)} %velocity.3) | copy-start | bytes 147460
  11.2 17.6 %copy-start.9 = (bf16[48,512]{1,0:T(8,128)(2,1)S(1)}, bf16[48,512]{1,0:T(8,128)(2,1)}, u32[]{:S(2)}) copy-start(bf16[48,512]{1,0:T(8,128)(2,1)} %diffusion.3) | copy-start | bytes 147460
  50.1 11.8 %collective-permute-start.2 = (bf16[176,512]{1,0:T(8,128)(2,1)S(1)}, bf16[176,512]{1,0:T(8,128)(2,1)S(1)}, u32[]{:S(2)}, u32[]{:S(2)}) collective-permute-start(bf16[176,512]{1,0:T(8,128)(2,1)S(1)} %get-tuple-element.27), channel_id=1, source_target_pairs={{0,4},{4,8},{8,12},{12,16},{16,20},{20,24},{24,28},{28,0},{1,5},{5... | collective-permute-start | bytes 540680 | tf_op jit(solution)/shard_map/ppermute | solution.py:231

commit v3 on v2

--- a/solution.py
+++ b/solution.py
@@ -9,6 +9,7 @@
 
 F32 = jnp.float32
 BF16 = jnp.bfloat16
+LIMIT = 16 << 20
 
 
 def ring(count, distance):
@@ -40,29 +41,41 @@
     def __init__(self, steps, own):
         self.steps = steps
         self.own = own
-        self.wide = 5 * steps
+        self.wide = 4 * steps
         self.keep = 3 * steps
         self.fine = 2 * steps
-        self.velocity = steps * self.wide
-        self.diffusion = self.velocity + self.wide
-        self.start = self.diffusion + self.wide
-        self.start_low = self.start + self.wide
-        self.rows = self.start_low + self.fine
+        self.velocity = steps * steps
+        self.diffusion = self.velocity + steps
+        self.start = self.diffusion + steps
+        self.start_low = self.start + steps
+        self.first_rows = self.start_low + steps
+        self.tail = self.wide
+        self.far_velocity = self.tail + self.fine
+        self.far_diffusion = self.far_velocity + self.wide
+        self.second_rows = self.far_diffusion + self.wide
 
     def centred(self, width, inside):
         return slice(width - inside, width + self.own + inside)
 
 
-def pack(lay, velocity, diffusion, forcing, start, head, tail):
-    for out, first in ((head, 0), (tail, lay.own - lay.wide)):
-        near = slice(first, first + lay.wide)
-        for step in range(lay.steps):
-            out[step * lay.wide : (step + 1) * lay.wide] = forcing[step, near]
-        out[lay.velocity : lay.diffusion] = velocity[near]
-        out[lay.diffusion : lay.start] = diffusion[near]
-        high, low = split(start[near])
+def pack(lay, velocity, diffusion, forcing, start, head, tail, start_kept, semaphores):
+    steps, own = lay.steps, lay.own
+    copies = [(start, start_kept)]
+    for out, first in ((head, 0), (tail, own - steps)):
+        near = pl.ds(first, steps)
+        for step in range(steps):
+            copies.append((forcing.at[step, near], out.at[pl.ds(step * steps, steps)]))
+        copies.append((velocity.at[near], out.at[pl.ds(lay.velocity, steps)]))
+        copies.append((diffusion.at[near], out.at[pl.ds(lay.diffusion, steps)]))
+    copies = [pltpu.make_async_copy(*pair, semaphores.at[i]) for i, pair in enumerate(copies)]
+    for copy in copies:
+        copy.start()
+    for copy in copies:
+        copy.wait()
+    for out, first in ((head, 0), (tail, own - steps)):
+        high, low = split(start_kept[first : first + steps])
         out[lay.start : lay.start_low] = high
-        out[lay.start_low : lay.rows] = low[: lay.fine] if first == 0 else low[lay.wide - lay.fine :]
+        out[lay.start_low : lay.first_rows] = low
 
 
 def split_matrices(implicit, coarse_implicit, high_m, low_m, coarse):
@@ -70,53 +83,68 @@
     coarse[...] = coarse_implicit[...].astype(BF16)
 
 
-def from_packs(lay, low, own, high, at, width):
-    return jnp.concatenate(
-        [
-            low[at + lay.wide - width : at + lay.wide].astype(F32),
-            own.astype(F32),
-            high[at : at + width].astype(F32),
-        ],
-        axis=0,
-    )
-
-
-def start_from_packs(lay, low, own, high, width):
-    value = from_packs(lay, low, own, high, lay.start, width)
-    fine = min(width, lay.fine)
-    low_tail = low[lay.start_low + lay.fine - fine : lay.rows].astype(F32)
-    high_tail = high[lay.start_low : lay.start_low + fine].astype(F32)
-    pieces = [
-        value[: width - fine] if width > fine else None,
-        value[width - fine : width] + low_tail,
-        value[width : width + lay.own],
-        value[width + lay.own : width + lay.own + fine] + high_tail,
-        value[width + lay.own + fine :] if width > fine else None,
-    ]
-    return jnp.concatenate([piece for piece in pieces if piece is not None], axis=0)
-
-
-def two_sweeps(lay, place, low, high, forcing, velocity, diffusion, start, high_m, low_m, rho, rho_low, a_near, weights):
-    wide, steps = lay.wide, lay.steps
-    moving = from_packs(lay, low, velocity[...], high, lay.velocity, wide)
-    spread = from_packs(lay, low, diffusion[...], high, lay.diffusion, wide)
-    weights[0] = spread + 0.5 * moving
-    weights[1] = 1.0 - 2.0 * spread
-    weights[2] = spread - 0.5 * moving
-    current = start_from_packs(lay, low, start[...], high, wide)
-    current = jnp.where(place[0] == 0, current, 0.0)
+def joined(low, own, high):
+    return jnp.concatenate([low.astype(F32), own.astype(F32), high.astype(F32)], axis=0)
+
+
+def from_first(lay, low, own, high, at):
+    rows = slice(at, at + lay.steps)
+    return joined(low[rows], own, high[rows])
+
+
+def start_from_first(lay, low, own, high):
+    value = from_first(lay, low, own, high, lay.start)
+    return value + from_first(lay, low, jnp.zeros(own.shape, F32), high, lay.start_low)
+
+
+def make_weights(moving, spread):
+    return spread + 0.5 * moving, 1.0 - 2.0 * spread, spread - 0.5 * moving
+
+
+def first_sweep(lay, place, low, high, forcing, velocity, diffusion, start, high_m, low_m, a, head, tail):
+    steps, own = lay.steps, lay.own
+    weights = make_weights(
+        from_first(lay, low, velocity[...], high, lay.velocity),
+        from_first(lay, low, diffusion[...], high, lay.diffusion),
+    )
+    current = jnp.where(place[0] == 0, start_from_first(lay, low, start[...], high), 0.0)
     for step in range(steps):
-        summed = stencil(current, weights[...]) + from_packs(lay, low, forcing[step], high, step * wide, wide)
+        summed = stencil(current, weights) + from_first(lay, low, forcing[step], high, step * steps)
         current = product3(summed, high_m[...], low_m[...])
+    current = current[lay.centred(steps, 0)]
+    a[...] = current
+    high_part, low_part = split(current)
+    for out, far, near in (
+        (head, slice(0, lay.wide), slice(0, lay.fine)),
+        (tail, slice(own - lay.wide, own), slice(own - lay.fine, own)),
+    ):
+        out[: lay.tail] = high_part[far]
+        out[lay.tail : lay.far_velocity] = low_part[near]
+        out[lay.far_velocity : lay.far_diffusion] = velocity[far]
+        out[lay.far_diffusion :] = diffusion[far]
+
+
+def second_sweep(lay, low, high, a, velocity, diffusion, high_m, low_m, rho, rho_low, a_near, weights):
+    wide, steps, fine = lay.wide, lay.steps, lay.fine
+
+    def extended(own, at):
+        return joined(low[at : at + wide], own, high[at : at + wide])
+
+    weights[0], weights[1], weights[2] = make_weights(
+        extended(velocity[...], lay.far_velocity), extended(diffusion[...], lay.far_diffusion)
+    )
+    tails = slice(lay.tail, lay.far_velocity)
+    current = joined(
+        jnp.concatenate([low[: wide - fine].astype(F32), low[wide - fine : wide].astype(F32) + low[tails].astype(F32)], axis=0),
+        a[...],
+        jnp.concatenate([high[:fine].astype(F32) + high[tails].astype(F32), high[fine:wide].astype(F32)], axis=0),
+    )
     a_near[...] = current[lay.centred(wide, steps)]
-    width = wide - steps
-    current = current[lay.centred(wide, width)]
-    narrow = weights[:, lay.centred(wide, width)]
     for _ in range(steps):
-        current = product3(stencil(current, narrow), high_m[...], low_m[...])
+        current = product3(stencil(current, weights[...]), high_m[...], low_m[...])
     high_part, low_part = split(current)
-    rho[...] = high_part[lay.centred(width, lay.keep)]
-    rho_low[...] = low_part[lay.centred(width, 0)]
+    rho[...] = high_part[lay.centred(wide, lay.keep)]
+    rho_low[...] = low_part[lay.centred(wide, 0)]
 
 
 def coarse_and_third(lay, place, rho, rho_low, a_near, weights, high_m, low_m, coarse, psi, passed, b_own, error_kept):
@@ -156,14 +184,14 @@
 
     error = lax.fori_loop(2, at - 1, turn, jnp.zeros((rows, start.shape[1]), F32))
     b_before = passed[:rows].astype(F32) + passed[rows : 2 * rows].astype(F32)
-    initial = start_from_packs(lay, low, start[...], high, steps)
+    initial = start_from_first(lay, low, start[...], high)
     current = jnp.where(at == 0, initial, b_before + error)
     mid = lay.centred(steps, 0)
     last = product(error[mid].astype(BF16), coarse[...]) + psi[jnp.maximum(at - 1, 0)].astype(F32)[mid]
     last = last + passed[2 * rows :].astype(F32)
     out[steps - 1] = b_own[...] + jnp.where(at == 0, 0.0, last)
     for step in range(steps - 1):
-        summed = stencil(current, narrow) + from_packs(lay, low, forcing[step], high, step * lay.wide, steps)
+        summed = stencil(current, narrow) + from_first(lay, low, forcing[step], high, step * steps)
         current = product3(summed, high_m[...], low_m[...])
         out[step] = current[mid]
 
@@ -180,7 +208,7 @@
         in_specs=[pl.BlockSpec(memory_space=space) for space in spaces],
         out_specs=jax.tree.map(lambda _: pl.BlockSpec(memory_space=pltpu.VMEM), outs),
         scratch_shapes=scratch,
-        compiler_params=pltpu.CompilerParams(vmem_limit_bytes=16 << 20),
+        compiler_params=pltpu.CompilerParams(vmem_limit_bytes=LIMIT),
         name=kernel.__name__,
     )(*operands)
 
@@ -197,15 +225,34 @@
     def kept(*shape, dtype=F32):
         return pltpu.VMEM(shape, dtype)
 
-    head, tail = call(pack, lay, [kept(lay.rows, columns, dtype=BF16)] * 2, velocity, diffusion, forcing, initial_state)
+    first_pack = kept(lay.first_rows, columns, dtype=BF16)
+    hbm = pl.BlockSpec(memory_space=pltpu.HBM)
+    head, tail = pl.pallas_call(
+        functools.partial(pack, lay),
+        out_shape=[first_pack] * 2,
+        in_specs=[hbm] * 4,
+        out_specs=[pl.BlockSpec(memory_space=pltpu.VMEM)] * 2,
+        scratch_shapes=[pltpu.VMEM((own, columns), F32), pltpu.SemaphoreType.DMA((1 + 2 * (steps + 2),))],
+        compiler_params=pltpu.CompilerParams(vmem_limit_bytes=LIMIT),
+        name="pack",
+    )(*(pltpu.with_memory_space_constraint(x, pltpu.HBM) for x in (velocity, diffusion, forcing, initial_state)))
     low = in_vmem(lax.ppermute(tail, "space", ring(slabs, 1)))
     high = in_vmem(lax.ppermute(head, "space", ring(slabs, -1)))
     high_m, low_m, coarse = call(
         split_matrices, None, [kept(*implicit.shape, dtype=BF16)] * 3, implicit, coarse_implicit
     )
     high_m, low_m, coarse = in_vmem(high_m), in_vmem(low_m), in_vmem(coarse)
+    second_pack = kept(lay.second_rows, columns, dtype=BF16)
+    a, head, tail = call(
+        first_sweep,
+        lay,
+        [kept(own, columns), second_pack, second_pack],
+        place, low, high, forcing, velocity, diffusion, initial_state, high_m, low_m,
+    )
+    far_low = in_vmem(lax.ppermute(tail, "space", ring(slabs, 1)))
+    far_high = in_vmem(lax.ppermute(head, "space", ring(slabs, -1)))
     rho, rho_low, a_near, weights = call(
-        two_sweeps,
+        second_sweep,
         lay,
         [
             kept(own + 2 * lay.keep, columns, dtype=BF16),
@@ -213,7 +260,7 @@
             kept(near, columns),
             kept(3, own + 2 * lay.wide, columns),
         ],
-        place, low, high, forcing, velocity, diffusion, initial_state, high_m, low_m,
+        far_low, far_high, in_vmem(a), velocity, diffusion, high_m, low_m,
     )
     weights = in_vmem(weights)
     rho_all = lax.all_gather(rho, "tm", axis=0)

time: 65.4 us -> 54.8 us (0.84)
  waiting for transfers between devices: 17.4 us -> 6.05 us
  starting transfers between devices: 5.61 us -> 9.48 us
  local copies, waits for them, and re-layouts: 5.95 us -> 2.46 us
    ppermute x1, waiting for transfers between devices: 8.87 us -> 0.71 us  [per_device(): low = in_vmem(lax.ppermute(tail, 'space', ring(slabs, 1)))]
    ppermute x1, waiting for transfers between devices: 8.55 us -> 0.9 us  [per_device(): high = in_vmem(lax.ppermute(head, 'space', ring(slabs, -1)))]
    ppermute x0 -> x2, waiting for transfers between devices: none -> 4.44 us  [the longest x1 3.75 us: per_device(): far_low = in_vmem(lax.ppermute(tail, 'space', ring(slabs, 1)))]
    ppermute x0 -> x2, starting transfers between devices: none -> 3.88 us  [the longest x1 2.7 us: per_device(): far_high = in_vmem(lax.ppermute(head, 'space', ring(slabs, -1)))]
    unnamed x20 -> x12, local copies, waits for them, and re-layouts: 5.95 us -> 2.46 us
    pallas_call x0 -> x1, Pallas kernels: none -> 1.12 us  [per_device(): pl.pallas_call(functools.partial(pack, lay), out_shape=[first_pack] * 2,...]
  transfers between devices with their start and end apart: 3 -> 5, of which waited for: 2 -> 4; matrix products, arithmetic and copies ran while one was open for 0% -> 0% of each run, Pallas kernels for 0% -> 0%
where the time goes in v3:
time: 54.8 us; the launch traced here: 54.5 us
  blocking collectives  21.8 us (40%)
  Pallas kernels  14.7 us (27%)
  starting transfers between devices  9.48 us (17%)
  waiting for transfers between devices  6.05 us (11%)
  local copies, waits for them, and re-layouts  2.46 us (4%)
    pallas_call x5, Pallas kernels, call(): pl.pallas_call(kernel if lay is None else functools.partial(kernel, lay),...  13.6 us
    all_gather x1, blocking collectives, per_device(): psi_all = lax.all_gather(psi, 'tm', axis=0)  11.4 us
    all_gather x1, blocking collectives, per_device(): rho_all = lax.all_gather(rho, 'tm', axis=0)  10.4 us
    ppermute x1, waiting for transfers between devices, per_device(): far_low = in_vmem(lax.ppermute(tail, 'space', ring(slabs, 1)))  3.75 us
    ppermute x1, starting transfers between devices, per_device(): low = in_vmem(lax.ppermute(tail, 'space', ring(slabs, 1)))  3.1 us
    ppermute x1, starting transfers between devices, per_device(): far_high = in_vmem(lax.ppermute(head, 'space', ring(slabs, -1)))  2.7 us
    unnamed x12, local copies, waits for them, and re-layouts  2.46 us
    ppermute x1, starting transfers between devices, per_device(): high = in_vmem(lax.ppermute(head, 'space', ring(slabs, -1)))  2.09 us
  transfers between devices with their start and end apart: 5, of which 4 were waited for; matrix products, arithmetic and copies ran while one was open for 0% of the time, Pallas kernels for 0%

profile of v3, /device:TPU:0, one launch (start us, length us, event | category | flops | bytes accessed | tf_op | source)
XLA Modules:
  0.0 54.5 jit_solution(12965235844639801562)
XLA Ops:
  0.0 1.1 %pack.1 = (bf16[96,512]{1,0:T(8,128)(2,1)S(1)}, bf16[96,512]{1,0:T(8,128)(2,1)S(1)}) custom-call(bf16[48,512]{1,0:T(8,128)(2,1)} %velocity.5, bf16[48,512]{1,0:T(8,128)(2,1)} %diffusion.5, bf16[8,48,512]{2,1,0:T(8,128)(2,1)} %forcing.5, f32[48,512]{1,0:T(8,128)} %start.5), custom_call_target="tpu_custom_call" | custom-call | tf_op jit(solution)/shard_map/pack/pallas_call | solution.py:230
  1.1 3.1 %collective-permute-start = (bf16[96,512]{1,0:T(8,128)(2,1)S(1)}, bf16[96,512]{1,0:T(8,128)(2,1)S(1)}, u32[]{:S(2)}, u32[]{:S(2)}) collective-permute-start(bf16[96,512]{1,0:T(8,128)(2,1)S(1)} %get-tuple-element.20), channel_id=1, source_target_pairs={{0,1},{1,2},{2,3},{3,0},{4,5},{5,6},{6,7},{7,4},{8,9},{9,10},{10,1... | collective-permute-start | bytes 294920 | tf_op jit(solution)/shard_map/ppermute | solution.py:239
  4.2 2.1 %collective-permute-start.1 = (bf16[96,512]{1,0:T(8,128)(2,1)S(1)}, bf16[96,512]{1,0:T(8,128)(2,1)S(1)}, u32[]{:S(2)}, u32[]{:S(2)}) collective-permute-start(bf16[96,512]{1,0:T(8,128)(2,1)S(1)} %get-tuple-element.21), channel_id=1, source_target_pairs={{0,3},{1,0},{2,1},{3,2},{4,7},{5,4},{6,5},{7,6},{8,11},{9,8},{10,9... | collective-permute-start | bytes 294920 | tf_op jit(solution)/shard_map/ppermute | solution.py:240
  6.3 0.0 copy-start.1
  6.3 1.2 %copy-done.1 = f32[512,512]{1,0:T(8,128)S(1)} copy-done((f32[512,512]{1,0:T(8,128)S(1)}, f32[512,512]{1,0:T(8,128)}, u32[]{:S(2)}) %copy-start.1) | copy-done | bytes 1048600
  7.5 0.0 copy-start.2
  7.6 1.2 %copy-done.2 = f32[512,512]{1,0:T(8,128)S(1)} copy-done((f32[512,512]{1,0:T(8,128)S(1)}, f32[512,512]{1,0:T(8,128)}, u32[]{:S(2)}) %copy-start.2) | copy-done | bytes 1048600
  8.8 0.0 copy-start
  8.8 0.0 copy-start.3
  8.8 0.0 copy-start.4
  8.8 0.0 copy-start.5
  8.8 0.2 split_matrices.1
  9.0 0.7 %collective-permute-done.low = bf16[96,512]{1,0:T(8,128)(2,1)S(1)} collective-permute-done((bf16[96,512]{1,0:T(8,128)(2,1)S(1)}, bf16[96,512]{1,0:T(8,128)(2,1)S(1)}, u32[]{:S(2)}, u32[]{:S(2)}) %collective-permute-start) | collective-permute-done | bytes 98336 | tf_op jit(solution)/shard_map/ppermute | solution.py:239
  9.7 0.9 %collective-permute-done.1.high = bf16[96,512]{1,0:T(8,128)(2,1)S(1)} collective-permute-done((bf16[96,512]{1,0:T(8,128)(2,1)S(1)}, bf16[96,512]{1,0:T(8,128)(2,1)S(1)}, u32[]{:S(2)}, u32[]{:S(2)}) %collective-permute-start.1) | collective-permute-done | bytes 98336 | tf_op jit(solution)/shard_map/ppermute | solution.py:240
  10.6 0.0 copy-done
  10.6 0.0 copy-done.3
  10.6 0.0 copy-done.4
  10.6 0.0 copy-done.5
  10.6 2.4 %first_sweep.1 = (f32[48,512]{1,0:T(8,128)S(1)}, bf16[112,512]{1,0:T(8,128)(2,1)S(1)}, bf16[112,512]{1,0:T(8,128)(2,1)S(1)}) custom-call(s32[1]{0:T(128)} %bitcast.place, bf16[96,512]{1,0:T(8,128)(2,1)S(1)} %collective-permute-done.low, bf16[96,512]{1,0:T(8,128)(2,1)S(1)} %collective-permute-done.1.high, bf16[8,48,512]{2,1,0:T(8,128)(2,1)S(1)} %copy-done, ...), custom_call_target="tpu_custom_call" | custom-call | tf_op jit(solution)/shard_map/first_sweep/pallas_call | solution.py:205
  13.0 1.2 %collective-permute-start.2 = (bf16[112,512]{1,0:T(8,128)(2,1)S(1)}, bf16[112,512]{1,0:T(8,128)(2,1)S(1)}, u32[]{:S(2)}, u32[]{:S(2)}) collective-permute-start(bf16[112,512]{1,0:T(8,128)(2,1)S(1)} %get-tuple-element.24), channel_id=1, source_target_pairs={{0,1},{1,2},{2,3},{3,0},{4,5},{5,6},{6,7},{7,4},{8,9},{9,10},{10,1... | collective-permute-start | bytes 344072 | tf_op jit(solution)/shard_map/ppermute | solution.py:252
  14.2 2.7 %collective-permute-start.3 = (bf16[112,512]{1,0:T(8,128)(2,1)S(1)}, bf16[112,512]{1,0:T(8,128)(2,1)S(1)}, u32[]{:S(2)}, u32[]{:S(2)}) collective-permute-start(bf16[112,512]{1,0:T(8,128)(2,1)S(1)} %get-tuple-element.25), channel_id=1, source_target_pairs={{0,3},{1,0},{2,1},{3,2},{4,7},{5,4},{6,5},{7,6},{8,11},{9,8},{10,9... | collective-permute-start | bytes 344072 | tf_op jit(solution)/shard_map/ppermute | solution.py:253
  16.9 3.8 %collective-permute-done.2.low = bf16[112,512]{1,0:T(8,128)(2,1)S(1)} collective-permute-done((bf16[112,512]{1,0:T(8,128)(2,1)S(1)}, bf16[112,512]{1,0:T(8,128)(2,1)S(1)}, u32[]{:S(2)}, u32[]{:S(2)}) %collective-permute-start.2) | collective-permute-done | bytes 114720 | tf_op jit(solution)/shard_map/ppermute | solution.py:252
  20.7 0.7 %collective-permute-done.3.high = bf16[112,512]{1,0:T(8,128)(2,1)S(1)} collective-permute-done((bf16[112,512]{1,0:T(8,128)(2,1)S(1)}, bf16[112,512]{1,0:T(8,128)(2,1)S(1)}, u32[]{:S(2)}, u32[]{:S(2)}) %collective-permute-start.3) | collective-permute-done | bytes 114720 | tf_op jit(solution)/shard_map/ppermute | solution.py:253
  21.4 3.0 %second_sweep.1 = (bf16[96,512]{1,0:T(8,128)(2,1)S(1)}, bf16[48,512]{1,0:T(8,128)(2,1)S(1)}, f32[64,512]{1,0:T(8,128)S(1)}, f32[3,112,512]{2,1,0:T(8,128)S(1)}) custom-call(bf16[112,512]{1,0:T(8,128)(2,1)S(1)} %collective-permute-done.2.low, bf16[112,512]{1,0:T(8,128)(2,1)S(1)} %collective-permute-done.3.high, f32[48,512]{1,0:T(8,128)S(1)} %get-tuple-element.26.a, ...), custom_call_target="tpu_custom_call" | custom-call | tf_op jit(solution)/shard_map/second_sweep/pallas_call | solution.py:205
  24.4 10.4 %all-gather = bf16[768,512]{1,0:T(8,128)(2,1)S(1)} all-gather(bf16[96,512]{1,0:T(8,128)(2,1)S(1)} %get-tuple-element.27), channel_id=2, replica_groups=mesh['tm'=8,'space'=4] {'tm'}, dimensions={0}, use_global_device_ids=true | all-gather | bytes 884736 | tf_op jit(solution)/shard_map/all_gather | solution.py:266
  34.8 4.8 %coarse_and_third.1 = (bf16[64,512]{1,0:T(8,128)(2,1)S(1)}, bf16[176,512]{1,0:T(8,128)(2,1)S(1)}, f32[48,512]{1,0:T(8,128)S(1)}) custom-call(s32[1]{0:T(128)} %bitcast.place, bf16[8,96,512]{2,1,0:T(8,128)(2,1)S(1)} %bitcast.3, bf16[48,512]{1,0:T(8,128)(2,1)S(1)} %get-tuple-element.28.rho_low, f32[64,512]{1,0:T(8,128)S(1)} %get-tuple-element.29.a_near, ...), custom_call_target="tpu_custom_call" | custom-call | tf_op jit(solution)/shard_map/coarse_and_third/pallas_call | solution.py:205
  39.6 0.4 collective-permute-start.4
  40.0 11.4 %all-gather.1 = bf16[512,512]{1,0:T(8,128)(2,1)S(1)} all-gather(bf16[64,512]{1,0:T(8,128)(2,1)S(1)} %get-tuple-element.32), channel_id=3, replica_groups=mesh['tm'=8,'space'=4] {'tm'}, dimensions={0}, use_global_device_ids=true | all-gather | bytes 589824 | tf_op jit(solution)/shard_map/all_gather | solution.py:279
  51.4 0.0 collective-permute-done.4.passed
  51.4 3.1 %last_sweep.1 = f32[8,48,512]{2,1,0:T(8,128)} custom-call(s32[1]{0:T(128)} %bitcast.place, bf16[8,64,512]{2,1,0:T(8,128)(2,1)S(1)} %bitcast.4, bf16[176,512]{1,0:T(8,128)(2,1)S(1)} %collective-permute-done.4.passed, f32[48,512]{1,0:T(8,128)S(1)} %get-tuple-element.34.b_own, bf16[96,512]{1,0:T(8,128)(2,1)S(1)} %collective-permute-done.low, ...), custom_call_target="tpu_custom_call" | custom-call | tf_op jit(solution)/shard_map/last_sweep/pallas_call | solution.py:205
Async XLA Ops:
  1.1 8.6 %collective-permute-start = (bf16[96,512]{1,0:T(8,128)(2,1)S(1)}, bf16[96,512]{1,0:T(8,128)(2,1)S(1)}, u32[]{:S(2)}, u32[]{:S(2)}) collective-permute-start(bf16[96,512]{1,0:T(8,128)(2,1)S(1)} %get-tuple-element.20), channel_id=1, source_target_pairs={{0,1},{1,2},{2,3},{3,0},{4,5},{5,6},{6,7},{7,4},{8,9},{9,10},{10,1... | collective-permute-start | bytes 294920 | tf_op jit(solution)/shard_map/ppermute | solution.py:239
  4.2 6.4 %collective-permute-start.1 = (bf16[96,512]{1,0:T(8,128)(2,1)S(1)}, bf16[96,512]{1,0:T(8,128)(2,1)S(1)}, u32[]{:S(2)}, u32[]{:S(2)}) collective-permute-start(bf16[96,512]{1,0:T(8,128)(2,1)S(1)} %get-tuple-element.21), channel_id=1, source_target_pairs={{0,3},{1,0},{2,1},{3,2},{4,7},{5,4},{6,5},{7,6},{8,11},{9,8},{10,9... | collective-permute-start | bytes 294920 | tf_op jit(solution)/shard_map/ppermute | solution.py:240
  6.3 1.2 %copy-start.1 = (f32[512,512]{1,0:T(8,128)S(1)}, f32[512,512]{1,0:T(8,128)}, u32[]{:S(2)}) copy-start(f32[512,512]{1,0:T(8,128)} %implicit.1) | copy-start | bytes 3145732
  7.5 1.2 %copy-start.2 = (f32[512,512]{1,0:T(8,128)S(1)}, f32[512,512]{1,0:T(8,128)}, u32[]{:S(2)}) copy-start(f32[512,512]{1,0:T(8,128)} %coarse_implicit.1) | copy-start | bytes 3145732
  8.8 1.8 %copy-start = (bf16[8,48,512]{2,1,0:T(8,128)(2,1)S(1)}, bf16[8,48,512]{2,1,0:T(8,128)(2,1)}, u32[]{:S(2)}) copy-start(bf16[8,48,512]{2,1,0:T(8,128)(2,1)} %forcing.5) | copy-start | bytes 1179652
  8.8 1.8 %copy-start.3 = (f32[48,512]{1,0:T(8,128)S(1)}, f32[48,512]{1,0:T(8,128)}, u32[]{:S(2)}) copy-start(f32[48,512]{1,0:T(8,128)} %start.5) | copy-start | bytes 294916
  8.8 1.8 %copy-start.4 = (bf16[48,512]{1,0:T(8,128)(2,1)S(1)}, bf16[48,512]{1,0:T(8,128)(2,1)}, u32[]{:S(2)}) copy-start(bf16[48,512]{1,0:T(8,128)(2,1)} %velocity.5) | copy-start | bytes 147460
  8.8 1.8 %copy-start.5 = (bf16[48,512]{1,0:T(8,128)(2,1)S(1)}, bf16[48,512]{1,0:T(8,128)(2,1)}, u32[]{:S(2)}) copy-start(bf16[48,512]{1,0:T(8,128)(2,1)} %diffusion.5) | copy-start | bytes 147460
  13.0 7.6 %collective-permute-start.2 = (bf16[112,512]{1,0:T(8,128)(2,1)S(1)}, bf16[112,512]{1,0:T(8,128)(2,1)S(1)}, u32[]{:S(2)}, u32[]{:S(2)}) collective-permute-start(bf16[112,512]{1,0:T(8,128)(2,1)S(1)} %get-tuple-element.24), channel_id=1, source_target_pairs={{0,1},{1,2},{2,3},{3,0},{4,5},{5,6},{6,7},{7,4},{8,9},{9,10},{10,1... | collective-permute-start | bytes 344072 | tf_op jit(solution)/shard_map/ppermute | solution.py:252
  14.2 7.1 %collective-permute-start.3 = (bf16[112,512]{1,0:T(8,128)(2,1)S(1)}, bf16[112,512]{1,0:T(8,128)(2,1)S(1)}, u32[]{:S(2)}, u32[]{:S(2)}) collective-permute-start(bf16[112,512]{1,0:T(8,128)(2,1)S(1)} %get-tuple-element.25), channel_id=1, source_target_pairs={{0,3},{1,0},{2,1},{3,2},{4,7},{5,4},{6,5},{7,6},{8,11},{9,8},{10,9... | collective-permute-start | bytes 344072 | tf_op jit(solution)/shard_map/ppermute | solution.py:253
  39.6 11.8 %collective-permute-start.4 = (bf16[176,512]{1,0:T(8,128)(2,1)S(1)}, bf16[176,512]{1,0:T(8,128)(2,1)S(1)}, u32[]{:S(2)}, u32[]{:S(2)}) collective-permute-start(bf16[176,512]{1,0:T(8,128)(2,1)S(1)} %get-tuple-element.33), channel_id=1, source_target_pairs={{0,4},{4,8},{8,12},{12,16},{16,20},{20,24},{24,28},{28,0},{1,5},{5... | collective-permute-start | bytes 540680 | tf_op jit(solution)/shard_map/ppermute | solution.py:278

commit v4 on v3

--- a/solution.py
+++ b/solution.py
@@ -147,47 +147,86 @@
     rho_low[...] = low_part[lay.centred(wide, 0)]
 
 
-def coarse_and_third(lay, place, rho, rho_low, a_near, weights, high_m, low_m, coarse, psi, passed, b_own, error_kept):
+def coarse_and_third(lay, place, rho, rho_low, a_near, weights, high_m, low_m, coarse, change, passed, b_own):
     keep, steps, own = lay.keep, lay.steps, lay.own
+    rows = own + 2 * keep
+    count = change.shape[0]
     at = place[0]
     narrow = weights[:, lay.centred(lay.wide, keep)]
-    first = jnp.where(at >= 2, rho[0].astype(F32), 0.0)
+    near = lay.centred(keep, steps)
+    shared = count > 1
 
     def turn(source, carried):
         return product(carried.astype(BF16), coarse[...]) + rho[source].astype(F32)
 
-    current = lax.fori_loop(1, at - 1, turn, first)
-    error_kept[...] = current
+    if shared:
+        odd = at % 2 == 1
+        error = rho[0].astype(F32)
+        errors = []
+        for item in range(count):
+            following = turn(2 * item + 1, error)
+            errors.append(jnp.where(odd, following, error))
+            if item < count - 1:
+                error = turn(2 * item + 2, following)
+    else:
+        first = jnp.where(at >= 2, rho[0].astype(F32), 0.0)
+        errors = [lax.fori_loop(1, at - 1, turn, first)]
+    kept = jnp.concatenate([error.astype(BF16) for error in errors], axis=0)
+    current = jnp.concatenate(errors, axis=0)
     for _ in range(steps):
-        current = product3(stencil(current, narrow), high_m[...], low_m[...])
-    near = lay.centred(keep, steps)
+        moved = [stencil(current[i * rows : (i + 1) * rows], narrow) for i in range(count)]
+        current = product3(jnp.concatenate(moved, axis=0), high_m[...], low_m[...])
+    coarse_part = product(kept, coarse[...])
+    mine = jnp.zeros((own + 2 * steps, current.shape[1]), F32)
+    inner = lay.centred(keep, lay.fine)
+    for i in range(count):
+        swept = current[i * rows : (i + 1) * rows]
+        here = (at - 2) // 2 == i if shared else True
+        mine = mine + jnp.where(jnp.logical_and(here, at >= 2), swept[near], 0.0)
+        change[i] = swept[inner] - coarse_part[i * rows : (i + 1) * rows][inner]
     before = rho[jnp.maximum(at - 1, 0)].astype(F32)[near]
-    b = a_near[...] + jnp.where(at == 0, 0.0, before) + current[near]
+    b = a_near[...] + jnp.where(at == 0, 0.0, before) + mine
     b_own[...] = b[lay.centred(steps, 0)]
     rows = own + 2 * steps
     passed[:rows], passed[rows : 2 * rows] = split(b)
     passed[2 * rows :] = rho_low[...]
-    current = current - product(error_kept[...].astype(BF16), coarse[...])
+
+
+def fourth_sweep(lay, change, weights, high_m, psi):
+    steps = lay.steps
+    count, rows, _ = change.shape
+    narrow = weights[:, lay.centred(lay.wide, lay.fine)]
+    current = jnp.concatenate([change[i] for i in range(count)], axis=0)
     for _ in range(steps):
-        current = product(stencil(current, narrow).astype(BF16), high_m[...])
-    psi[...] = current[near].astype(BF16)
-
-
-def last_sweep(lay, place, psi, passed, b_own, low, high, forcing, weights, start, high_m, low_m, coarse, out):
+        moved = [stencil(current[i * rows : (i + 1) * rows], narrow).astype(BF16) for i in range(count)]
+        current = product(jnp.concatenate(moved, axis=0), high_m[...])
+    for i in range(count):
+        psi[i] = current[i * rows : (i + 1) * rows][lay.centred(lay.fine, steps)].astype(BF16)
+
+
+def last_sweep(lay, place, psi, psi_other, passed, b_own, low, high, forcing, weights, start, high_m, low_m, coarse, out):
     steps, own = lay.steps, lay.own
     at = place[0]
     rows = own + 2 * steps
     narrow = weights[:, lay.centred(lay.wide, steps)]
-
-    def turn(source, carried):
-        return product(carried.astype(BF16), coarse[...]) + psi[source].astype(F32)
+    shared = psi_other is not None
+
+    def source(block):
+        if not shared:
+            return psi[block].astype(F32)
+        item = block // 2 - 1
+        return jnp.where((block - at) % 2 == 0, psi[item].astype(F32), psi_other[item].astype(F32))
+
+    def turn(block, carried):
+        return product(carried.astype(BF16), coarse[...]) + source(block)
 
     error = lax.fori_loop(2, at - 1, turn, jnp.zeros((rows, start.shape[1]), F32))
     b_before = passed[:rows].astype(F32) + passed[rows : 2 * rows].astype(F32)
     initial = start_from_first(lay, low, start[...], high)
     current = jnp.where(at == 0, initial, b_before + error)
     mid = lay.centred(steps, 0)
-    last = product(error[mid].astype(BF16), coarse[...]) + psi[jnp.maximum(at - 1, 0)].astype(F32)[mid]
+    last = product(error[mid].astype(BF16), coarse[...])
+    last = last + jnp.where(at >= 3, source(jnp.maximum(at - 1, 2))[mid], 0.0)
     last = last + passed[2 * rows :].astype(F32)
     out[steps - 1] = b_own[...] + jnp.where(at == 0, 0.0, last)
     for step in range(steps - 1):
@@ -196,18 +235,22 @@
         out[step] = current[mid]
 
 
+def last_sweep_gathered(lay, place, psi, *rest):
+    last_sweep(lay, place, psi, None, *rest)
+
+
 def in_vmem(value):
     return pltpu.with_memory_space_constraint(value, pltpu.VMEM)
 
 
-def call(kernel, lay, outs, *operands, scratch=()):
+def call(kernel, lay, outs, *operands, cost=None):
     spaces = [pltpu.SMEM if o.dtype == jnp.int32 else pltpu.VMEM for o in operands]
     return pl.pallas_call(
         kernel if lay is None else functools.partial(kernel, lay),
         out_shape=outs,
         in_specs=[pl.BlockSpec(memory_space=space) for space in spaces],
         out_specs=jax.tree.map(lambda _: pl.BlockSpec(memory_space=pltpu.VMEM), outs),
-        scratch_shapes=scratch,
+        cost_estimate=cost,
         compiler_params=pltpu.CompilerParams(vmem_limit_bytes=LIMIT),
         name=kernel.__name__,
     )(*operands)
@@ -264,24 +307,41 @@
     )
     weights = in_vmem(weights)
     rho_all = lax.all_gather(rho, "tm", axis=0)
-    psi, passed, b_own = call(
+    shared = blocks % 2 == 0 and 4 <= blocks <= 8
+    count = (blocks - 2) // 2 if shared else 1
+    change, passed, b_own = call(
         coarse_and_third,
         lay,
         [
-            kept(near, columns, dtype=BF16),
+            kept(count, own + 2 * lay.fine, columns),
             kept(2 * near + own, columns, dtype=BF16),
             kept(own, columns),
         ],
         place, rho_all, in_vmem(rho_low), in_vmem(a_near), weights, high_m, low_m, coarse,
-        scratch=[pltpu.VMEM((own + 2 * lay.keep, columns), F32)],
     )
     passed = lax.ppermute(passed, "tm", ring(blocks, 1))
-    psi_all = lax.all_gather(psi, "tm", axis=0)
+    psi = call(
+        fourth_sweep,
+        lay,
+        kept(count, near, columns, dtype=BF16),
+        in_vmem(change), weights, high_m,
+        cost=pl.CostEstimate(
+            flops=2 * steps * count * (own + 2 * lay.fine) * columns * columns,
+            bytes_accessed=4 * count * (own + 2 * lay.fine) * columns,
+            transcendentals=0,
+        ),
+    )
+    if shared:
+        psi_other = lax.ppermute(psi, "tm", [(i, i ^ 1) for i in range(blocks)])
+        sources, kernel = (in_vmem(psi), in_vmem(psi_other)), last_sweep
+    else:
+        sources, kernel = (lax.all_gather(psi[0], "tm", axis=0),), last_sweep_gathered
     return call(
-        last_sweep,
+        kernel,
         lay,
         jax.ShapeDtypeStruct((steps, own, columns), F32),
-        place, psi_all, in_vmem(passed), in_vmem(b_own), low, high, forcing, weights, initial_state, high_m, low_m, coarse,
+        place, *sources, in_vmem(passed), in_vmem(b_own), low, high, forcing, weights, initial_state,
+        high_m, low_m, coarse,
     )
 
 

time: 54.8 us -> 53.3 us (0.973)
  blocking collectives: 21.8 us -> 10.4 us
  waiting for transfers between devices: 6.05 us -> 11.7 us
  Pallas kernels: 14.7 us -> 18.8 us
    all_gather x1 -> x0, blocking collectives: 11.4 us -> none  [per_device(): psi_all = lax.all_gather(psi, 'tm', axis=0)]
    ppermute x1, waiting for transfers between devices: 0.01 us -> 5.66 us  [per_device(): passed = lax.ppermute(passed, 'tm', ring(blocks, 1))]
    pallas_call x5 -> x6, Pallas kernels: 13.6 us -> 17.6 us  [call(): pl.pallas_call(kernel if lay is None else functools.partial(kernel, lay),...]
  transfers between devices with their start and end apart: 5 -> 6, of which waited for: 4 -> 5; matrix products, arithmetic and copies ran while one was open for 0% -> 0% of each run, Pallas kernels for 0% -> 0%
where the time goes in v4:
time: 53.3 us; the launch traced here: 53.1 us
  Pallas kernels  18.8 us (35%)
  waiting for transfers between devices  11.7 us (22%)
  blocking collectives  10.4 us (20%)
  starting transfers between devices  9.65 us (18%)
  local copies, waits for them, and re-layouts  2.46 us (5%)
    pallas_call x6, Pallas kernels, call(): pl.pallas_call(kernel if lay is None else functools.partial(kernel, lay),...  17.6 us
    all_gather x1, blocking collectives, per_device(): rho_all = lax.all_gather(rho, 'tm', axis=0)  10.4 us
    ppermute x1, waiting for transfers between devices, per_device(): passed = lax.ppermute(passed, 'tm', ring(blocks, 1))  5.66 us
    ppermute x1, waiting for transfers between devices, per_device(): far_low = in_vmem(lax.ppermute(tail, 'space', ring(slabs, 1)))  3.75 us
    ppermute x1, starting transfers between devices, per_device(): low = in_vmem(lax.ppermute(tail, 'space', ring(slabs, 1)))  3.1 us
    ppermute x1, starting transfers between devices, per_device(): far_high = in_vmem(lax.ppermute(head, 'space', ring(slabs, -1)))  2.7 us
    unnamed x12, local copies, waits for them, and re-layouts  2.46 us
    ppermute x1, starting transfers between devices, per_device(): high = in_vmem(lax.ppermute(head, 'space', ring(slabs, -1)))  2.09 us
  transfers between devices with their start and end apart: 6, of which 5 were waited for; matrix products, arithmetic and copies ran while one was open for 0% of the time, Pallas kernels for 0%

profile of v4, /device:TPU:0, one launch (start us, length us, event | category | flops | bytes accessed | tf_op | source)
XLA Modules:
  0.0 53.1 jit_solution(11513863151995181775)
XLA Ops:
  0.0 1.1 %pack.1 = (bf16[96,512]{1,0:T(8,128)(2,1)S(1)}, bf16[96,512]{1,0:T(8,128)(2,1)S(1)}) custom-call(bf16[48,512]{1,0:T(8,128)(2,1)} %velocity.5, bf16[48,512]{1,0:T(8,128)(2,1)} %diffusion.5, bf16[8,48,512]{2,1,0:T(8,128)(2,1)} %forcing.5, f32[48,512]{1,0:T(8,128)} %start.5), custom_call_target="tpu_custom_call" | custom-call | tf_op jit(solution)/shard_map/pack/pallas_call | solution.py:273
  1.1 3.1 %collective-permute-start = (bf16[96,512]{1,0:T(8,128)(2,1)S(1)}, bf16[96,512]{1,0:T(8,128)(2,1)S(1)}, u32[]{:S(2)}, u32[]{:S(2)}) collective-permute-start(bf16[96,512]{1,0:T(8,128)(2,1)S(1)} %get-tuple-element.20), channel_id=1, source_target_pairs={{0,1},{1,2},{2,3},{3,0},{4,5},{5,6},{6,7},{7,4},{8,9},{9,10},{10,1... | collective-permute-start | bytes 294920 | tf_op jit(solution)/shard_map/ppermute | solution.py:282
  4.2 2.1 %collective-permute-start.1 = (bf16[96,512]{1,0:T(8,128)(2,1)S(1)}, bf16[96,512]{1,0:T(8,128)(2,1)S(1)}, u32[]{:S(2)}, u32[]{:S(2)}) collective-permute-start(bf16[96,512]{1,0:T(8,128)(2,1)S(1)} %get-tuple-element.21), channel_id=1, source_target_pairs={{0,3},{1,0},{2,1},{3,2},{4,7},{5,4},{6,5},{7,6},{8,11},{9,8},{10,9... | collective-permute-start | bytes 294920 | tf_op jit(solution)/shard_map/ppermute | solution.py:283
  6.3 0.0 copy-start.1
  6.3 1.2 %copy-done.1 = f32[512,512]{1,0:T(8,128)S(1)} copy-done((f32[512,512]{1,0:T(8,128)S(1)}, f32[512,512]{1,0:T(8,128)}, u32[]{:S(2)}) %copy-start.1) | copy-done | bytes 1048600
  7.5 0.0 copy-start.2
  7.6 1.2 %copy-done.2 = f32[512,512]{1,0:T(8,128)S(1)} copy-done((f32[512,512]{1,0:T(8,128)S(1)}, f32[512,512]{1,0:T(8,128)}, u32[]{:S(2)}) %copy-start.2) | copy-done | bytes 1048600
  8.8 0.0 copy-start
  8.8 0.0 copy-start.3
  8.8 0.0 copy-start.4
  8.8 0.0 copy-start.5
  8.8 0.2 split_matrices.1
  9.0 0.7 %collective-permute-done.low = bf16[96,512]{1,0:T(8,128)(2,1)S(1)} collective-permute-done((bf16[96,512]{1,0:T(8,128)(2,1)S(1)}, bf16[96,512]{1,0:T(8,128)(2,1)S(1)}, u32[]{:S(2)}, u32[]{:S(2)}) %collective-permute-start) | collective-permute-done | bytes 98336 | tf_op jit(solution)/shard_map/ppermute | solution.py:282
  9.7 0.9 %collective-permute-done.1.high = bf16[96,512]{1,0:T(8,128)(2,1)S(1)} collective-permute-done((bf16[96,512]{1,0:T(8,128)(2,1)S(1)}, bf16[96,512]{1,0:T(8,128)(2,1)S(1)}, u32[]{:S(2)}, u32[]{:S(2)}) %collective-permute-start.1) | collective-permute-done | bytes 98336 | tf_op jit(solution)/shard_map/ppermute | solution.py:283
  10.6 0.0 copy-done
  10.6 0.0 copy-done.3
  10.6 0.0 copy-done.4
  10.6 0.0 copy-done.5
  10.6 2.4 %first_sweep.1 = (f32[48,512]{1,0:T(8,128)S(1)}, bf16[112,512]{1,0:T(8,128)(2,1)S(1)}, bf16[112,512]{1,0:T(8,128)(2,1)S(1)}) custom-call(s32[1]{0:T(128)} %bitcast.place, bf16[96,512]{1,0:T(8,128)(2,1)S(1)} %collective-permute-done.low, bf16[96,512]{1,0:T(8,128)(2,1)S(1)} %collective-permute-done.1.high, bf16[8,48,512]{2,1,0:T(8,128)(2,1)S(1)} %copy-done, ...), custom_call_target="tpu_custom_call" | custom-call | tf_op jit(solution)/shard_map/first_sweep/pallas_call | solution.py:248
  13.0 1.2 %collective-permute-start.2 = (bf16[112,512]{1,0:T(8,128)(2,1)S(1)}, bf16[112,512]{1,0:T(8,128)(2,1)S(1)}, u32[]{:S(2)}, u32[]{:S(2)}) collective-permute-start(bf16[112,512]{1,0:T(8,128)(2,1)S(1)} %get-tuple-element.24), channel_id=1, source_target_pairs={{0,1},{1,2},{2,3},{3,0},{4,5},{5,6},{6,7},{7,4},{8,9},{9,10},{10,1... | collective-permute-start | bytes 344072 | tf_op jit(solution)/shard_map/ppermute | solution.py:295
  14.2 2.7 %collective-permute-start.3 = (bf16[112,512]{1,0:T(8,128)(2,1)S(1)}, bf16[112,512]{1,0:T(8,128)(2,1)S(1)}, u32[]{:S(2)}, u32[]{:S(2)}) collective-permute-start(bf16[112,512]{1,0:T(8,128)(2,1)S(1)} %get-tuple-element.25), channel_id=1, source_target_pairs={{0,3},{1,0},{2,1},{3,2},{4,7},{5,4},{6,5},{7,6},{8,11},{9,8},{10,9... | collective-permute-start | bytes 344072 | tf_op jit(solution)/shard_map/ppermute | solution.py:296
  16.9 3.8 %collective-permute-done.2.low = bf16[112,512]{1,0:T(8,128)(2,1)S(1)} collective-permute-done((bf16[112,512]{1,0:T(8,128)(2,1)S(1)}, bf16[112,512]{1,0:T(8,128)(2,1)S(1)}, u32[]{:S(2)}, u32[]{:S(2)}) %collective-permute-start.2) | collective-permute-done | bytes 114720 | tf_op jit(solution)/shard_map/ppermute | solution.py:295
  20.7 0.7 %collective-permute-done.3.high = bf16[112,512]{1,0:T(8,128)(2,1)S(1)} collective-permute-done((bf16[112,512]{1,0:T(8,128)(2,1)S(1)}, bf16[112,512]{1,0:T(8,128)(2,1)S(1)}, u32[]{:S(2)}, u32[]{:S(2)}) %collective-permute-start.3) | collective-permute-done | bytes 114720 | tf_op jit(solution)/shard_map/ppermute | solution.py:296
  21.4 3.0 %second_sweep.1 = (bf16[96,512]{1,0:T(8,128)(2,1)S(1)}, bf16[48,512]{1,0:T(8,128)(2,1)S(1)}, f32[64,512]{1,0:T(8,128)S(1)}, f32[3,112,512]{2,1,0:T(8,128)S(1)}) custom-call(bf16[112,512]{1,0:T(8,128)(2,1)S(1)} %collective-permute-done.2.low, bf16[112,512]{1,0:T(8,128)(2,1)S(1)} %collective-permute-done.3.high, f32[48,512]{1,0:T(8,128)S(1)} %get-tuple-element.26.a, ...), custom_call_target="tpu_custom_call" | custom-call | tf_op jit(solution)/shard_map/second_sweep/pallas_call | solution.py:248
  24.4 10.4 %all-gather = bf16[768,512]{1,0:T(8,128)(2,1)S(1)} all-gather(bf16[96,512]{1,0:T(8,128)(2,1)S(1)} %get-tuple-element.27), channel_id=2, replica_groups=mesh['tm'=8,'space'=4] {'tm'}, dimensions={0}, use_global_device_ids=true | all-gather | bytes 884736 | tf_op jit(solution)/shard_map/all_gather | solution.py:309
  34.8 6.3 %coarse_and_third.1 = (f32[3,80,512]{2,1,0:T(8,128)S(1)}, bf16[176,512]{1,0:T(8,128)(2,1)S(1)}, f32[48,512]{1,0:T(8,128)S(1)}) custom-call(s32[1]{0:T(128)} %bitcast.place, bf16[8,96,512]{2,1,0:T(8,128)(2,1)S(1)} %bitcast.2, bf16[48,512]{1,0:T(8,128)(2,1)S(1)} %get-tuple-element.28.rho_low, f32[64,512]{1,0:T(8,128)S(1)} %get-tuple-element.29.a_near, ...), custom_call_target="tpu_custom_call" | custom-call | tf_op jit(solution)/shard_map/coarse_and_third/pallas_call | solution.py:248
  41.1 2.6 %fourth_sweep.1.psi = bf16[3,64,512]{2,1,0:T(8,128)(2,1)S(1)} custom-call(f32[3,80,512]{2,1,0:T(8,128)S(1)} %get-tuple-element.32.change, f32[3,112,512]{2,1,0:T(8,128)S(1)} %get-tuple-element.30.weights, bf16[512,512]{1,0:T(8,128)(2,1)S(1)} %get-tuple-element.22.high_m), custom_call_target="tpu_custom_call" | custom-call | flops 1006632960 | bytes 491520 | tf_op jit(solution)/shard_map/fourth_sweep/pallas_call | solution.py:248
  43.7 0.4 collective-permute-start.4
  44.1 0.2 collective-permute-start.5
  44.3 5.7 %collective-permute-done.5.passed = bf16[176,512]{1,0:T(8,128)(2,1)S(1)} collective-permute-done((bf16[176,512]{1,0:T(8,128)(2,1)S(1)}, bf16[176,512]{1,0:T(8,128)(2,1)S(1)}, u32[]{:S(2)}, u32[]{:S(2)}) %collective-permute-start.5) | collective-permute-done | bytes 180256 | tf_op jit(solution)/shard_map/ppermute | solution.py:322
  49.9 0.0 collective-permute-done.4.psi_other
  49.9 3.1 %last_sweep.1 = f32[8,48,512]{2,1,0:T(8,128)} custom-call(s32[1]{0:T(128)} %bitcast.place, bf16[3,64,512]{2,1,0:T(8,128)(2,1)S(1)} %fourth_sweep.1.psi, bf16[3,64,512]{2,1,0:T(8,128)(2,1)S(1)} %collective-permute-done.4.psi_other, bf16[176,512]{1,0:T(8,128)(2,1)S(1)} %collective-permute-done.5.passed, f32[48,512]{1,0:T(8,128)S(1)} %get-tuple-element.34.b_own, ...), custom_call_target="tpu_custom_call" | custom-call | tf_op jit(solution)/shard_map/last_sweep/pallas_call | solution.py:248
Async XLA Ops:
  1.1 8.6 %collective-permute-start = (bf16[96,512]{1,0:T(8,128)(2,1)S(1)}, bf16[96,512]{1,0:T(8,128)(2,1)S(1)}, u32[]{:S(2)}, u32[]{:S(2)}) collective-permute-start(bf16[96,512]{1,0:T(8,128)(2,1)S(1)} %get-tuple-element.20), channel_id=1, source_target_pairs={{0,1},{1,2},{2,3},{3,0},{4,5},{5,6},{6,7},{7,4},{8,9},{9,10},{10,1... | collective-permute-start | bytes 294920 | tf_op jit(solution)/shard_map/ppermute | solution.py:282
  4.2 6.4 %collective-permute-start.1 = (bf16[96,512]{1,0:T(8,128)(2,1)S(1)}, bf16[96,512]{1,0:T(8,128)(2,1)S(1)}, u32[]{:S(2)}, u32[]{:S(2)}) collective-permute-start(bf16[96,512]{1,0:T(8,128)(2,1)S(1)} %get-tuple-element.21), channel_id=1, source_target_pairs={{0,3},{1,0},{2,1},{3,2},{4,7},{5,4},{6,5},{7,6},{8,11},{9,8},{10,9... | collective-permute-start | bytes 294920 | tf_op jit(solution)/shard_map/ppermute | solution.py:283
  6.3 1.2 %copy-start.1 = (f32[512,512]{1,0:T(8,128)S(1)}, f32[512,512]{1,0:T(8,128)}, u32[]{:S(2)}) copy-start(f32[512,512]{1,0:T(8,128)} %implicit.1) | copy-start | bytes 3145732
  7.5 1.2 %copy-start.2 = (f32[512,512]{1,0:T(8,128)S(1)}, f32[512,512]{1,0:T(8,128)}, u32[]{:S(2)}) copy-start(f32[512,512]{1,0:T(8,128)} %coarse_implicit.1) | copy-start | bytes 3145732
  8.8 1.8 %copy-start = (bf16[8,48,512]{2,1,0:T(8,128)(2,1)S(1)}, bf16[8,48,512]{2,1,0:T(8,128)(2,1)}, u32[]{:S(2)}) copy-start(bf16[8,48,512]{2,1,0:T(8,128)(2,1)} %forcing.5) | copy-start | bytes 1179652
  8.8 1.8 %copy-start.3 = (f32[48,512]{1,0:T(8,128)S(1)}, f32[48,512]{1,0:T(8,128)}, u32[]{:S(2)}) copy-start(f32[48,512]{1,0:T(8,128)} %start.5) | copy-start | bytes 294916
  8.8 1.8 %copy-start.4 = (bf16[48,512]{1,0:T(8,128)(2,1)S(1)}, bf16[48,512]{1,0:T(8,128)(2,1)}, u32[]{:S(2)}) copy-start(bf16[48,512]{1,0:T(8,128)(2,1)} %velocity.5) | copy-start | bytes 147460
  8.8 1.8 %copy-start.5 = (bf16[48,512]{1,0:T(8,128)(2,1)S(1)}, bf16[48,512]{1,0:T(8,128)(2,1)}, u32[]{:S(2)}) copy-start(bf16[48,512]{1,0:T(8,128)(2,1)} %diffusion.5) | copy-start | bytes 147460
  13.0 7.6 %collective-permute-start.2 = (bf16[112,512]{1,0:T(8,128)(2,1)S(1)}, bf16[112,512]{1,0:T(8,128)(2,1)S(1)}, u32[]{:S(2)}, u32[]{:S(2)}) collective-permute-start(bf16[112,512]{1,0:T(8,128)(2,1)S(1)} %get-tuple-element.24), channel_id=1, source_target_pairs={{0,1},{1,2},{2,3},{3,0},{4,5},{5,6},{6,7},{7,4},{8,9},{9,10},{10,1... | collective-permute-start | bytes 344072 | tf_op jit(solution)/shard_map/ppermute | solution.py:295
  14.2 7.1 %collective-permute-start.3 = (bf16[112,512]{1,0:T(8,128)(2,1)S(1)}, bf16[112,512]{1,0:T(8,128)(2,1)S(1)}, u32[]{:S(2)}, u32[]{:S(2)}) collective-permute-start(bf16[112,512]{1,0:T(8,128)(2,1)S(1)} %get-tuple-element.25), channel_id=1, source_target_pairs={{0,3},{1,0},{2,1},{3,2},{4,7},{5,4},{6,5},{7,6},{8,11},{9,8},{10,9... | collective-permute-start | bytes 344072 | tf_op jit(solution)/shard_map/ppermute | solution.py:296
  43.7 6.2 %collective-permute-start.4 = (bf16[3,64,512]{2,1,0:T(8,128)(2,1)S(1)}, bf16[3,64,512]{2,1,0:T(8,128)(2,1)S(1)}, u32[]{:S(2)}, u32[]{:S(2)}) collective-permute-start(bf16[3,64,512]{2,1,0:T(8,128)(2,1)S(1)} %fourth_sweep.1.psi), channel_id=1, source_target_pairs={{0,4},{4,0},{8,12},{12,8},{16,20},{20,16},{24,28},{28,24},{1,5},{5... | collective-permute-start | bytes 589832 | tf_op jit(solution)/shard_map/ppermute | solution.py:335
  44.1 5.8 %collective-permute-start.5 = (bf16[176,512]{1,0:T(8,128)(2,1)S(1)}, bf16[176,512]{1,0:T(8,128)(2,1)S(1)}, u32[]{:S(2)}, u32[]{:S(2)}) collective-permute-start(bf16[176,512]{1,0:T(8,128)(2,1)S(1)} %get-tuple-element.33), channel_id=1, source_target_pairs={{0,4},{4,8},{8,12},{12,16},{16,20},{20,24},{24,28},{28,0},{1,5},{5... | collective-permute-start | bytes 540680 | tf_op jit(solution)/shard_map/ppermute | solution.py:322

commit v5 on v4

--- a/solution.py
+++ b/solution.py
@@ -6,6 +6,7 @@
 from jax.experimental import pallas as pl
 from jax.experimental.pallas import tpu as pltpu
 from jax.sharding import PartitionSpec as P
+
 
 F32 = jnp.float32
 BF16 = jnp.bfloat16
@@ -78,9 +79,15 @@
         out[lay.start_low : lay.first_rows] = low
 
 
-def split_matrices(implicit, coarse_implicit, high_m, low_m, coarse):
-    high_m[...], low_m[...] = split(implicit[...])
-    coarse[...] = coarse_implicit[...].astype(BF16)
+def split_matrices(implicit, coarse_implicit, high_m, low_m, coarse, fine_kept, coarse_kept, semaphores):
+    fine_copy = pltpu.make_async_copy(implicit, fine_kept, semaphores.at[0])
+    coarse_copy = pltpu.make_async_copy(coarse_implicit, coarse_kept, semaphores.at[1])
+    fine_copy.start()
+    coarse_copy.start()
+    fine_copy.wait()
+    high_m[...], low_m[...] = split(fine_kept[...])
+    coarse_copy.wait()
+    coarse[...] = coarse_kept[...].astype(BF16)
 
 
 def joined(low, own, high):
@@ -243,17 +250,26 @@
     return pltpu.with_memory_space_constraint(value, pltpu.VMEM)
 
 
-def call(kernel, lay, outs, *operands, cost=None):
+def call(kernel, lay, outs, *operands):
     spaces = [pltpu.SMEM if o.dtype == jnp.int32 else pltpu.VMEM for o in operands]
     return pl.pallas_call(
         kernel if lay is None else functools.partial(kernel, lay),
         out_shape=outs,
         in_specs=[pl.BlockSpec(memory_space=space) for space in spaces],
         out_specs=jax.tree.map(lambda _: pl.BlockSpec(memory_space=pltpu.VMEM), outs),
-        cost_estimate=cost,
         compiler_params=pltpu.CompilerParams(vmem_limit_bytes=LIMIT),
-        name=kernel.__name__,
     )(*operands)
+
+
+def call_from_hbm(kernel, outs, scratch, *operands):
+    return pl.pallas_call(
+        kernel,
+        out_shape=outs,
+        in_specs=[pl.BlockSpec(memory_space=pltpu.HBM)] * len(operands),
+        out_specs=[pl.BlockSpec(memory_space=pltpu.VMEM)] * len(outs),
+        scratch_shapes=scratch,
+        compiler_params=pltpu.CompilerParams(vmem_limit_bytes=LIMIT),
+    )(*(pltpu.with_memory_space_constraint(value, pltpu.HBM) for value in operands))
 
 
 def per_device(initial_state, velocity, diffusion, forcing, implicit, coarse_implicit):
@@ -269,20 +285,19 @@
         return pltpu.VMEM(shape, dtype)
 
     first_pack = kept(lay.first_rows, columns, dtype=BF16)
-    hbm = pl.BlockSpec(memory_space=pltpu.HBM)
-    head, tail = pl.pallas_call(
+    head, tail = call_from_hbm(
         functools.partial(pack, lay),
-        out_shape=[first_pack] * 2,
-        in_specs=[hbm] * 4,
-        out_specs=[pl.BlockSpec(memory_space=pltpu.VMEM)] * 2,
-        scratch_shapes=[pltpu.VMEM((own, columns), F32), pltpu.SemaphoreType.DMA((1 + 2 * (steps + 2),))],
-        compiler_params=pltpu.CompilerParams(vmem_limit_bytes=LIMIT),
-        name="pack",
-    )(*(pltpu.with_memory_space_constraint(x, pltpu.HBM) for x in (velocity, diffusion, forcing, initial_state)))
+        [first_pack] * 2,
+        [pltpu.VMEM((own, columns), F32), pltpu.SemaphoreType.DMA((1 + 2 * (steps + 2),))],
+        velocity, diffusion, forcing, initial_state,
+    )
     low = in_vmem(lax.ppermute(tail, "space", ring(slabs, 1)))
     high = in_vmem(lax.ppermute(head, "space", ring(slabs, -1)))
-    high_m, low_m, coarse = call(
-        split_matrices, None, [kept(*implicit.shape, dtype=BF16)] * 3, implicit, coarse_implicit
+    high_m, low_m, coarse = call_from_hbm(
+        split_matrices,
+        [kept(*implicit.shape, dtype=BF16)] * 3,
+        [pltpu.VMEM(implicit.shape, F32), pltpu.VMEM(implicit.shape, F32), pltpu.SemaphoreType.DMA((2,))],
+        implicit, coarse_implicit,
     )
     high_m, low_m, coarse = in_vmem(high_m), in_vmem(low_m), in_vmem(coarse)
     second_pack = kept(lay.second_rows, columns, dtype=BF16)
@@ -320,17 +335,7 @@
         place, rho_all, in_vmem(rho_low), in_vmem(a_near), weights, high_m, low_m, coarse,
     )
     passed = lax.ppermute(passed, "tm", ring(blocks, 1))
-    psi = call(
-        fourth_sweep,
-        lay,
-        kept(count, near, columns, dtype=BF16),
-        in_vmem(change), weights, high_m,
-        cost=pl.CostEstimate(
-            flops=2 * steps * count * (own + 2 * lay.fine) * columns * columns,
-            bytes_accessed=4 * count * (own + 2 * lay.fine) * columns,
-            transcendentals=0,
-        ),
-    )
+    psi = call(fourth_sweep, lay, kept(count, near, columns, dtype=BF16), in_vmem(change), weights, high_m)
     if shared:
         psi_other = lax.ppermute(psi, "tm", [(i, i ^ 1) for i in range(blocks)])
         sources, kernel = (in_vmem(psi), in_vmem(psi_other)), last_sweep

time: 53.3 us -> 53.3 us (level)
  local copies, waits for them, and re-layouts: 2.46 us -> 0.01 us
  Pallas kernels: 18.8 us -> 20.2 us
  waiting for transfers between devices: 11.7 us -> 12.7 us
    unnamed x12 -> x8, local copies, waits for them, and re-layouts: 2.46 us -> 0.01 us
    pallas_call x1 -> x2, Pallas kernels: 1.12 us -> 2.78 us  [call_from_hbm(): pl.pallas_call(kernel, out_shape=outs, in_specs=[pl.BlockSpec(memory_spac...]
    ppermute x1, waiting for transfers between devices: 0.71 us -> 1.68 us  [per_device(): low = in_vmem(lax.ppermute(tail, 'space', ring(slabs, 1)))]
    pallas_call x6 -> x5, Pallas kernels: 17.6 us -> 17.5 us  [call(): pl.pallas_call(kernel if lay is None else functools.partial(kernel, lay),...]
  transfers between devices with their start and end apart: 6 -> 6, of which waited for: 5 -> 5; matrix products, arithmetic and copies ran while one was open for 0% -> 0% of each run, Pallas kernels for 0% -> 3%
where the time goes in v5:
time: 53.3 us; the launch traced here: 53.1 us
  Pallas kernels  20.2 us (38%)
  waiting for transfers between devices  12.7 us (24%)
  blocking collectives  10.4 us (20%)
  starting transfers between devices  9.65 us (18%)
    pallas_call x5, Pallas kernels, call(): pl.pallas_call(kernel if lay is None else functools.partial(kernel, lay),...  17.5 us
    all_gather x1, blocking collectives, per_device(): rho_all = lax.all_gather(rho, 'tm', axis=0)  10.4 us
    ppermute x1, waiting for transfers between devices, per_device(): passed = lax.ppermute(passed, 'tm', ring(blocks, 1))  5.66 us
    ppermute x1, waiting for transfers between devices, per_device(): far_low = in_vmem(lax.ppermute(tail, 'space', ring(slabs, 1)))  3.75 us
    ppermute x1, starting transfers between devices, per_device(): low = in_vmem(lax.ppermute(tail, 'space', ring(slabs, 1)))  3.1 us
    pallas_call x2, Pallas kernels, call_from_hbm(): pl.pallas_call(kernel, out_shape=outs, in_specs=[pl.BlockSpec(memory_spac...  2.78 us
    ppermute x1, starting transfers between devices, per_device(): far_high = in_vmem(lax.ppermute(head, 'space', ring(slabs, -1)))  2.68 us
    ppermute x1, starting transfers between devices, per_device(): high = in_vmem(lax.ppermute(head, 'space', ring(slabs, -1)))  2.09 us
  transfers between devices with their start and end apart: 6, of which 5 were waited for; matrix products, arithmetic and copies ran while one was open for 0% of the time, Pallas kernels for 3%

profile of v5, /device:TPU:0, one launch (start us, length us, event | category | flops | bytes accessed | tf_op | source)
XLA Modules:
  0.0 53.1 jit_solution(14497525753290219501)
XLA Ops:
  0.0 1.1 %shard_map.64 = (bf16[96,512]{1,0:T(8,128)(2,1)S(1)}, bf16[96,512]{1,0:T(8,128)(2,1)S(1)}) custom-call(bf16[48,512]{1,0:T(8,128)(2,1)} %velocity.5, bf16[48,512]{1,0:T(8,128)(2,1)} %diffusion.5, bf16[8,48,512]{2,1,0:T(8,128)(2,1)} %forcing.5, f32[48,512]{1,0:T(8,128)} %start.5), custom_call_target="tpu_custom_call" | custom-call | tf_op jit(solution)/shard_map/pallas_call | solution.py:265
  1.1 3.1 %collective-permute-start = (bf16[96,512]{1,0:T(8,128)(2,1)S(1)}, bf16[96,512]{1,0:T(8,128)(2,1)S(1)}, u32[]{:S(2)}, u32[]{:S(2)}) collective-permute-start(bf16[96,512]{1,0:T(8,128)(2,1)S(1)} %get-tuple-element.20), channel_id=1, source_target_pairs={{0,1},{1,2},{2,3},{3,0},{4,5},{5,6},{6,7},{7,4},{8,9},{9,10},{10,1... | collective-permute-start | bytes 294920 | tf_op jit(solution)/shard_map/ppermute | solution.py:294
  4.2 2.1 %collective-permute-start.1 = (bf16[96,512]{1,0:T(8,128)(2,1)S(1)}, bf16[96,512]{1,0:T(8,128)(2,1)S(1)}, u32[]{:S(2)}, u32[]{:S(2)}) collective-permute-start(bf16[96,512]{1,0:T(8,128)(2,1)S(1)} %get-tuple-element.21), channel_id=1, source_target_pairs={{0,3},{1,0},{2,1},{3,2},{4,7},{5,4},{6,5},{7,6},{8,11},{9,8},{10,9... | collective-permute-start | bytes 294920 | tf_op jit(solution)/shard_map/ppermute | solution.py:295
  6.3 0.0 copy-start
  6.3 0.0 copy-start.1
  6.3 0.0 copy-start.2
  6.3 0.0 copy-start.3
  6.3 1.7 %shard_map.65 = (bf16[512,512]{1,0:T(8,128)(2,1)S(1)}, bf16[512,512]{1,0:T(8,128)(2,1)S(1)}, bf16[512,512]{1,0:T(8,128)(2,1)S(1)}) custom-call(f32[512,512]{1,0:T(8,128)} %implicit.1, f32[512,512]{1,0:T(8,128)} %coarse_implicit.1), custom_call_target="tpu_custom_call" | custom-call | tf_op jit(solution)/shard_map/pallas_call | solution.py:265
  8.0 1.7 %collective-permute-done.low = bf16[96,512]{1,0:T(8,128)(2,1)S(1)} collective-permute-done((bf16[96,512]{1,0:T(8,128)(2,1)S(1)}, bf16[96,512]{1,0:T(8,128)(2,1)S(1)}, u32[]{:S(2)}, u32[]{:S(2)}) %collective-permute-start) | collective-permute-done | bytes 98336 | tf_op jit(solution)/shard_map/ppermute | solution.py:294
  9.7 0.9 %collective-permute-done.1.high = bf16[96,512]{1,0:T(8,128)(2,1)S(1)} collective-permute-done((bf16[96,512]{1,0:T(8,128)(2,1)S(1)}, bf16[96,512]{1,0:T(8,128)(2,1)S(1)}, u32[]{:S(2)}, u32[]{:S(2)}) %collective-permute-start.1) | collective-permute-done | bytes 98336 | tf_op jit(solution)/shard_map/ppermute | solution.py:295
  10.6 0.0 copy-done
  10.6 0.0 copy-done.1
  10.6 0.0 copy-done.2
  10.6 0.0 copy-done.3
  10.6 2.4 %shard_map.66 = (f32[48,512]{1,0:T(8,128)S(1)}, bf16[112,512]{1,0:T(8,128)(2,1)S(1)}, bf16[112,512]{1,0:T(8,128)(2,1)S(1)}) custom-call(s32[1]{0:T(128)} %bitcast.place, bf16[96,512]{1,0:T(8,128)(2,1)S(1)} %collective-permute-done.low, bf16[96,512]{1,0:T(8,128)(2,1)S(1)} %collective-permute-done.1.high, bf16[8,48,512]{2,1,0:T(8,128)(2,1)S(1)} %copy-done, ...), custom_call_target="tpu_custom_call" | custom-call | tf_op jit(solution)/shard_map/pallas_call | solution.py:255
  13.0 1.2 %collective-permute-start.2 = (bf16[112,512]{1,0:T(8,128)(2,1)S(1)}, bf16[112,512]{1,0:T(8,128)(2,1)S(1)}, u32[]{:S(2)}, u32[]{:S(2)}) collective-permute-start(bf16[112,512]{1,0:T(8,128)(2,1)S(1)} %get-tuple-element.24), channel_id=1, source_target_pairs={{0,1},{1,2},{2,3},{3,0},{4,5},{5,6},{6,7},{7,4},{8,9},{9,10},{10,1... | collective-permute-start | bytes 344072 | tf_op jit(solution)/shard_map/ppermute | solution.py:310
  14.2 2.7 %collective-permute-start.3 = (bf16[112,512]{1,0:T(8,128)(2,1)S(1)}, bf16[112,512]{1,0:T(8,128)(2,1)S(1)}, u32[]{:S(2)}, u32[]{:S(2)}) collective-permute-start(bf16[112,512]{1,0:T(8,128)(2,1)S(1)} %get-tuple-element.25), channel_id=1, source_target_pairs={{0,3},{1,0},{2,1},{3,2},{4,7},{5,4},{6,5},{7,6},{8,11},{9,8},{10,9... | collective-permute-start | bytes 344072 | tf_op jit(solution)/shard_map/ppermute | solution.py:311
  16.9 3.8 %collective-permute-done.2.low = bf16[112,512]{1,0:T(8,128)(2,1)S(1)} collective-permute-done((bf16[112,512]{1,0:T(8,128)(2,1)S(1)}, bf16[112,512]{1,0:T(8,128)(2,1)S(1)}, u32[]{:S(2)}, u32[]{:S(2)}) %collective-permute-start.2) | collective-permute-done | bytes 114720 | tf_op jit(solution)/shard_map/ppermute | solution.py:310
  20.7 0.7 %collective-permute-done.3.high = bf16[112,512]{1,0:T(8,128)(2,1)S(1)} collective-permute-done((bf16[112,512]{1,0:T(8,128)(2,1)S(1)}, bf16[112,512]{1,0:T(8,128)(2,1)S(1)}, u32[]{:S(2)}, u32[]{:S(2)}) %collective-permute-start.3) | collective-permute-done | bytes 114720 | tf_op jit(solution)/shard_map/ppermute | solution.py:311
  21.4 3.0 %shard_map.67 = (bf16[96,512]{1,0:T(8,128)(2,1)S(1)}, bf16[48,512]{1,0:T(8,128)(2,1)S(1)}, f32[64,512]{1,0:T(8,128)S(1)}, f32[3,112,512]{2,1,0:T(8,128)S(1)}) custom-call(bf16[112,512]{1,0:T(8,128)(2,1)S(1)} %collective-permute-done.2.low, bf16[112,512]{1,0:T(8,128)(2,1)S(1)} %collective-permute-done.3.high, f32[48,512]{1,0:T(8,128)S(1)} %get-tuple-element.26.a, ...), custom_call_target="tpu_custom_call" | custom-call | tf_op jit(solution)/shard_map/pallas_call | solution.py:255
  24.4 10.4 %all-gather = bf16[768,512]{1,0:T(8,128)(2,1)S(1)} all-gather(bf16[96,512]{1,0:T(8,128)(2,1)S(1)} %get-tuple-element.27), channel_id=2, replica_groups=mesh['tm'=8,'space'=4] {'tm'}, dimensions={0}, use_global_device_ids=true | all-gather | bytes 884736 | tf_op jit(solution)/shard_map/all_gather | solution.py:324
  34.8 6.3 %shard_map.68 = (f32[3,80,512]{2,1,0:T(8,128)S(1)}, bf16[176,512]{1,0:T(8,128)(2,1)S(1)}, f32[48,512]{1,0:T(8,128)S(1)}) custom-call(s32[1]{0:T(128)} %bitcast.place, bf16[8,96,512]{2,1,0:T(8,128)(2,1)S(1)} %bitcast.2, bf16[48,512]{1,0:T(8,128)(2,1)S(1)} %get-tuple-element.28.rho_low, f32[64,512]{1,0:T(8,128)S(1)} %get-tuple-element.29.a_near, ...), custom_call_target="tpu_custom_call" | custom-call | tf_op jit(solution)/shard_map/pallas_call | solution.py:255
  41.1 2.6 %shard_map.69.psi = bf16[3,64,512]{2,1,0:T(8,128)(2,1)S(1)} custom-call(f32[3,80,512]{2,1,0:T(8,128)S(1)} %get-tuple-element.32.change, f32[3,112,512]{2,1,0:T(8,128)S(1)} %get-tuple-element.30.weights, bf16[512,512]{1,0:T(8,128)(2,1)S(1)} %get-tuple-element.22.high_m), custom_call_target="tpu_custom_call" | custom-call | tf_op jit(solution)/shard_map/pallas_call | solution.py:255
  43.7 0.4 collective-permute-start.4
  44.1 0.2 collective-permute-start.5
  44.3 5.7 %collective-permute-done.5.passed = bf16[176,512]{1,0:T(8,128)(2,1)S(1)} collective-permute-done((bf16[176,512]{1,0:T(8,128)(2,1)S(1)}, bf16[176,512]{1,0:T(8,128)(2,1)S(1)}, u32[]{:S(2)}, u32[]{:S(2)}) %collective-permute-start.5) | collective-permute-done | bytes 180256 | tf_op jit(solution)/shard_map/ppermute | solution.py:337
  50.0 0.0 collective-permute-done.4.psi_other
  50.0 3.1 %shard_map.70 = f32[8,48,512]{2,1,0:T(8,128)} custom-call(s32[1]{0:T(128)} %bitcast.place, bf16[3,64,512]{2,1,0:T(8,128)(2,1)S(1)} %shard_map.69.psi, bf16[3,64,512]{2,1,0:T(8,128)(2,1)S(1)} %collective-permute-done.4.psi_other, bf16[176,512]{1,0:T(8,128)(2,1)S(1)} %collective-permute-done.5.passed, f32[48,512]{1,0:T(8,128)S(1)} %get-tuple-element.34.b_own, ...), custom_call_target="tpu_custom_call" | custom-call | tf_op jit(solution)/shard_map/pallas_call | solution.py:255
Async XLA Ops:
  1.1 8.6 %collective-permute-start = (bf16[96,512]{1,0:T(8,128)(2,1)S(1)}, bf16[96,512]{1,0:T(8,128)(2,1)S(1)}, u32[]{:S(2)}, u32[]{:S(2)}) collective-permute-start(bf16[96,512]{1,0:T(8,128)(2,1)S(1)} %get-tuple-element.20), channel_id=1, source_target_pairs={{0,1},{1,2},{2,3},{3,0},{4,5},{5,6},{6,7},{7,4},{8,9},{9,10},{10,1... | collective-permute-start | bytes 294920 | tf_op jit(solution)/shard_map/ppermute | solution.py:294
  4.2 6.4 %collective-permute-start.1 = (bf16[96,512]{1,0:T(8,128)(2,1)S(1)}, bf16[96,512]{1,0:T(8,128)(2,1)S(1)}, u32[]{:S(2)}, u32[]{:S(2)}) collective-permute-start(bf16[96,512]{1,0:T(8,128)(2,1)S(1)} %get-tuple-element.21), channel_id=1, source_target_pairs={{0,3},{1,0},{2,1},{3,2},{4,7},{5,4},{6,5},{7,6},{8,11},{9,8},{10,9... | collective-permute-start | bytes 294920 | tf_op jit(solution)/shard_map/ppermute | solution.py:295
  6.3 4.3 %copy-start = (bf16[8,48,512]{2,1,0:T(8,128)(2,1)S(1)}, bf16[8,48,512]{2,1,0:T(8,128)(2,1)}, u32[]{:S(2)}) copy-start(bf16[8,48,512]{2,1,0:T(8,128)(2,1)} %forcing.5) | copy-start | bytes 1179652
  6.3 4.3 %copy-start.1 = (f32[48,512]{1,0:T(8,128)S(1)}, f32[48,512]{1,0:T(8,128)}, u32[]{:S(2)}) copy-start(f32[48,512]{1,0:T(8,128)} %start.5) | copy-start | bytes 294916
  6.3 4.3 %copy-start.2 = (bf16[48,512]{1,0:T(8,128)(2,1)S(1)}, bf16[48,512]{1,0:T(8,128)(2,1)}, u32[]{:S(2)}) copy-start(bf16[48,512]{1,0:T(8,128)(2,1)} %velocity.5) | copy-start | bytes 147460
  6.3 4.3 %copy-start.3 = (bf16[48,512]{1,0:T(8,128)(2,1)S(1)}, bf16[48,512]{1,0:T(8,128)(2,1)}, u32[]{:S(2)}) copy-start(bf16[48,512]{1,0:T(8,128)(2,1)} %diffusion.5) | copy-start | bytes 147460
  13.0 7.6 %collective-permute-start.2 = (bf16[112,512]{1,0:T(8,128)(2,1)S(1)}, bf16[112,512]{1,0:T(8,128)(2,1)S(1)}, u32[]{:S(2)}, u32[]{:S(2)}) collective-permute-start(bf16[112,512]{1,0:T(8,128)(2,1)S(1)} %get-tuple-element.24), channel_id=1, source_target_pairs={{0,1},{1,2},{2,3},{3,0},{4,5},{5,6},{6,7},{7,4},{8,9},{9,10},{10,1... | collective-permute-start | bytes 344072 | tf_op jit(solution)/shard_map/ppermute | solution.py:310
  14.2 7.1 %collective-permute-start.3 = (bf16[112,512]{1,0:T(8,128)(2,1)S(1)}, bf16[112,512]{1,0:T(8,128)(2,1)S(1)}, u32[]{:S(2)}, u32[]{:S(2)}) collective-permute-start(bf16[112,512]{1,0:T(8,128)(2,1)S(1)} %get-tuple-element.25), channel_id=1, source_target_pairs={{0,3},{1,0},{2,1},{3,2},{4,7},{5,4},{6,5},{7,6},{8,11},{9,8},{10,9... | collective-permute-start | bytes 344072 | tf_op jit(solution)/shard_map/ppermute | solution.py:311
  43.7 6.2 %collective-permute-start.4 = (bf16[3,64,512]{2,1,0:T(8,128)(2,1)S(1)}, bf16[3,64,512]{2,1,0:T(8,128)(2,1)S(1)}, u32[]{:S(2)}, u32[]{:S(2)}) collective-permute-start(bf16[3,64,512]{2,1,0:T(8,128)(2,1)S(1)} %shard_map.69.psi), channel_id=1, source_target_pairs={{0,4},{4,0},{8,12},{12,8},{16,20},{20,16},{24,28},{28,24},{1,5},{5... | collective-permute-start | bytes 589832 | tf_op jit(solution)/shard_map/ppermute | solution.py:340
  44.1 5.8 %collective-permute-start.5 = (bf16[176,512]{1,0:T(8,128)(2,1)S(1)}, bf16[176,512]{1,0:T(8,128)(2,1)S(1)}, u32[]{:S(2)}, u32[]{:S(2)}) collective-permute-start(bf16[176,512]{1,0:T(8,128)(2,1)S(1)} %get-tuple-element.33), channel_id=1, source_target_pairs={{0,4},{4,8},{8,12},{12,16},{16,20},{20,24},{24,28},{28,0},{1,5},{5... | collective-permute-start | bytes 540680 | tf_op jit(solution)/shard_map/ppermute | solution.py:337

commit v6 on v5

--- a/solution.py
+++ b/solution.py
@@ -38,45 +38,63 @@
     return centre * value + east * jnp.roll(value, -1, 0) + west * jnp.roll(value, 1, 0)
 
 
+def turned(value, shift):
+    return value if shift % value.shape[0] == 0 else jnp.roll(value, shift, 0)
+
+
 class Layout:
     def __init__(self, steps, own):
         self.steps = steps
         self.own = own
+        self.fine = 2 * steps
+        self.keep = 3 * steps
         self.wide = 4 * steps
-        self.keep = 3 * steps
-        self.fine = 2 * steps
-        self.velocity = steps * steps
-        self.diffusion = self.velocity + steps
-        self.start = self.diffusion + steps
-        self.start_low = self.start + steps
-        self.first_rows = self.start_low + steps
-        self.tail = self.wide
-        self.far_velocity = self.tail + self.fine
-        self.far_diffusion = self.far_velocity + self.wide
-        self.second_rows = self.far_diffusion + self.wide
+        self.groups = steps // 2
+        self.outer = steps * steps
+        self.velocity = self.outer + self.groups * steps
+        self.diffusion = self.velocity + self.fine
+        self.start = self.diffusion + self.fine
+        self.start_low = self.start + self.fine
+        self.first_rows = self.start_low + self.fine
+        self.sent = self.wide - steps
+        self.far_velocity = self.sent
+        self.far_diffusion = self.far_velocity + self.wide - self.fine
+        self.second_rows = self.far_diffusion + self.wide - self.fine
 
     def centred(self, width, inside):
         return slice(width - inside, width + self.own + inside)
 
 
-def pack(lay, velocity, diffusion, forcing, start, head, tail, start_kept, semaphores):
-    steps, own = lay.steps, lay.own
+def pack(lay, velocity, diffusion, forcing, start, head, tail, start_kept, outer_kept, semaphores):
+    steps, own, fine = lay.steps, lay.own, lay.fine
+    sides = ((head, 0, 0, steps), (tail, own - fine, own - steps, own - fine))
     copies = [(start, start_kept)]
-    for out, first in ((head, 0), (tail, own - steps)):
-        near = pl.ds(first, steps)
+    for side, (out, first, inner, outer) in enumerate(sides):
+        near = pl.ds(first, fine)
+        copies.append((forcing.at[:, pl.ds(outer, steps)], outer_kept.at[side]))
         for step in range(steps):
-            copies.append((forcing.at[step, near], out.at[pl.ds(step * steps, steps)]))
-        copies.append((velocity.at[near], out.at[pl.ds(lay.velocity, steps)]))
-        copies.append((diffusion.at[near], out.at[pl.ds(lay.diffusion, steps)]))
+            copies.append((forcing.at[step, pl.ds(inner, steps)], out.at[pl.ds(step * steps, steps)]))
+        copies.append((velocity.at[near], out.at[pl.ds(lay.velocity, fine)]))
+        copies.append((diffusion.at[near], out.at[pl.ds(lay.diffusion, fine)]))
     copies = [pltpu.make_async_copy(*pair, semaphores.at[i]) for i, pair in enumerate(copies)]
     for copy in copies:
         copy.start()
     for copy in copies:
         copy.wait()
-    for out, first in ((head, 0), (tail, own - steps)):
-        high, low = split(start_kept[first : first + steps])
+    for side, (out, first, _, _) in enumerate(sides):
+        high, low = split(start_kept[first : first + fine])
         out[lay.start : lay.start_low] = high
         out[lay.start_low : lay.first_rows] = low
+        for group in range(lay.groups):
+            one = outer_kept[side, group].astype(F32)
+            other = outer_kept[side, steps - 1 - group].astype(F32)
+            row = lax.broadcasted_iota(jnp.int32, one.shape, 0)
+            if side == 0:
+                both = jnp.where(row < steps - 1 - group, one, turned(other, -group))
+            else:
+                both = jnp.where(row > group, one, turned(other, group))
+            at = lay.outer + group * steps
+            out[at : at + steps] = both.astype(BF16)
 
 
 def split_matrices(implicit, coarse_implicit, high_m, low_m, coarse, fine_kept, coarse_kept, semaphores):
@@ -94,59 +112,92 @@
     return jnp.concatenate([low.astype(F32), own.astype(F32), high.astype(F32)], axis=0)
 
 
-def from_first(lay, low, own, high, at):
-    rows = slice(at, at + lay.steps)
+def near_forcing(lay, low, own, high, step):
+    rows = slice(step * lay.steps, (step + 1) * lay.steps)
     return joined(low[rows], own, high[rows])
 
 
-def start_from_first(lay, low, own, high):
-    value = from_first(lay, low, own, high, lay.start)
-    return value + from_first(lay, low, jnp.zeros(own.shape, F32), high, lay.start_low)
+def near_start(lay, low, own, high):
+    def side(packed, at):
+        rows = slice(at, at + lay.steps)
+        shift = lay.start_low - lay.start
+        return packed[rows].astype(F32) + packed[rows.start + shift : rows.stop + shift].astype(F32)
+
+    return joined(side(low, lay.start + lay.fine - lay.steps), own, side(high, lay.start))
 
 
 def make_weights(moving, spread):
     return spread + 0.5 * moving, 1.0 - 2.0 * spread, spread - 0.5 * moving
 
 
-def first_sweep(lay, place, low, high, forcing, velocity, diffusion, start, high_m, low_m, a, head, tail):
+def inner_sweep(lay, place, forcing, velocity, diffusion, start, high_m, low_m, a, head, tail):
     steps, own = lay.steps, lay.own
-    weights = make_weights(
-        from_first(lay, low, velocity[...], high, lay.velocity),
-        from_first(lay, low, diffusion[...], high, lay.diffusion),
-    )
-    current = jnp.where(place[0] == 0, start_from_first(lay, low, start[...], high), 0.0)
+    weights = make_weights(velocity[...].astype(F32), diffusion[...].astype(F32))
+    current = jnp.where(place[0] == 0, start[...], 0.0)
     for step in range(steps):
-        summed = stencil(current, weights) + from_first(lay, low, forcing[step], high, step * steps)
-        current = product3(summed, high_m[...], low_m[...])
-    current = current[lay.centred(steps, 0)]
+        current = product3(stencil(current, weights) + forcing[step].astype(F32), high_m[...], low_m[...])
     a[...] = current
-    high_part, low_part = split(current)
-    for out, far, near in (
-        (head, slice(0, lay.wide), slice(0, lay.fine)),
-        (tail, slice(own - lay.wide, own), slice(own - lay.fine, own)),
+    for out, first, far in (
+        (head, steps, slice(lay.fine, lay.wide)),
+        (tail, own - steps - lay.sent, slice(own - lay.wide, own - lay.fine)),
     ):
-        out[: lay.tail] = high_part[far]
-        out[lay.tail : lay.far_velocity] = low_part[near]
+        out[: lay.sent] = current[first : first + lay.sent].astype(BF16)
         out[lay.far_velocity : lay.far_diffusion] = velocity[far]
         out[lay.far_diffusion :] = diffusion[far]
 
 
-def second_sweep(lay, low, high, a, velocity, diffusion, high_m, low_m, rho, rho_low, a_near, weights):
-    wide, steps, fine = lay.wide, lay.steps, lay.fine
-
-    def extended(own, at):
-        return joined(low[at : at + wide], own, high[at : at + wide])
+def edge_sweep(lay, place, low, high, forcing, velocity, diffusion, start, high_m, low_m, edges):
+    steps, own, fine = lay.steps, lay.own, lay.fine
+
+    def windows(before, ours, after):
+        return jnp.concatenate(
+            [part.astype(F32) for part in (before, ours[:fine], ours[own - fine :], after)], axis=0
+        )
+
+    def packed(ours, at):
+        return windows(low[at : at + fine], ours, high[at : at + fine])
+
+    weights = make_weights(packed(velocity[...], lay.velocity), packed(diffusion[...], lay.diffusion))
+    current = packed(start[...], lay.start)
+    current = current + packed(jnp.zeros((own, start.shape[1]), F32), lay.start_low)
+    current = jnp.where(place[0] == 0, current, 0.0)
+    for step in range(steps):
+        rows = slice(step * steps, (step + 1) * steps)
+        group = min(step, steps - 1 - step)
+        at = lay.outer + group * steps
+        before, after = low[at : at + steps].astype(F32), high[at : at + steps].astype(F32)
+        if step > group:
+            before, after = turned(before, -group), turned(after, group)
+        source = windows(
+            jnp.concatenate([before, low[rows].astype(F32)], axis=0),
+            forcing[step],
+            jnp.concatenate([high[rows].astype(F32), after], axis=0),
+        )
+        current = product3(stencil(current, weights) + source, high_m[...], low_m[...])
+    edges[:fine] = current[steps : steps + fine]
+    edges[fine:] = current[3 * steps + fine : 3 * steps + 2 * fine]
+
+
+def second_sweep(
+    lay, low, high, far_low, far_high, a, edges, velocity, diffusion, high_m, low_m, rho, rho_low, a_near, weights
+):
+    steps, fine, wide, own = lay.steps, lay.fine, lay.wide, lay.own
+
+    def extended(ours, at, far):
+        rows, far_rows = slice(at, at + fine), slice(far, far + wide - fine)
+        return joined(
+            jnp.concatenate([far_low[far_rows].astype(F32), low[rows].astype(F32)], axis=0),
+            ours,
+            jnp.concatenate([high[rows].astype(F32), far_high[far_rows].astype(F32)], axis=0),
+        )
 
     weights[0], weights[1], weights[2] = make_weights(
-        extended(velocity[...], lay.far_velocity), extended(diffusion[...], lay.far_diffusion)
-    )
-    tails = slice(lay.tail, lay.far_velocity)
-    current = joined(
-        jnp.concatenate([low[: wide - fine].astype(F32), low[wide - fine : wide].astype(F32) + low[tails].astype(F32)], axis=0),
-        a[...],
-        jnp.concatenate([high[:fine].astype(F32) + high[tails].astype(F32), high[fine:wide].astype(F32)], axis=0),
-    )
-    a_near[...] = current[lay.centred(wide, steps)]
+        extended(velocity[...], lay.velocity, lay.far_velocity),
+        extended(diffusion[...], lay.diffusion, lay.far_diffusion),
+    )
+    near = jnp.concatenate([edges[:fine], a[steps : own - steps], edges[fine:]], axis=0)
+    a_near[...] = near
+    current = joined(far_low[: lay.sent], near, far_high[: lay.sent])
     for _ in range(steps):
         current = product3(stencil(current, weights[...]), high_m[...], low_m[...])
     high_part, low_part = split(current)
@@ -229,7 +280,7 @@
 
     error = lax.fori_loop(2, at - 1, turn, jnp.zeros((rows, start.shape[1]), F32))
     b_before = passed[:rows].astype(F32) + passed[rows : 2 * rows].astype(F32)
-    initial = start_from_first(lay, low, start[...], high)
+    initial = near_start(lay, low, start[...], high)
     current = jnp.where(at == 0, initial, b_before + error)
     mid = lay.centred(steps, 0)
     last = product(error[mid].astype(BF16), coarse[...])
@@ -237,7 +288,7 @@
     last = last + passed[2 * rows :].astype(F32)
     out[steps - 1] = b_own[...] + jnp.where(at == 0, 0.0, last)
     for step in range(steps - 1):
-        summed = stencil(current, narrow) + from_first(lay, low, forcing[step], high, step * steps)
+        summed = stencil(current, narrow) + near_forcing(lay, low, forcing[step], high, step)
         current = product3(summed, high_m[...], low_m[...])
         out[step] = current[mid]
 
@@ -288,7 +339,11 @@
     head, tail = call_from_hbm(
         functools.partial(pack, lay),
         [first_pack] * 2,
-        [pltpu.VMEM((own, columns), F32), pltpu.SemaphoreType.DMA((1 + 2 * (steps + 2),))],
+        [
+            pltpu.VMEM((own, columns), F32),
+            pltpu.VMEM((2, steps, steps, columns), BF16),
+            pltpu.SemaphoreType.DMA((1 + 2 * (steps + 3),)),
+        ],
         velocity, diffusion, forcing, initial_state,
     )
     low = in_vmem(lax.ppermute(tail, "space", ring(slabs, 1)))
@@ -302,13 +357,19 @@
     high_m, low_m, coarse = in_vmem(high_m), in_vmem(low_m), in_vmem(coarse)
     second_pack = kept(lay.second_rows, columns, dtype=BF16)
     a, head, tail = call(
-        first_sweep,
+        inner_sweep,
         lay,
         [kept(own, columns), second_pack, second_pack],
-        place, low, high, forcing, velocity, diffusion, initial_state, high_m, low_m,
+        place, forcing, velocity, diffusion, initial_state, high_m, low_m,
     )
     far_low = in_vmem(lax.ppermute(tail, "space", ring(slabs, 1)))
     far_high = in_vmem(lax.ppermute(head, "space", ring(slabs, -1)))
+    edges = call(
+        edge_sweep,
+        lay,
+        kept(2 * lay.fine, columns),
+        place, low, high, forcing, velocity, diffusion, initial_state, high_m, low_m,
+    )
     rho, rho_low, a_near, weights = call(
         second_sweep,
         lay,
@@ -318,7 +379,7 @@
             kept(near, columns),
             kept(3, own + 2 * lay.wide, columns),
         ],
-        far_low, far_high, in_vmem(a), velocity, diffusion, high_m, low_m,
+        low, high, far_low, far_high, in_vmem(a), in_vmem(edges), velocity, diffusion, high_m, low_m,
     )
     weights = in_vmem(weights)
     rho_all = lax.all_gather(rho, "tm", axis=0)

time: 53.3 us -> 49.1 us (0.921)
  waiting for transfers between devices: 12.7 us -> 5.67 us
  Pallas kernels: 20.2 us -> 22.7 us
    ppermute x1, waiting for transfers between devices: 3.75 us -> 0.01 us  [per_device(): far_low = in_vmem(lax.ppermute(tail, 'space', ring(slabs, 1)))]
    pallas_call x5 -> x6, Pallas kernels: 17.5 us -> 19.7 us  [call(): pl.pallas_call(kernel if lay is None else functools.partial(kernel, lay),...]
    ppermute x1, waiting for transfers between devices: 1.68 us -> 0.01 us  [per_device(): low = in_vmem(lax.ppermute(tail, 'space', ring(slabs, 1)))]
    ppermute x1, starting transfers between devices: 1.19 us -> 0.06 us  [per_device(): far_low = in_vmem(lax.ppermute(tail, 'space', ring(slabs, 1)))]
    ppermute x1, starting transfers between devices: 2.68 us -> 3.81 us  [per_device(): far_high = in_vmem(lax.ppermute(head, 'space', ring(slabs, -1)))]
    ppermute x1, waiting for transfers between devices: 0.9 us -> 0.01 us  [per_device(): high = in_vmem(lax.ppermute(head, 'space', ring(slabs, -1)))]
    ppermute x1, waiting for transfers between devices: 0.7 us -> 0.01 us  [per_device(): far_high = in_vmem(lax.ppermute(head, 'space', ring(slabs, -1)))]
  transfers between devices with their start and end apart: 6 -> 6, of which waited for: 5 -> 1; matrix products, arithmetic and copies ran while one was open for 0% -> 0% of each run, Pallas kernels for 3% -> 13%
where the time goes in v6:
time: 49.1 us; the launch traced here: 48.8 us
  Pallas kernels  22.7 us (46%)
  blocking collectives  10.7 us (22%)
  starting transfers between devices  9.64 us (20%)
  waiting for transfers between devices  5.67 us (12%)
    pallas_call x6, Pallas kernels, call(): pl.pallas_call(kernel if lay is None else functools.partial(kernel, lay),...  19.7 us
    all_gather x1, blocking collectives, per_device(): rho_all = lax.all_gather(rho, 'tm', axis=0)  10.7 us
    ppermute x1, waiting for transfers between devices, per_device(): passed = lax.ppermute(passed, 'tm', ring(blocks, 1))  5.66 us
    ppermute x1, starting transfers between devices, per_device(): far_high = in_vmem(lax.ppermute(head, 'space', ring(slabs, -1)))  3.81 us
    ppermute x1, starting transfers between devices, per_device(): low = in_vmem(lax.ppermute(tail, 'space', ring(slabs, 1)))  3.1 us
    pallas_call x2, Pallas kernels, call_from_hbm(): pl.pallas_call(kernel, out_shape=outs, in_specs=[pl.BlockSpec(memory_spac...  2.95 us
    ppermute x1, starting transfers between devices, per_device(): high = in_vmem(lax.ppermute(head, 'space', ring(slabs, -1)))  2.09 us
  transfers between devices with their start and end apart: 6, of which 1 were waited for; matrix products, arithmetic and copies ran while one was open for 0% of the time, Pallas kernels for 13%

profile of v6, /device:TPU:0, one launch (start us, length us, event | category | flops | bytes accessed | tf_op | source)
XLA Modules:
  0.0 48.8 jit_solution(14708153403577760486)
XLA Ops:
  0.0 1.3 %shard_map.64 = (bf16[160,512]{1,0:T(8,128)(2,1)S(1)}, bf16[160,512]{1,0:T(8,128)(2,1)S(1)}) custom-call(bf16[48,512]{1,0:T(8,128)(2,1)} %velocity.7, bf16[48,512]{1,0:T(8,128)(2,1)} %diffusion.7, bf16[8,48,512]{2,1,0:T(8,128)(2,1)} %forcing.7, f32[48,512]{1,0:T(8,128)} %start.7), custom_call_target="tpu_custom_call" | custom-call | tf_op jit(solution)/shard_map/pallas_call | solution.py:316
  1.3 3.1 %collective-permute-start = (bf16[160,512]{1,0:T(8,128)(2,1)S(1)}, bf16[160,512]{1,0:T(8,128)(2,1)S(1)}, u32[]{:S(2)}, u32[]{:S(2)}) collective-permute-start(bf16[160,512]{1,0:T(8,128)(2,1)S(1)} %get-tuple-element.20), channel_id=1, source_target_pairs={{0,1},{1,2},{2,3},{3,0},{4,5},{5,6},{6,7},{7,4},{8,9},{9,10},{10,1... | collective-permute-start | bytes 491528 | tf_op jit(solution)/shard_map/ppermute | solution.py:349
  4.4 2.1 %collective-permute-start.1 = (bf16[160,512]{1,0:T(8,128)(2,1)S(1)}, bf16[160,512]{1,0:T(8,128)(2,1)S(1)}, u32[]{:S(2)}, u32[]{:S(2)}) collective-permute-start(bf16[160,512]{1,0:T(8,128)(2,1)S(1)} %get-tuple-element.21), channel_id=1, source_target_pairs={{0,3},{1,0},{2,1},{3,2},{4,7},{5,4},{6,5},{7,6},{8,11},{9,8},{10,9... | collective-permute-start | bytes 491528 | tf_op jit(solution)/shard_map/ppermute | solution.py:350
  6.5 0.0 copy-start
  6.5 0.0 copy-start.1
  6.5 0.0 copy-start.2
  6.5 0.0 copy-start.3
  6.5 1.7 %shard_map.65 = (bf16[512,512]{1,0:T(8,128)(2,1)S(1)}, bf16[512,512]{1,0:T(8,128)(2,1)S(1)}, bf16[512,512]{1,0:T(8,128)(2,1)S(1)}) custom-call(f32[512,512]{1,0:T(8,128)} %implicit.1, f32[512,512]{1,0:T(8,128)} %coarse_implicit.1), custom_call_target="tpu_custom_call" | custom-call | tf_op jit(solution)/shard_map/pallas_call | solution.py:316
  8.2 0.0 copy-done
  8.2 0.0 copy-done.1
  8.2 0.0 copy-done.2
  8.2 0.0 copy-done.3
  8.2 2.3 %shard_map.66 = (f32[48,512]{1,0:T(8,128)S(1)}, bf16[56,512]{1,0:T(8,128)(2,1)S(1)}, bf16[56,512]{1,0:T(8,128)(2,1)S(1)}) custom-call(s32[1]{0:T(128)} %bitcast.place, bf16[8,48,512]{2,1,0:T(8,128)(2,1)S(1)} %copy-done, bf16[48,512]{1,0:T(8,128)(2,1)S(1)} %copy-done.2, bf16[48,512]{1,0:T(8,128)(2,1)S(1)} %copy-done.3, f32[48,512]{1,0:T(8,128)S(1)} %copy-done.1, ...), custom_call_target="tpu_custom_call" | custom-call | tf_op jit(solution)/shard_map/pallas_call | solution.py:306
  10.5 0.1 collective-permute-start.2
  10.6 3.8 %collective-permute-start.3 = (bf16[56,512]{1,0:T(8,128)(2,1)S(1)}, bf16[56,512]{1,0:T(8,128)(2,1)S(1)}, u32[]{:S(2)}, u32[]{:S(2)}) collective-permute-start(bf16[56,512]{1,0:T(8,128)(2,1)S(1)} %get-tuple-element.25), channel_id=1, source_target_pairs={{0,3},{1,0},{2,1},{3,2},{4,7},{5,4},{6,5},{7,6},{8,11},{9,8},{10,9... | collective-permute-start | bytes 172040 | tf_op jit(solution)/shard_map/ppermute | solution.py:366
  14.4 0.0 collective-permute-done.low
  14.4 0.0 collective-permute-done.1.high
  14.4 2.4 %shard_map.67.edges = f32[32,512]{1,0:T(8,128)S(1)} custom-call(s32[1]{0:T(128)} %bitcast.place, bf16[160,512]{1,0:T(8,128)(2,1)S(1)} %collective-permute-done.low, bf16[160,512]{1,0:T(8,128)(2,1)S(1)} %collective-permute-done.1.high, bf16[8,48,512]{2,1,0:T(8,128)(2,1)S(1)} %copy-done, bf16[48,512]{1,0:T(8,128)(2,1)S(1)} %copy-done.2, ...), custom_call_target="tpu_custom_call" | custom-call | tf_op jit(solution)/shard_map/pallas_call | solution.py:306
  16.8 0.0 collective-permute-done.2.far_low
  16.8 0.0 collective-permute-done.3.far_high
  16.8 3.0 %shard_map.68 = (bf16[96,512]{1,0:T(8,128)(2,1)S(1)}, bf16[48,512]{1,0:T(8,128)(2,1)S(1)}, f32[64,512]{1,0:T(8,128)S(1)}, f32[3,112,512]{2,1,0:T(8,128)S(1)}) custom-call(bf16[160,512]{1,0:T(8,128)(2,1)S(1)} %collective-permute-done.low, bf16[160,512]{1,0:T(8,128)(2,1)S(1)} %collective-permute-done.1.high, ...), custom_call_target="tpu_custom_call" | custom-call | tf_op jit(solution)/shard_map/pallas_call | solution.py:306
  19.8 10.7 %all-gather = bf16[768,512]{1,0:T(8,128)(2,1)S(1)} all-gather(bf16[96,512]{1,0:T(8,128)(2,1)S(1)} %get-tuple-element.27), channel_id=2, replica_groups=mesh['tm'=8,'space'=4] {'tm'}, dimensions={0}, use_global_device_ids=true | all-gather | bytes 884736 | tf_op jit(solution)/shard_map/all_gather | solution.py:385
  30.6 6.4 %shard_map.69 = (f32[3,80,512]{2,1,0:T(8,128)S(1)}, bf16[176,512]{1,0:T(8,128)(2,1)S(1)}, f32[48,512]{1,0:T(8,128)S(1)}) custom-call(s32[1]{0:T(128)} %bitcast.place, bf16[8,96,512]{2,1,0:T(8,128)(2,1)S(1)} %bitcast.2, bf16[48,512]{1,0:T(8,128)(2,1)S(1)} %get-tuple-element.28.rho_low, f32[64,512]{1,0:T(8,128)S(1)} %get-tuple-element.29.a_near, ...), custom_call_target="tpu_custom_call" | custom-call | tf_op jit(solution)/shard_map/pallas_call | solution.py:306
  36.9 2.6 %shard_map.70.psi = bf16[3,64,512]{2,1,0:T(8,128)(2,1)S(1)} custom-call(f32[3,80,512]{2,1,0:T(8,128)S(1)} %get-tuple-element.32.change, f32[3,112,512]{2,1,0:T(8,128)S(1)} %get-tuple-element.30.weights, bf16[512,512]{1,0:T(8,128)(2,1)S(1)} %get-tuple-element.22.high_m), custom_call_target="tpu_custom_call" | custom-call | tf_op jit(solution)/shard_map/pallas_call | solution.py:306
  39.5 0.4 collective-permute-start.4
  39.9 0.2 collective-permute-start.5
  40.1 5.7 %collective-permute-done.5.passed = bf16[176,512]{1,0:T(8,128)(2,1)S(1)} collective-permute-done((bf16[176,512]{1,0:T(8,128)(2,1)S(1)}, bf16[176,512]{1,0:T(8,128)(2,1)S(1)}, u32[]{:S(2)}, u32[]{:S(2)}) %collective-permute-start.5) | collective-permute-done | bytes 180256 | tf_op jit(solution)/shard_map/ppermute | solution.py:398
  45.7 0.0 collective-permute-done.4.psi_other
  45.7 3.1 %shard_map.71 = f32[8,48,512]{2,1,0:T(8,128)} custom-call(s32[1]{0:T(128)} %bitcast.place, bf16[3,64,512]{2,1,0:T(8,128)(2,1)S(1)} %shard_map.70.psi, bf16[3,64,512]{2,1,0:T(8,128)(2,1)S(1)} %collective-permute-done.4.psi_other, bf16[176,512]{1,0:T(8,128)(2,1)S(1)} %collective-permute-done.5.passed, f32[48,512]{1,0:T(8,128)S(1)} %get-tuple-element.34.b_own, ...), custom_call_target="tpu_custom_call" | custom-call | tf_op jit(solution)/shard_map/pallas_call | solution.py:306
Async XLA Ops:
  1.3 13.1 %collective-permute-start = (bf16[160,512]{1,0:T(8,128)(2,1)S(1)}, bf16[160,512]{1,0:T(8,128)(2,1)S(1)}, u32[]{:S(2)}, u32[]{:S(2)}) collective-permute-start(bf16[160,512]{1,0:T(8,128)(2,1)S(1)} %get-tuple-element.20), channel_id=1, source_target_pairs={{0,1},{1,2},{2,3},{3,0},{4,5},{5,6},{6,7},{7,4},{8,9},{9,10},{10,1... | collective-permute-start | bytes 491528 | tf_op jit(solution)/shard_map/ppermute | solution.py:349
  4.4 10.0 %collective-permute-start.1 = (bf16[160,512]{1,0:T(8,128)(2,1)S(1)}, bf16[160,512]{1,0:T(8,128)(2,1)S(1)}, u32[]{:S(2)}, u32[]{:S(2)}) collective-permute-start(bf16[160,512]{1,0:T(8,128)(2,1)S(1)} %get-tuple-element.21), channel_id=1, source_target_pairs={{0,3},{1,0},{2,1},{3,2},{4,7},{5,4},{6,5},{7,6},{8,11},{9,8},{10,9... | collective-permute-start | bytes 491528 | tf_op jit(solution)/shard_map/ppermute | solution.py:350
  6.5 1.7 %copy-start = (bf16[8,48,512]{2,1,0:T(8,128)(2,1)S(1)}, bf16[8,48,512]{2,1,0:T(8,128)(2,1)}, u32[]{:S(2)}) copy-start(bf16[8,48,512]{2,1,0:T(8,128)(2,1)} %forcing.7) | copy-start | bytes 1179652
  6.5 1.7 %copy-start.1 = (f32[48,512]{1,0:T(8,128)S(1)}, f32[48,512]{1,0:T(8,128)}, u32[]{:S(2)}) copy-start(f32[48,512]{1,0:T(8,128)} %start.7) | copy-start | bytes 294916
  6.5 1.7 %copy-start.2 = (bf16[48,512]{1,0:T(8,128)(2,1)S(1)}, bf16[48,512]{1,0:T(8,128)(2,1)}, u32[]{:S(2)}) copy-start(bf16[48,512]{1,0:T(8,128)(2,1)} %velocity.7) | copy-start | bytes 147460
  6.5 1.7 %copy-start.3 = (bf16[48,512]{1,0:T(8,128)(2,1)S(1)}, bf16[48,512]{1,0:T(8,128)(2,1)}, u32[]{:S(2)}) copy-start(bf16[48,512]{1,0:T(8,128)(2,1)} %diffusion.7) | copy-start | bytes 147460
  10.5 6.3 %collective-permute-start.2 = (bf16[56,512]{1,0:T(8,128)(2,1)S(1)}, bf16[56,512]{1,0:T(8,128)(2,1)S(1)}, u32[]{:S(2)}, u32[]{:S(2)}) collective-permute-start(bf16[56,512]{1,0:T(8,128)(2,1)S(1)} %get-tuple-element.24), channel_id=1, source_target_pairs={{0,1},{1,2},{2,3},{3,0},{4,5},{5,6},{6,7},{7,4},{8,9},{9,10},{10,1... | collective-permute-start | bytes 172040 | tf_op jit(solution)/shard_map/ppermute | solution.py:365
  10.6 6.3 %collective-permute-start.3 = (bf16[56,512]{1,0:T(8,128)(2,1)S(1)}, bf16[56,512]{1,0:T(8,128)(2,1)S(1)}, u32[]{:S(2)}, u32[]{:S(2)}) collective-permute-start(bf16[56,512]{1,0:T(8,128)(2,1)S(1)} %get-tuple-element.25), channel_id=1, source_target_pairs={{0,3},{1,0},{2,1},{3,2},{4,7},{5,4},{6,5},{7,6},{8,11},{9,8},{10,9... | collective-permute-start | bytes 172040 | tf_op jit(solution)/shard_map/ppermute | solution.py:366
  39.5 6.2 %collective-permute-start.4 = (bf16[3,64,512]{2,1,0:T(8,128)(2,1)S(1)}, bf16[3,64,512]{2,1,0:T(8,128)(2,1)S(1)}, u32[]{:S(2)}, u32[]{:S(2)}) collective-permute-start(bf16[3,64,512]{2,1,0:T(8,128)(2,1)S(1)} %shard_map.70.psi), channel_id=1, source_target_pairs={{0,4},{4,0},{8,12},{12,8},{16,20},{20,16},{24,28},{28,24},{1,5},{5... | collective-permute-start | bytes 589832 | tf_op jit(solution)/shard_map/ppermute | solution.py:401
  39.9 5.8 %collective-permute-start.5 = (bf16[176,512]{1,0:T(8,128)(2,1)S(1)}, bf16[176,512]{1,0:T(8,128)(2,1)S(1)}, u32[]{:S(2)}, u32[]{:S(2)}) collective-permute-start(bf16[176,512]{1,0:T(8,128)(2,1)S(1)} %get-tuple-element.33), channel_id=1, source_target_pairs={{0,4},{4,8},{8,12},{12,16},{16,20},{20,24},{24,28},{28,0},{1,5},{5... | collective-permute-start | bytes 540680 | tf_op jit(solution)/shard_map/ppermute | solution.py:398

commit v7 on v6

--- a/solution.py
+++ b/solution.py
@@ -11,6 +11,7 @@
 F32 = jnp.float32
 BF16 = jnp.bfloat16
 LIMIT = 16 << 20
+MARGIN = 8
 
 
 def ring(count, distance):
@@ -36,6 +37,19 @@
 def stencil(value, weights):
     west, centre, east = weights
     return centre * value + east * jnp.roll(value, -1, 0) + west * jnp.roll(value, 1, 0)
+
+
+def stored_stencil(kept, value, weights):
+    west, centre, east = weights
+    rows = value.shape[0]
+    kept[MARGIN : MARGIN + rows] = value
+    return centre * value + east * kept[MARGIN + 1 : MARGIN + 1 + rows] + west * kept[MARGIN - 1 : MARGIN - 1 + rows]
+
+
+def clear_margins(kept):
+    rows = kept.shape[0]
+    kept[:MARGIN] = jnp.zeros((MARGIN, kept.shape[1]), F32)
+    kept[rows - MARGIN :] = jnp.zeros((MARGIN, kept.shape[1]), F32)
 
 
 def turned(value, shift):
@@ -179,7 +193,7 @@
 
 
 def second_sweep(
-    lay, low, high, far_low, far_high, a, edges, velocity, diffusion, high_m, low_m, rho, rho_low, a_near, weights
+    lay, low, high, far_low, far_high, a, edges, velocity, diffusion, high_m, low_m, rho, rho_low, a_near, weights, kept
 ):
     steps, fine, wide, own = lay.steps, lay.fine, lay.wide, lay.own
 
@@ -198,14 +212,15 @@
     near = jnp.concatenate([edges[:fine], a[steps : own - steps], edges[fine:]], axis=0)
     a_near[...] = near
     current = joined(far_low[: lay.sent], near, far_high[: lay.sent])
+    clear_margins(kept)
     for _ in range(steps):
-        current = product3(stencil(current, weights[...]), high_m[...], low_m[...])
+        current = product3(stored_stencil(kept, current, weights[...]), high_m[...], low_m[...])
     high_part, low_part = split(current)
     rho[...] = high_part[lay.centred(wide, lay.keep)]
     rho_low[...] = low_part[lay.centred(wide, 0)]
 
 
-def coarse_and_third(lay, place, rho, rho_low, a_near, weights, high_m, low_m, coarse, change, passed, b_own):
+def coarse_and_third(lay, place, rho, rho_low, a_near, weights, high_m, low_m, coarse, change, passed, b_own, field):
     keep, steps, own = lay.keep, lay.steps, lay.own
     rows = own + 2 * keep
     count = change.shape[0]
@@ -231,9 +246,10 @@
         errors = [lax.fori_loop(1, at - 1, turn, first)]
     kept = jnp.concatenate([error.astype(BF16) for error in errors], axis=0)
     current = jnp.concatenate(errors, axis=0)
+    narrow = jnp.concatenate([narrow] * count, axis=1)
+    clear_margins(field)
     for _ in range(steps):
-        moved = [stencil(current[i * rows : (i + 1) * rows], narrow) for i in range(count)]
-        current = product3(jnp.concatenate(moved, axis=0), high_m[...], low_m[...])
+        current = product3(stored_stencil(field, current, narrow), high_m[...], low_m[...])
     coarse_part = product(kept, coarse[...])
     mine = jnp.zeros((own + 2 * steps, current.shape[1]), F32)
     inner = lay.centred(keep, lay.fine)
@@ -250,14 +266,15 @@
     passed[2 * rows :] = rho_low[...]
 
 
-def fourth_sweep(lay, change, weights, high_m, psi):
+def fourth_sweep(lay, change, weights, high_m, psi, field):
     steps = lay.steps
     count, rows, _ = change.shape
     narrow = weights[:, lay.centred(lay.wide, lay.fine)]
+    narrow = jnp.concatenate([narrow] * count, axis=1)
     current = jnp.concatenate([change[i] for i in range(count)], axis=0)
+    clear_margins(field)
     for _ in range(steps):
-        moved = [stencil(current[i * rows : (i + 1) * rows], narrow).astype(BF16) for i in range(count)]
-        current = product(jnp.concatenate(moved, axis=0), high_m[...])
+        current = product(stored_stencil(field, current, narrow).astype(BF16), high_m[...])
     for i in range(count):
         psi[i] = current[i * rows : (i + 1) * rows][lay.centred(lay.fine, steps)].astype(BF16)
 
@@ -301,13 +318,14 @@
     return pltpu.with_memory_space_constraint(value, pltpu.VMEM)
 
 
-def call(kernel, lay, outs, *operands):
+def call(kernel, lay, outs, *operands, field=0):
     spaces = [pltpu.SMEM if o.dtype == jnp.int32 else pltpu.VMEM for o in operands]
     return pl.pallas_call(
         kernel if lay is None else functools.partial(kernel, lay),
         out_shape=outs,
         in_specs=[pl.BlockSpec(memory_space=space) for space in spaces],
         out_specs=jax.tree.map(lambda _: pl.BlockSpec(memory_space=pltpu.VMEM), outs),
+        scratch_shapes=[pltpu.VMEM((field + 2 * MARGIN, operands[-1].shape[1]), F32)] if field else [],
         compiler_params=pltpu.CompilerParams(vmem_limit_bytes=LIMIT),
     )(*operands)
 
@@ -380,6 +398,7 @@
             kept(3, own + 2 * lay.wide, columns),
         ],
         low, high, far_low, far_high, in_vmem(a), in_vmem(edges), velocity, diffusion, high_m, low_m,
+        field=own + 2 * lay.wide,
     )
     weights = in_vmem(weights)
     rho_all = lax.all_gather(rho, "tm", axis=0)
@@ -394,9 +413,16 @@
             kept(own, columns),
         ],
         place, rho_all, in_vmem(rho_low), in_vmem(a_near), weights, high_m, low_m, coarse,
+        field=count * (own + 2 * lay.keep),
     )
     passed = lax.ppermute(passed, "tm", ring(blocks, 1))
-    psi = call(fourth_sweep, lay, kept(count, near, columns, dtype=BF16), in_vmem(change), weights, high_m)
+    psi = call(
+        fourth_sweep,
+        lay,
+        kept(count, near, columns, dtype=BF16),
+        in_vmem(change), weights, high_m,
+        field=count * (own + 2 * lay.fine),
+    )
     if shared:
         psi_other = lax.ppermute(psi, "tm", [(i, i ^ 1) for i in range(blocks)])
         sources, kernel = (in_vmem(psi), in_vmem(psi_other)), last_sweep

time: 49.1 us -> 47.9 us (0.976)
  Pallas kernels: 22.7 us -> 21.7 us
    pallas_call x6, Pallas kernels: 19.7 us -> 18.7 us  [call(): pl.pallas_call(kernel if lay is None else functools.partial(kernel, lay),...]
where the time goes in v7:
time: 47.9 us; the launch traced here: 47.7 us
  Pallas kernels  21.7 us (45%)
  blocking collectives  10.6 us (22%)
  starting transfers between devices  9.64 us (20%)
  waiting for transfers between devices  5.68 us (12%)
    pallas_call x6, Pallas kernels, call(): pl.pallas_call(kernel if lay is None else functools.partial(kernel, lay),...  18.7 us
    all_gather x1, blocking collectives, per_device(): rho_all = lax.all_gather(rho, 'tm', axis=0)  10.6 us
    ppermute x1, waiting for transfers between devices, per_device(): passed = lax.ppermute(passed, 'tm', ring(blocks, 1))  5.67 us
    ppermute x1, starting transfers between devices, per_device(): far_high = in_vmem(lax.ppermute(head, 'space', ring(slabs, -1)))  3.81 us
    ppermute x1, starting transfers between devices, per_device(): low = in_vmem(lax.ppermute(tail, 'space', ring(slabs, 1)))  3.1 us
    pallas_call x2, Pallas kernels, call_from_hbm(): pl.pallas_call(kernel, out_shape=outs, in_specs=[pl.BlockSpec(memory_spac...  2.95 us
    ppermute x1, starting transfers between devices, per_device(): high = in_vmem(lax.ppermute(head, 'space', ring(slabs, -1)))  2.09 us
  transfers between devices with their start and end apart: 6, of which 1 were waited for; matrix products, arithmetic and copies ran while one was open for 0% of the time, Pallas kernels for 13%

profile of v7, /device:TPU:0, one launch (start us, length us, event | category | flops | bytes accessed | tf_op | source)
XLA Modules:
  0.0 47.7 jit_solution(2164729044118236463)
XLA Ops:
  0.0 1.3 %shard_map.64 = (bf16[160,512]{1,0:T(8,128)(2,1)S(1)}, bf16[160,512]{1,0:T(8,128)(2,1)S(1)}) custom-call(bf16[48,512]{1,0:T(8,128)(2,1)} %velocity.7, bf16[48,512]{1,0:T(8,128)(2,1)} %diffusion.7, bf16[8,48,512]{2,1,0:T(8,128)(2,1)} %forcing.7, f32[48,512]{1,0:T(8,128)} %start.7), custom_call_target="tpu_custom_call" | custom-call | tf_op jit(solution)/shard_map/pallas_call | solution.py:334
  1.3 3.1 %collective-permute-start = (bf16[160,512]{1,0:T(8,128)(2,1)S(1)}, bf16[160,512]{1,0:T(8,128)(2,1)S(1)}, u32[]{:S(2)}, u32[]{:S(2)}) collective-permute-start(bf16[160,512]{1,0:T(8,128)(2,1)S(1)} %get-tuple-element.20), channel_id=1, source_target_pairs={{0,1},{1,2},{2,3},{3,0},{4,5},{5,6},{6,7},{7,4},{8,9},{9,10},{10,1... | collective-permute-start | bytes 491528 | tf_op jit(solution)/shard_map/ppermute | solution.py:367
  4.4 2.1 %collective-permute-start.1 = (bf16[160,512]{1,0:T(8,128)(2,1)S(1)}, bf16[160,512]{1,0:T(8,128)(2,1)S(1)}, u32[]{:S(2)}, u32[]{:S(2)}) collective-permute-start(bf16[160,512]{1,0:T(8,128)(2,1)S(1)} %get-tuple-element.21), channel_id=1, source_target_pairs={{0,3},{1,0},{2,1},{3,2},{4,7},{5,4},{6,5},{7,6},{8,11},{9,8},{10,9... | collective-permute-start | bytes 491528 | tf_op jit(solution)/shard_map/ppermute | solution.py:368
  6.5 0.0 copy-start
  6.5 0.0 copy-start.1
  6.5 0.0 copy-start.2
  6.5 0.0 copy-start.3
  6.5 1.7 %shard_map.65 = (bf16[512,512]{1,0:T(8,128)(2,1)S(1)}, bf16[512,512]{1,0:T(8,128)(2,1)S(1)}, bf16[512,512]{1,0:T(8,128)(2,1)S(1)}) custom-call(f32[512,512]{1,0:T(8,128)} %implicit.1, f32[512,512]{1,0:T(8,128)} %coarse_implicit.1), custom_call_target="tpu_custom_call" | custom-call | tf_op jit(solution)/shard_map/pallas_call | solution.py:334
  8.2 0.0 copy-done
  8.2 0.0 copy-done.1
  8.2 0.0 copy-done.2
  8.2 0.0 copy-done.3
  8.2 2.3 %shard_map.66 = (f32[48,512]{1,0:T(8,128)S(1)}, bf16[56,512]{1,0:T(8,128)(2,1)S(1)}, bf16[56,512]{1,0:T(8,128)(2,1)S(1)}) custom-call(s32[1]{0:T(128)} %bitcast.place, bf16[8,48,512]{2,1,0:T(8,128)(2,1)S(1)} %copy-done, bf16[48,512]{1,0:T(8,128)(2,1)S(1)} %copy-done.2, bf16[48,512]{1,0:T(8,128)(2,1)S(1)} %copy-done.3, f32[48,512]{1,0:T(8,128)S(1)} %copy-done.1, ...), custom_call_target="tpu_custom_call" | custom-call | tf_op jit(solution)/shard_map/pallas_call | solution.py:323
  10.5 0.1 collective-permute-start.2
  10.5 3.8 %collective-permute-start.3 = (bf16[56,512]{1,0:T(8,128)(2,1)S(1)}, bf16[56,512]{1,0:T(8,128)(2,1)S(1)}, u32[]{:S(2)}, u32[]{:S(2)}) collective-permute-start(bf16[56,512]{1,0:T(8,128)(2,1)S(1)} %get-tuple-element.25), channel_id=1, source_target_pairs={{0,3},{1,0},{2,1},{3,2},{4,7},{5,4},{6,5},{7,6},{8,11},{9,8},{10,9... | collective-permute-start | bytes 172040 | tf_op jit(solution)/shard_map/ppermute | solution.py:384
  14.4 0.0 collective-permute-done.low
  14.4 0.0 collective-permute-done.1.high
  14.4 2.4 %shard_map.67.edges = f32[32,512]{1,0:T(8,128)S(1)} custom-call(s32[1]{0:T(128)} %bitcast.place, bf16[160,512]{1,0:T(8,128)(2,1)S(1)} %collective-permute-done.low, bf16[160,512]{1,0:T(8,128)(2,1)S(1)} %collective-permute-done.1.high, bf16[8,48,512]{2,1,0:T(8,128)(2,1)S(1)} %copy-done, bf16[48,512]{1,0:T(8,128)(2,1)S(1)} %copy-done.2, ...), custom_call_target="tpu_custom_call" | custom-call | tf_op jit(solution)/shard_map/pallas_call | solution.py:323
  16.8 0.0 collective-permute-done.2.far_low
  16.8 0.0 collective-permute-done.3.far_high
  16.8 2.8 %shard_map.68 = (bf16[96,512]{1,0:T(8,128)(2,1)S(1)}, bf16[48,512]{1,0:T(8,128)(2,1)S(1)}, f32[64,512]{1,0:T(8,128)S(1)}, f32[3,112,512]{2,1,0:T(8,128)S(1)}) custom-call(bf16[160,512]{1,0:T(8,128)(2,1)S(1)} %collective-permute-done.low, bf16[160,512]{1,0:T(8,128)(2,1)S(1)} %collective-permute-done.1.high, ...), custom_call_target="tpu_custom_call" | custom-call | tf_op jit(solution)/shard_map/pallas_call | solution.py:323
  19.6 10.6 %all-gather = bf16[768,512]{1,0:T(8,128)(2,1)S(1)} all-gather(bf16[96,512]{1,0:T(8,128)(2,1)S(1)} %get-tuple-element.27), channel_id=2, replica_groups=mesh['tm'=8,'space'=4] {'tm'}, dimensions={0}, use_global_device_ids=true | all-gather | bytes 884736 | tf_op jit(solution)/shard_map/all_gather | solution.py:404
  30.2 6.0 %shard_map.69 = (f32[3,80,512]{2,1,0:T(8,128)S(1)}, bf16[176,512]{1,0:T(8,128)(2,1)S(1)}, f32[48,512]{1,0:T(8,128)S(1)}) custom-call(s32[1]{0:T(128)} %bitcast.place, bf16[8,96,512]{2,1,0:T(8,128)(2,1)S(1)} %bitcast.2, bf16[48,512]{1,0:T(8,128)(2,1)S(1)} %get-tuple-element.28.rho_low, f32[64,512]{1,0:T(8,128)S(1)} %get-tuple-element.29.a_near, ...), custom_call_target="tpu_custom_call" | custom-call | tf_op jit(solution)/shard_map/pallas_call | solution.py:323
  36.2 2.2 %shard_map.70.psi = bf16[3,64,512]{2,1,0:T(8,128)(2,1)S(1)} custom-call(f32[3,80,512]{2,1,0:T(8,128)S(1)} %get-tuple-element.32.change, f32[3,112,512]{2,1,0:T(8,128)S(1)} %get-tuple-element.30.weights, bf16[512,512]{1,0:T(8,128)(2,1)S(1)} %get-tuple-element.22.high_m), custom_call_target="tpu_custom_call" | custom-call | tf_op jit(solution)/shard_map/pallas_call | solution.py:323
  38.3 0.4 collective-permute-start.4
  38.8 0.2 collective-permute-start.5
  38.9 5.7 %collective-permute-done.5.passed = bf16[176,512]{1,0:T(8,128)(2,1)S(1)} collective-permute-done((bf16[176,512]{1,0:T(8,128)(2,1)S(1)}, bf16[176,512]{1,0:T(8,128)(2,1)S(1)}, u32[]{:S(2)}, u32[]{:S(2)}) %collective-permute-start.5) | collective-permute-done | bytes 180256 | tf_op jit(solution)/shard_map/ppermute | solution.py:418
  44.6 0.0 collective-permute-done.4.psi_other
  44.6 3.1 %shard_map.71 = f32[8,48,512]{2,1,0:T(8,128)} custom-call(s32[1]{0:T(128)} %bitcast.place, bf16[3,64,512]{2,1,0:T(8,128)(2,1)S(1)} %shard_map.70.psi, bf16[3,64,512]{2,1,0:T(8,128)(2,1)S(1)} %collective-permute-done.4.psi_other, bf16[176,512]{1,0:T(8,128)(2,1)S(1)} %collective-permute-done.5.passed, f32[48,512]{1,0:T(8,128)S(1)} %get-tuple-element.34.b_own, ...), custom_call_target="tpu_custom_call" | custom-call | tf_op jit(solution)/shard_map/pallas_call | solution.py:323
Async XLA Ops:
  1.3 13.1 %collective-permute-start = (bf16[160,512]{1,0:T(8,128)(2,1)S(1)}, bf16[160,512]{1,0:T(8,128)(2,1)S(1)}, u32[]{:S(2)}, u32[]{:S(2)}) collective-permute-start(bf16[160,512]{1,0:T(8,128)(2,1)S(1)} %get-tuple-element.20), channel_id=1, source_target_pairs={{0,1},{1,2},{2,3},{3,0},{4,5},{5,6},{6,7},{7,4},{8,9},{9,10},{10,1... | collective-permute-start | bytes 491528 | tf_op jit(solution)/shard_map/ppermute | solution.py:367
  4.4 10.0 %collective-permute-start.1 = (bf16[160,512]{1,0:T(8,128)(2,1)S(1)}, bf16[160,512]{1,0:T(8,128)(2,1)S(1)}, u32[]{:S(2)}, u32[]{:S(2)}) collective-permute-start(bf16[160,512]{1,0:T(8,128)(2,1)S(1)} %get-tuple-element.21), channel_id=1, source_target_pairs={{0,3},{1,0},{2,1},{3,2},{4,7},{5,4},{6,5},{7,6},{8,11},{9,8},{10,9... | collective-permute-start | bytes 491528 | tf_op jit(solution)/shard_map/ppermute | solution.py:368
  6.5 1.7 %copy-start = (bf16[8,48,512]{2,1,0:T(8,128)(2,1)S(1)}, bf16[8,48,512]{2,1,0:T(8,128)(2,1)}, u32[]{:S(2)}) copy-start(bf16[8,48,512]{2,1,0:T(8,128)(2,1)} %forcing.7) | copy-start | bytes 1179652
  6.5 1.7 %copy-start.1 = (f32[48,512]{1,0:T(8,128)S(1)}, f32[48,512]{1,0:T(8,128)}, u32[]{:S(2)}) copy-start(f32[48,512]{1,0:T(8,128)} %start.7) | copy-start | bytes 294916
  6.5 1.7 %copy-start.2 = (bf16[48,512]{1,0:T(8,128)(2,1)S(1)}, bf16[48,512]{1,0:T(8,128)(2,1)}, u32[]{:S(2)}) copy-start(bf16[48,512]{1,0:T(8,128)(2,1)} %velocity.7) | copy-start | bytes 147460
  6.5 1.7 %copy-start.3 = (bf16[48,512]{1,0:T(8,128)(2,1)S(1)}, bf16[48,512]{1,0:T(8,128)(2,1)}, u32[]{:S(2)}) copy-start(bf16[48,512]{1,0:T(8,128)(2,1)} %diffusion.7) | copy-start | bytes 147460
  10.5 6.3 %collective-permute-start.2 = (bf16[56,512]{1,0:T(8,128)(2,1)S(1)}, bf16[56,512]{1,0:T(8,128)(2,1)S(1)}, u32[]{:S(2)}, u32[]{:S(2)}) collective-permute-start(bf16[56,512]{1,0:T(8,128)(2,1)S(1)} %get-tuple-element.24), channel_id=1, source_target_pairs={{0,1},{1,2},{2,3},{3,0},{4,5},{5,6},{6,7},{7,4},{8,9},{9,10},{10,1... | collective-permute-start | bytes 172040 | tf_op jit(solution)/shard_map/ppermute | solution.py:383
  10.5 6.2 %collective-permute-start.3 = (bf16[56,512]{1,0:T(8,128)(2,1)S(1)}, bf16[56,512]{1,0:T(8,128)(2,1)S(1)}, u32[]{:S(2)}, u32[]{:S(2)}) collective-permute-start(bf16[56,512]{1,0:T(8,128)(2,1)S(1)} %get-tuple-element.25), channel_id=1, source_target_pairs={{0,3},{1,0},{2,1},{3,2},{4,7},{5,4},{6,5},{7,6},{8,11},{9,8},{10,9... | collective-permute-start | bytes 172040 | tf_op jit(solution)/shard_map/ppermute | solution.py:384
  38.3 6.2 %collective-permute-start.4 = (bf16[3,64,512]{2,1,0:T(8,128)(2,1)S(1)}, bf16[3,64,512]{2,1,0:T(8,128)(2,1)S(1)}, u32[]{:S(2)}, u32[]{:S(2)}) collective-permute-start(bf16[3,64,512]{2,1,0:T(8,128)(2,1)S(1)} %shard_map.70.psi), channel_id=1, source_target_pairs={{0,4},{4,0},{8,12},{12,8},{16,20},{20,16},{24,28},{28,24},{1,5},{5... | collective-permute-start | bytes 589832 | tf_op jit(solution)/shard_map/ppermute | solution.py:427
  38.8 5.8 %collective-permute-start.5 = (bf16[176,512]{1,0:T(8,128)(2,1)S(1)}, bf16[176,512]{1,0:T(8,128)(2,1)S(1)}, u32[]{:S(2)}, u32[]{:S(2)}) collective-permute-start(bf16[176,512]{1,0:T(8,128)(2,1)S(1)} %get-tuple-element.33), channel_id=1, source_target_pairs={{0,4},{4,8},{8,12},{12,16},{16,20},{20,24},{24,28},{28,0},{1,5},{5... | collective-permute-start | bytes 540680 | tf_op jit(solution)/shard_map/ppermute | solution.py:418

commit v8 on v7

--- a/solution.py
+++ b/solution.py
@@ -64,12 +64,14 @@
         self.keep = 3 * steps
         self.wide = 4 * steps
         self.groups = steps // 2
-        self.outer = steps * steps
+        self.half = steps - self.groups
+        self.late_rows = self.groups * steps
+        self.outer = self.half * steps
         self.velocity = self.outer + self.groups * steps
         self.diffusion = self.velocity + self.fine
         self.start = self.diffusion + self.fine
         self.start_low = self.start + self.fine
-        self.first_rows = self.start_low + self.fine
+        self.first_rows = self.start_low + steps
         self.sent = self.wide - steps
         self.far_velocity = self.sent
         self.far_diffusion = self.far_velocity + self.wide - self.fine
@@ -79,15 +81,18 @@
         return slice(width - inside, width + self.own + inside)
 
 
-def pack(lay, velocity, diffusion, forcing, start, head, tail, start_kept, outer_kept, semaphores):
+def pack(
+    lay, velocity, diffusion, forcing, start, head, tail, late_head, late_tail, start_kept, outer_kept, semaphores
+):
     steps, own, fine = lay.steps, lay.own, lay.fine
-    sides = ((head, 0, 0, steps), (tail, own - fine, own - steps, own - fine))
+    sides = ((head, late_head, 0, 0, steps), (tail, late_tail, own - fine, own - steps, own - fine))
     copies = [(start, start_kept)]
-    for side, (out, first, inner, outer) in enumerate(sides):
+    for side, (out, late, first, inner, outer) in enumerate(sides):
         near = pl.ds(first, fine)
         copies.append((forcing.at[:, pl.ds(outer, steps)], outer_kept.at[side]))
         for step in range(steps):
-            copies.append((forcing.at[step, pl.ds(inner, steps)], out.at[pl.ds(step * steps, steps)]))
+            target, at = (out, step) if step < lay.half else (late, step - lay.half)
+            copies.append((forcing.at[step, pl.ds(inner, steps)], target.at[pl.ds(at * steps, steps)]))
         copies.append((velocity.at[near], out.at[pl.ds(lay.velocity, fine)]))
         copies.append((diffusion.at[near], out.at[pl.ds(lay.diffusion, fine)]))
     copies = [pltpu.make_async_copy(*pair, semaphores.at[i]) for i, pair in enumerate(copies)]
@@ -95,10 +100,10 @@
         copy.start()
     for copy in copies:
         copy.wait()
-    for side, (out, first, _, _) in enumerate(sides):
+    for side, (out, _, first, _, _) in enumerate(sides):
         high, low = split(start_kept[first : first + fine])
         out[lay.start : lay.start_low] = high
-        out[lay.start_low : lay.first_rows] = low
+        out[lay.start_low : lay.first_rows] = low[:steps] if side == 0 else low[fine - steps :]
         for group in range(lay.groups):
             one = outer_kept[side, group].astype(F32)
             other = outer_kept[side, steps - 1 - group].astype(F32)
@@ -126,18 +131,14 @@
     return jnp.concatenate([low.astype(F32), own.astype(F32), high.astype(F32)], axis=0)
 
 
-def near_forcing(lay, low, own, high, step):
-    rows = slice(step * lay.steps, (step + 1) * lay.steps)
-    return joined(low[rows], own, high[rows])
-
-
-def near_start(lay, low, own, high):
-    def side(packed, at):
-        rows = slice(at, at + lay.steps)
-        shift = lay.start_low - lay.start
-        return packed[rows].astype(F32) + packed[rows.start + shift : rows.stop + shift].astype(F32)
-
-    return joined(side(low, lay.start + lay.fine - lay.steps), own, side(high, lay.start))
+def inner_rows(lay, packed, late, step):
+    source, at = (packed, step) if step < lay.half else (late, step - lay.half)
+    return source[at * lay.steps : (at + 1) * lay.steps].astype(F32)
+
+
+def start_rows(lay, packed, first):
+    at = lay.start + first
+    return packed[at : at + lay.steps].astype(F32) + packed[lay.start_low : lay.first_rows].astype(F32)
 
 
 def make_weights(moving, spread):
@@ -160,34 +161,52 @@
         out[lay.far_diffusion :] = diffusion[far]
 
 
-def edge_sweep(lay, place, low, high, forcing, velocity, diffusion, start, high_m, low_m, edges):
-    steps, own, fine = lay.steps, lay.own, lay.fine
-
-    def windows(before, ours, after):
-        return jnp.concatenate(
-            [part.astype(F32) for part in (before, ours[:fine], ours[own - fine :], after)], axis=0
-        )
+def edge_windows(lay, before, ours, after):
+    parts = (before, ours[: lay.fine], ours[lay.own - lay.fine :], after)
+    return jnp.concatenate([part.astype(F32) for part in parts], axis=0)
+
+
+def edge_steps(lay, current, steps_at, low, high, late_low, late_high, forcing, velocity, diffusion, high_m, low_m):
+    steps, fine = lay.steps, lay.fine
 
     def packed(ours, at):
-        return windows(low[at : at + fine], ours, high[at : at + fine])
+        return edge_windows(lay, low[at : at + fine], ours, high[at : at + fine])
 
     weights = make_weights(packed(velocity[...], lay.velocity), packed(diffusion[...], lay.diffusion))
-    current = packed(start[...], lay.start)
-    current = current + packed(jnp.zeros((own, start.shape[1]), F32), lay.start_low)
-    current = jnp.where(place[0] == 0, current, 0.0)
-    for step in range(steps):
-        rows = slice(step * steps, (step + 1) * steps)
+    for step in steps_at:
         group = min(step, steps - 1 - step)
         at = lay.outer + group * steps
         before, after = low[at : at + steps].astype(F32), high[at : at + steps].astype(F32)
         if step > group:
             before, after = turned(before, -group), turned(after, group)
-        source = windows(
-            jnp.concatenate([before, low[rows].astype(F32)], axis=0),
+        source = edge_windows(
+            lay,
+            jnp.concatenate([before, inner_rows(lay, low, late_low, step)], axis=0),
             forcing[step],
-            jnp.concatenate([high[rows].astype(F32), after], axis=0),
+            jnp.concatenate([inner_rows(lay, high, late_high, step), after], axis=0),
         )
         current = product3(stencil(current, weights) + source, high_m[...], low_m[...])
+    return current
+
+
+def early_edge_sweep(lay, place, low, high, forcing, velocity, diffusion, start, high_m, low_m, windows):
+    steps, fine = lay.steps, lay.fine
+    far = slice(lay.start, lay.start + steps)
+    before = jnp.concatenate([low[far].astype(F32), start_rows(lay, low, fine - steps)], axis=0)
+    far = slice(lay.start + fine - steps, lay.start + fine)
+    after = jnp.concatenate([start_rows(lay, high, 0), high[far].astype(F32)], axis=0)
+    current = edge_windows(lay, before, start[...], after)
+    current = jnp.where(place[0] == 0, current, 0.0)
+    operands = (low, high, None, None, forcing, velocity, diffusion, high_m, low_m)
+    windows[...] = edge_steps(lay, current, range(lay.half), *operands)
+
+
+def late_edge_sweep(
+    lay, windows, low, high, late_low, late_high, forcing, velocity, diffusion, high_m, low_m, edges
+):
+    steps, fine = lay.steps, lay.fine
+    operands = (low, high, late_low, late_high, forcing, velocity, diffusion, high_m, low_m)
+    current = edge_steps(lay, windows[...], range(lay.half, steps), *operands)
     edges[:fine] = current[steps : steps + fine]
     edges[fine:] = current[3 * steps + fine : 3 * steps + 2 * fine]
 
@@ -279,7 +298,7 @@
         psi[i] = current[i * rows : (i + 1) * rows][lay.centred(lay.fine, steps)].astype(BF16)
 
 
-def last_sweep(lay, place, psi, psi_other, passed, b_own, low, high, forcing, weights, start, high_m, low_m, coarse, out):
+def last_sweep(lay, place, psi, psi_other, passed, b_own, low, high, late_low, late_high, forcing, weights, start, high_m, low_m, coarse, out):
     steps, own = lay.steps, lay.own
     at = place[0]
     rows = own + 2 * steps
@@ -297,7 +316,7 @@
 
     error = lax.fori_loop(2, at - 1, turn, jnp.zeros((rows, start.shape[1]), F32))
     b_before = passed[:rows].astype(F32) + passed[rows : 2 * rows].astype(F32)
-    initial = near_start(lay, low, start[...], high)
+    initial = joined(start_rows(lay, low, lay.fine - steps), start[...], start_rows(lay, high, 0))
     current = jnp.where(at == 0, initial, b_before + error)
     mid = lay.centred(steps, 0)
     last = product(error[mid].astype(BF16), coarse[...])
@@ -305,7 +324,8 @@
     last = last + passed[2 * rows :].astype(F32)
     out[steps - 1] = b_own[...] + jnp.where(at == 0, 0.0, last)
     for step in range(steps - 1):
-        summed = stencil(current, narrow) + near_forcing(lay, low, forcing[step], high, step)
+        source = joined(inner_rows(lay, low, late_low, step), forcing[step], inner_rows(lay, high, late_high, step))
+        summed = stencil(current, narrow) + source
         current = product3(summed, high_m[...], low_m[...])
         out[step] = current[mid]
 
@@ -354,9 +374,10 @@
         return pltpu.VMEM(shape, dtype)
 
     first_pack = kept(lay.first_rows, columns, dtype=BF16)
-    head, tail = call_from_hbm(
+    late_pack = kept(lay.late_rows, columns, dtype=BF16)
+    head, tail, late_head, late_tail = call_from_hbm(
         functools.partial(pack, lay),
-        [first_pack] * 2,
+        [first_pack, first_pack, late_pack, late_pack],
         [
             pltpu.VMEM((own, columns), F32),
             pltpu.VMEM((2, steps, steps, columns), BF16),
@@ -364,8 +385,11 @@
         ],
         velocity, diffusion, forcing, initial_state,
     )
-    low = in_vmem(lax.ppermute(tail, "space", ring(slabs, 1)))
-    high = in_vmem(lax.ppermute(head, "space", ring(slabs, -1)))
+    low = lax.ppermute(tail, "space", ring(slabs, 1))
+    high = lax.ppermute(head, "space", ring(slabs, -1))
+    late_low = lax.ppermute(late_tail, "space", ring(slabs, 1))
+    late_high = lax.ppermute(late_head, "space", ring(slabs, -1))
+    low, high, late_low, late_high = in_vmem(low), in_vmem(high), in_vmem(late_low), in_vmem(late_high)
     high_m, low_m, coarse = call_from_hbm(
         split_matrices,
         [kept(*implicit.shape, dtype=BF16)] * 3,
@@ -382,11 +406,17 @@
     )
     far_low = in_vmem(lax.ppermute(tail, "space", ring(slabs, 1)))
     far_high = in_vmem(lax.ppermute(head, "space", ring(slabs, -1)))
+    windows = call(
+        early_edge_sweep,
+        lay,
+        kept(4 * lay.fine, columns),
+        place, low, high, forcing, velocity, diffusion, initial_state, high_m, low_m,
+    )
     edges = call(
-        edge_sweep,
+        late_edge_sweep,
         lay,
         kept(2 * lay.fine, columns),
-        place, low, high, forcing, velocity, diffusion, initial_state, high_m, low_m,
+        in_vmem(windows), low, high, late_low, late_high, forcing, velocity, diffusion, high_m, low_m,
     )
     rho, rho_low, a_near, weights = call(
         second_sweep,
@@ -432,7 +462,7 @@
         kernel,
         lay,
         jax.ShapeDtypeStruct((steps, own, columns), F32),
-        place, *sources, in_vmem(passed), in_vmem(b_own), low, high, forcing, weights, initial_state,
+        place, *sources, in_vmem(passed), in_vmem(b_own), low, high, late_low, late_high, forcing, weights, initial_state,
         high_m, low_m, coarse,
     )
 

time: 47.9 us -> 52.4 us (1.094)
  starting transfers between devices: 9.64 us -> 13.5 us
  waiting for transfers between devices: 5.68 us -> 6.33 us
    ppermute x2 -> x4, starting transfers between devices: 5.2 us -> 9.02 us  [the longest x1 3.82 us: per_device(): late_high = lax.ppermute(late_head, 'space', ring(slabs, -1))]
    ppermute x2 -> x4, waiting for transfers between devices: 0.01 us -> 0.66 us  [the longest x1 0.65 us: per_device(): late_low = lax.ppermute(late_tail, 'space', ring(slabs, 1))]
    pallas_call x6 -> x7, Pallas kernels: 18.7 us -> 18.7 us  [call(): pl.pallas_call(kernel if lay is None else functools.partial(kernel, lay),...]
  transfers between devices with their start and end apart: 6 -> 8, of which waited for: 1 -> 2; matrix products, arithmetic and copies ran while one was open for 0% -> 0% of each run, Pallas kernels for 13% -> 12%
where the time goes in v8:
time: 52.4 us; the launch traced here: 52.2 us
  Pallas kernels  21.7 us (41%)
  starting transfers between devices  13.5 us (26%)
  blocking collectives  10.6 us (20%)
  waiting for transfers between devices  6.33 us (12%)
    pallas_call x7, Pallas kernels, call(): pl.pallas_call(kernel if lay is None else functools.partial(kernel, lay),...  18.7 us
    all_gather x1, blocking collectives, per_device(): rho_all = lax.all_gather(rho, 'tm', axis=0)  10.6 us
    ppermute x1, waiting for transfers between devices, per_device(): passed = lax.ppermute(passed, 'tm', ring(blocks, 1))  5.66 us
    ppermute x1, starting transfers between devices, per_device(): late_high = lax.ppermute(late_head, 'space', ring(slabs, -1))  3.82 us
    ppermute x1, starting transfers between devices, per_device(): far_high = in_vmem(lax.ppermute(head, 'space', ring(slabs, -1)))  3.81 us
    ppermute x1, starting transfers between devices, per_device(): low = lax.ppermute(tail, 'space', ring(slabs, 1))  3.1 us
    pallas_call x2, Pallas kernels, call_from_hbm(): pl.pallas_call(kernel, out_shape=outs, in_specs=[pl.BlockSpec(memory_spac...  2.95 us
    ppermute x1, starting transfers between devices, per_device(): high = lax.ppermute(head, 'space', ring(slabs, -1))  2.09 us
  transfers between devices with their start and end apart: 8, of which 2 were waited for; matrix products, arithmetic and copies ran while one was open for 0% of the time, Pallas kernels for 12%

profile of v8, /device:TPU:0, one launch (start us, length us, event | category | flops | bytes accessed | tf_op | source)
XLA Modules:
  0.0 52.2 jit_solution(14483421377398425598)
XLA Ops:
  0.0 1.3 %shard_map.64 = (bf16[120,512]{1,0:T(8,128)(2,1)S(1)}, bf16[120,512]{1,0:T(8,128)(2,1)S(1)}, bf16[32,512]{1,0:T(8,128)(2,1)S(1)}, bf16[32,512]{1,0:T(8,128)(2,1)S(1)}) custom-call(bf16[48,512]{1,0:T(8,128)(2,1)} %velocity.9, bf16[48,512]{1,0:T(8,128)(2,1)} %diffusion.9, bf16[8,48,512]{2,1,0:T(8,128)(2,1)} %forcing.9, f32[48,512]{1,0:T(8,128)} %start.7), custom_call_target="tpu_custom_call" | custom-call | tf_op jit(solution)/shard_map/pallas_call | solution.py:354
  1.3 3.1 %collective-permute-start = (bf16[120,512]{1,0:T(8,128)(2,1)S(1)}, bf16[120,512]{1,0:T(8,128)(2,1)S(1)}, u32[]{:S(2)}, u32[]{:S(2)}) collective-permute-start(bf16[120,512]{1,0:T(8,128)(2,1)S(1)} %get-tuple-element.22), channel_id=1, source_target_pairs={{0,1},{1,2},{2,3},{3,0},{4,5},{5,6},{6,7},{7,4},{8,9},{9,10},{10,1... | collective-permute-start | bytes 368648 | tf_op jit(solution)/shard_map/ppermute | solution.py:388
  4.4 2.1 %collective-permute-start.1 = (bf16[120,512]{1,0:T(8,128)(2,1)S(1)}, bf16[120,512]{1,0:T(8,128)(2,1)S(1)}, u32[]{:S(2)}, u32[]{:S(2)}) collective-permute-start(bf16[120,512]{1,0:T(8,128)(2,1)S(1)} %get-tuple-element.23), channel_id=1, source_target_pairs={{0,3},{1,0},{2,1},{3,2},{4,7},{5,4},{6,5},{7,6},{8,11},{9,8},{10,9... | collective-permute-start | bytes 368648 | tf_op jit(solution)/shard_map/ppermute | solution.py:389
  6.5 0.0 copy-start
  6.5 0.0 copy-start.1
  6.5 1.7 %shard_map.65 = (bf16[512,512]{1,0:T(8,128)(2,1)S(1)}, bf16[512,512]{1,0:T(8,128)(2,1)S(1)}, bf16[512,512]{1,0:T(8,128)(2,1)S(1)}) custom-call(f32[512,512]{1,0:T(8,128)} %implicit.1, f32[512,512]{1,0:T(8,128)} %coarse_implicit.1), custom_call_target="tpu_custom_call" | custom-call | tf_op jit(solution)/shard_map/pallas_call | solution.py:354
  8.2 0.0 copy-done
  8.2 0.0 copy-done.1
  8.2 0.0 copy-done.2
  8.2 0.0 copy-done.3
  8.2 2.3 %shard_map.66 = (f32[48,512]{1,0:T(8,128)S(1)}, bf16[56,512]{1,0:T(8,128)(2,1)S(1)}, bf16[56,512]{1,0:T(8,128)(2,1)S(1)}) custom-call(s32[1]{0:T(128)} %bitcast.place, bf16[8,48,512]{2,1,0:T(8,128)(2,1)S(1)} %copy-done, bf16[48,512]{1,0:T(8,128)(2,1)S(1)} %copy-done.2, bf16[48,512]{1,0:T(8,128)(2,1)S(1)} %copy-done.3, f32[48,512]{1,0:T(8,128)S(1)} %copy-done.1, ...), custom_call_target="tpu_custom_call" | custom-call | tf_op jit(solution)/shard_map/pallas_call | solution.py:343
  10.5 0.1 collective-permute-start.2
  10.5 3.8 %collective-permute-start.3 = (bf16[56,512]{1,0:T(8,128)(2,1)S(1)}, bf16[56,512]{1,0:T(8,128)(2,1)S(1)}, u32[]{:S(2)}, u32[]{:S(2)}) collective-permute-start(bf16[56,512]{1,0:T(8,128)(2,1)S(1)} %get-tuple-element.27), channel_id=1, source_target_pairs={{0,3},{1,0},{2,1},{3,2},{4,7},{5,4},{6,5},{7,6},{8,11},{9,8},{10,9... | collective-permute-start | bytes 172040 | tf_op jit(solution)/shard_map/ppermute | solution.py:408
  14.4 0.0 collective-permute-start.4
  14.4 0.0 collective-permute-done.low
  14.4 3.8 %collective-permute-start.5 = (bf16[32,512]{1,0:T(8,128)(2,1)S(1)}, bf16[32,512]{1,0:T(8,128)(2,1)S(1)}, u32[]{:S(2)}, u32[]{:S(2)}) collective-permute-start(bf16[32,512]{1,0:T(8,128)(2,1)S(1)} %get-tuple-element.30), channel_id=1, source_target_pairs={{0,3},{1,0},{2,1},{3,2},{4,7},{5,4},{6,5},{7,6},{8,11},{9,8},{10,9... | collective-permute-start | bytes 98312 | tf_op jit(solution)/shard_map/ppermute | solution.py:391
  18.2 0.0 collective-permute-done.1.high
  18.2 1.2 %shard_map.67.windows = f32[64,512]{1,0:T(8,128)S(1)} custom-call(s32[1]{0:T(128)} %bitcast.place, bf16[120,512]{1,0:T(8,128)(2,1)S(1)} %collective-permute-done.low, bf16[120,512]{1,0:T(8,128)(2,1)S(1)} %collective-permute-done.1.high, bf16[8,48,512]{2,1,0:T(8,128)(2,1)S(1)} %copy-done, bf16[48,512]{1,0:T(8,128)(2,1)S(1)} %copy-done.2, ...), custom_call_target="tpu_custom_call" | custom-call | tf_op jit(solution)/shard_map/pallas_call | solution.py:343
  19.4 0.7 %collective-permute-done.4.late_low = bf16[32,512]{1,0:T(8,128)(2,1)S(1)} collective-permute-done((bf16[32,512]{1,0:T(8,128)(2,1)S(1)}, bf16[32,512]{1,0:T(8,128)(2,1)S(1)}, u32[]{:S(2)}, u32[]{:S(2)}) %collective-permute-start.4) | collective-permute-done | bytes 32800 | tf_op jit(solution)/shard_map/ppermute | solution.py:390
  20.1 0.0 collective-permute-done.5.late_high
  20.1 1.2 %shard_map.68.edges = f32[32,512]{1,0:T(8,128)S(1)} custom-call(f32[64,512]{1,0:T(8,128)S(1)} %shard_map.67.windows, bf16[120,512]{1,0:T(8,128)(2,1)S(1)} %collective-permute-done.low, bf16[120,512]{1,0:T(8,128)(2,1)S(1)} %collective-permute-done.1.high, bf16[32,512]{1,0:T(8,128)(2,1)S(1)} %collective-permute-done.4.late_low, ...), custom_call_target="tpu_custom_call" | custom-call | tf_op jit(solution)/shard_map/pallas_call | solution.py:343
  21.3 0.0 collective-permute-done.2.far_low
  21.3 0.0 collective-permute-done.3.far_high
  21.3 2.8 %shard_map.69 = (bf16[96,512]{1,0:T(8,128)(2,1)S(1)}, bf16[48,512]{1,0:T(8,128)(2,1)S(1)}, f32[64,512]{1,0:T(8,128)S(1)}, f32[3,112,512]{2,1,0:T(8,128)S(1)}) custom-call(bf16[120,512]{1,0:T(8,128)(2,1)S(1)} %collective-permute-done.low, bf16[120,512]{1,0:T(8,128)(2,1)S(1)} %collective-permute-done.1.high, ...), custom_call_target="tpu_custom_call" | custom-call | tf_op jit(solution)/shard_map/pallas_call | solution.py:343
  24.1 10.6 %all-gather = bf16[768,512]{1,0:T(8,128)(2,1)S(1)} all-gather(bf16[96,512]{1,0:T(8,128)(2,1)S(1)} %get-tuple-element.31), channel_id=2, replica_groups=mesh['tm'=8,'space'=4] {'tm'}, dimensions={0}, use_global_device_ids=true | all-gather | bytes 884736 | tf_op jit(solution)/shard_map/all_gather | solution.py:434
  34.7 6.0 %shard_map.70 = (f32[3,80,512]{2,1,0:T(8,128)S(1)}, bf16[176,512]{1,0:T(8,128)(2,1)S(1)}, f32[48,512]{1,0:T(8,128)S(1)}) custom-call(s32[1]{0:T(128)} %bitcast.place, bf16[8,96,512]{2,1,0:T(8,128)(2,1)S(1)} %bitcast.2, bf16[48,512]{1,0:T(8,128)(2,1)S(1)} %get-tuple-element.32.rho_low, f32[64,512]{1,0:T(8,128)S(1)} %get-tuple-element.33.a_near, ...), custom_call_target="tpu_custom_call" | custom-call | tf_op jit(solution)/shard_map/pallas_call | solution.py:343
  40.7 2.2 %shard_map.71.psi = bf16[3,64,512]{2,1,0:T(8,128)(2,1)S(1)} custom-call(f32[3,80,512]{2,1,0:T(8,128)S(1)} %get-tuple-element.36.change, f32[3,112,512]{2,1,0:T(8,128)S(1)} %get-tuple-element.34.weights, bf16[512,512]{1,0:T(8,128)(2,1)S(1)} %get-tuple-element.24.high_m), custom_call_target="tpu_custom_call" | custom-call | tf_op jit(solution)/shard_map/pallas_call | solution.py:343
  42.8 0.4 collective-permute-start.6
  43.3 0.2 collective-permute-start.7
  43.4 5.7 %collective-permute-done.7.passed = bf16[176,512]{1,0:T(8,128)(2,1)S(1)} collective-permute-done((bf16[176,512]{1,0:T(8,128)(2,1)S(1)}, bf16[176,512]{1,0:T(8,128)(2,1)S(1)}, u32[]{:S(2)}, u32[]{:S(2)}) %collective-permute-start.7) | collective-permute-done | bytes 180256 | tf_op jit(solution)/shard_map/ppermute | solution.py:448
  49.1 0.0 collective-permute-done.6.psi_other
  49.1 3.1 %shard_map.72 = f32[8,48,512]{2,1,0:T(8,128)} custom-call(s32[1]{0:T(128)} %bitcast.place, bf16[3,64,512]{2,1,0:T(8,128)(2,1)S(1)} %shard_map.71.psi, bf16[3,64,512]{2,1,0:T(8,128)(2,1)S(1)} %collective-permute-done.6.psi_other, bf16[176,512]{1,0:T(8,128)(2,1)S(1)} %collective-permute-done.7.passed, f32[48,512]{1,0:T(8,128)S(1)} %get-tuple-element.38.b_own, ...), custom_call_target="tpu_custom_call" | custom-call | tf_op jit(solution)/shard_map/pallas_call | solution.py:343
  (2 shorter events, 0.0 us)
Async XLA Ops:
  1.3 13.1 %collective-permute-start = (bf16[120,512]{1,0:T(8,128)(2,1)S(1)}, bf16[120,512]{1,0:T(8,128)(2,1)S(1)}, u32[]{:S(2)}, u32[]{:S(2)}) collective-permute-start(bf16[120,512]{1,0:T(8,128)(2,1)S(1)} %get-tuple-element.22), channel_id=1, source_target_pairs={{0,1},{1,2},{2,3},{3,0},{4,5},{5,6},{6,7},{7,4},{8,9},{9,10},{10,1... | collective-permute-start | bytes 368648 | tf_op jit(solution)/shard_map/ppermute | solution.py:388
  4.4 13.8 %collective-permute-start.1 = (bf16[120,512]{1,0:T(8,128)(2,1)S(1)}, bf16[120,512]{1,0:T(8,128)(2,1)S(1)}, u32[]{:S(2)}, u32[]{:S(2)}) collective-permute-start(bf16[120,512]{1,0:T(8,128)(2,1)S(1)} %get-tuple-element.23), channel_id=1, source_target_pairs={{0,3},{1,0},{2,1},{3,2},{4,7},{5,4},{6,5},{7,6},{8,11},{9,8},{10,9... | collective-permute-start | bytes 368648 | tf_op jit(solution)/shard_map/ppermute | solution.py:389
  6.5 1.7 %copy-start = (bf16[8,48,512]{2,1,0:T(8,128)(2,1)S(1)}, bf16[8,48,512]{2,1,0:T(8,128)(2,1)}, u32[]{:S(2)}) copy-start(bf16[8,48,512]{2,1,0:T(8,128)(2,1)} %forcing.9) | copy-start | bytes 1179652
  6.5 1.7 %copy-start.1 = (f32[48,512]{1,0:T(8,128)S(1)}, f32[48,512]{1,0:T(8,128)}, u32[]{:S(2)}) copy-start(f32[48,512]{1,0:T(8,128)} %start.7) | copy-start | bytes 294916
  6.5 1.7 %copy-start.2 = (bf16[48,512]{1,0:T(8,128)(2,1)S(1)}, bf16[48,512]{1,0:T(8,128)(2,1)}, u32[]{:S(2)}) copy-start(bf16[48,512]{1,0:T(8,128)(2,1)} %velocity.9) | copy-start | bytes 147460
  6.5 1.7 %copy-start.3 = (bf16[48,512]{1,0:T(8,128)(2,1)S(1)}, bf16[48,512]{1,0:T(8,128)(2,1)}, u32[]{:S(2)}) copy-start(bf16[48,512]{1,0:T(8,128)(2,1)} %diffusion.9) | copy-start | bytes 147460
  10.5 10.8 %collective-permute-start.2 = (bf16[56,512]{1,0:T(8,128)(2,1)S(1)}, bf16[56,512]{1,0:T(8,128)(2,1)S(1)}, u32[]{:S(2)}, u32[]{:S(2)}) collective-permute-start(bf16[56,512]{1,0:T(8,128)(2,1)S(1)} %get-tuple-element.26), channel_id=1, source_target_pairs={{0,1},{1,2},{2,3},{3,0},{4,5},{5,6},{6,7},{7,4},{8,9},{9,10},{10,1... | collective-permute-start | bytes 172040 | tf_op jit(solution)/shard_map/ppermute | solution.py:407
  10.5 10.8 %collective-permute-start.3 = (bf16[56,512]{1,0:T(8,128)(2,1)S(1)}, bf16[56,512]{1,0:T(8,128)(2,1)S(1)}, u32[]{:S(2)}, u32[]{:S(2)}) collective-permute-start(bf16[56,512]{1,0:T(8,128)(2,1)S(1)} %get-tuple-element.27), channel_id=1, source_target_pairs={{0,3},{1,0},{2,1},{3,2},{4,7},{5,4},{6,5},{7,6},{8,11},{9,8},{10,9... | collective-permute-start | bytes 172040 | tf_op jit(solution)/shard_map/ppermute | solution.py:408
  14.4 5.7 %collective-permute-start.4 = (bf16[32,512]{1,0:T(8,128)(2,1)S(1)}, bf16[32,512]{1,0:T(8,128)(2,1)S(1)}, u32[]{:S(2)}, u32[]{:S(2)}) collective-permute-start(bf16[32,512]{1,0:T(8,128)(2,1)S(1)} %get-tuple-element.29), channel_id=1, source_target_pairs={{0,1},{1,2},{2,3},{3,0},{4,5},{5,6},{6,7},{7,4},{8,9},{9,10},{10,1... | collective-permute-start | bytes 98312 | tf_op jit(solution)/shard_map/ppermute | solution.py:390
  14.4 5.7 %collective-permute-start.5 = (bf16[32,512]{1,0:T(8,128)(2,1)S(1)}, bf16[32,512]{1,0:T(8,128)(2,1)S(1)}, u32[]{:S(2)}, u32[]{:S(2)}) collective-permute-start(bf16[32,512]{1,0:T(8,128)(2,1)S(1)} %get-tuple-element.30), channel_id=1, source_target_pairs={{0,3},{1,0},{2,1},{3,2},{4,7},{5,4},{6,5},{7,6},{8,11},{9,8},{10,9... | collective-permute-start | bytes 98312 | tf_op jit(solution)/shard_map/ppermute | solution.py:391
  42.8 6.2 %collective-permute-start.6 = (bf16[3,64,512]{2,1,0:T(8,128)(2,1)S(1)}, bf16[3,64,512]{2,1,0:T(8,128)(2,1)S(1)}, u32[]{:S(2)}, u32[]{:S(2)}) collective-permute-start(bf16[3,64,512]{2,1,0:T(8,128)(2,1)S(1)} %shard_map.71.psi), channel_id=1, source_target_pairs={{0,4},{4,0},{8,12},{12,8},{16,20},{20,16},{24,28},{28,24},{1,5},{5... | collective-permute-start | bytes 589832 | tf_op jit(solution)/shard_map/ppermute | solution.py:457
  43.3 5.8 %collective-permute-start.7 = (bf16[176,512]{1,0:T(8,128)(2,1)S(1)}, bf16[176,512]{1,0:T(8,128)(2,1)S(1)}, u32[]{:S(2)}, u32[]{:S(2)}) collective-permute-start(bf16[176,512]{1,0:T(8,128)(2,1)S(1)} %get-tuple-element.37), channel_id=1, source_target_pairs={{0,4},{4,8},{8,12},{12,16},{16,20},{20,24},{24,28},{28,0},{1,5},{5... | collective-permute-start | bytes 540680 | tf_op jit(solution)/shard_map/ppermute | solution.py:448

commit v9 on v7

--- a/solution.py
+++ b/solution.py
@@ -69,7 +69,7 @@
         self.diffusion = self.velocity + self.fine
         self.start = self.diffusion + self.fine
         self.start_low = self.start + self.fine
-        self.first_rows = self.start_low + self.fine
+        self.first_rows = self.start_low + steps
         self.sent = self.wide - steps
         self.far_velocity = self.sent
         self.far_diffusion = self.far_velocity + self.wide - self.fine
@@ -98,7 +98,7 @@
     for side, (out, first, _, _) in enumerate(sides):
         high, low = split(start_kept[first : first + fine])
         out[lay.start : lay.start_low] = high
-        out[lay.start_low : lay.first_rows] = low
+        out[lay.start_low : lay.first_rows] = low[:steps] if side == 0 else low[fine - steps :]
         for group in range(lay.groups):
             one = outer_kept[side, group].astype(F32)
             other = outer_kept[side, steps - 1 - group].astype(F32)
@@ -131,13 +131,9 @@
     return joined(low[rows], own, high[rows])
 
 
-def near_start(lay, low, own, high):
-    def side(packed, at):
-        rows = slice(at, at + lay.steps)
-        shift = lay.start_low - lay.start
-        return packed[rows].astype(F32) + packed[rows.start + shift : rows.stop + shift].astype(F32)
-
-    return joined(side(low, lay.start + lay.fine - lay.steps), own, side(high, lay.start))
+def start_rows(lay, packed, first):
+    at = lay.start + first
+    return packed[at : at + lay.steps].astype(F32) + packed[lay.start_low : lay.first_rows].astype(F32)
 
 
 def make_weights(moving, spread):
@@ -172,8 +168,13 @@
         return windows(low[at : at + fine], ours, high[at : at + fine])
 
     weights = make_weights(packed(velocity[...], lay.velocity), packed(diffusion[...], lay.diffusion))
-    current = packed(start[...], lay.start)
-    current = current + packed(jnp.zeros((own, start.shape[1]), F32), lay.start_low)
+    far_before = low[lay.start : lay.start + steps].astype(F32)
+    far_after = high[lay.start + fine - steps : lay.start + fine].astype(F32)
+    current = windows(
+        jnp.concatenate([far_before, start_rows(lay, low, fine - steps)], axis=0),
+        start[...],
+        jnp.concatenate([start_rows(lay, high, 0), far_after], axis=0),
+    )
     current = jnp.where(place[0] == 0, current, 0.0)
     for step in range(steps):
         rows = slice(step * steps, (step + 1) * steps)
@@ -279,7 +280,7 @@
         psi[i] = current[i * rows : (i + 1) * rows][lay.centred(lay.fine, steps)].astype(BF16)
 
 
-def last_sweep(lay, place, psi, psi_other, passed, b_own, low, high, forcing, weights, start, high_m, low_m, coarse, out):
+def last_sweep(lay, place, psi, psi_other, passed, b_own, low, high, forcing, weights, start, high_m, low_m, coarse, out, out_kept, semaphores):
     steps, own = lay.steps, lay.own
     at = place[0]
     rows = own + 2 * steps
@@ -297,17 +298,22 @@
 
     error = lax.fori_loop(2, at - 1, turn, jnp.zeros((rows, start.shape[1]), F32))
     b_before = passed[:rows].astype(F32) + passed[rows : 2 * rows].astype(F32)
-    initial = near_start(lay, low, start[...], high)
+    initial = joined(start_rows(lay, low, lay.fine - steps), start[...], start_rows(lay, high, 0))
     current = jnp.where(at == 0, initial, b_before + error)
     mid = lay.centred(steps, 0)
     last = product(error[mid].astype(BF16), coarse[...])
     last = last + jnp.where(at >= 3, source(jnp.maximum(at - 1, 2))[mid], 0.0)
     last = last + passed[2 * rows :].astype(F32)
-    out[steps - 1] = b_own[...] + jnp.where(at == 0, 0.0, last)
+    copies = [pltpu.make_async_copy(out_kept.at[step], out.at[step], semaphores.at[step]) for step in range(steps)]
+    out_kept[steps - 1] = b_own[...] + jnp.where(at == 0, 0.0, last)
+    copies[steps - 1].start()
     for step in range(steps - 1):
         summed = stencil(current, narrow) + near_forcing(lay, low, forcing[step], high, step)
         current = product3(summed, high_m[...], low_m[...])
-        out[step] = current[mid]
+        out_kept[step] = current[mid]
+        copies[step].start()
+    for copy in copies:
+        copy.wait()
 
 
 def last_sweep_gathered(lay, place, psi, *rest):
@@ -428,13 +434,20 @@
         sources, kernel = (in_vmem(psi), in_vmem(psi_other)), last_sweep
     else:
         sources, kernel = (lax.all_gather(psi[0], "tm", axis=0),), last_sweep_gathered
-    return call(
-        kernel,
-        lay,
-        jax.ShapeDtypeStruct((steps, own, columns), F32),
+    operands = (
         place, *sources, in_vmem(passed), in_vmem(b_own), low, high, forcing, weights, initial_state,
         high_m, low_m, coarse,
     )
+    return pl.pallas_call(
+        functools.partial(kernel, lay),
+        out_shape=jax.ShapeDtypeStruct((steps, own, columns), F32),
+        in_specs=[pl.BlockSpec(memory_space=pltpu.SMEM)]
+        + [pl.BlockSpec(memory_space=pltpu.VMEM)] * (len(operands) - 1),
+        out_specs=pl.BlockSpec(memory_space=pltpu.HBM),
+        scratch_shapes=[pltpu.VMEM((steps, own, columns), F32), pltpu.SemaphoreType.DMA((steps,))],
+        compiler_params=pltpu.CompilerParams(vmem_limit_bytes=LIMIT),
+        name="last_sweep",
+    )(*operands)
 
 
 def solution(mesh):

time: 47.9 us -> 47.7 us (level)
    pallas_call x6 -> x5, Pallas kernels: 18.7 us -> 15.6 us  [call(): pl.pallas_call(kernel if lay is None else functools.partial(kernel, lay),...]
    pallas_call x0 -> x1, Pallas kernels: none -> 2.94 us  [per_device(): pl.pallas_call(functools.partial(kernel, lay), out_shape=jax.ShapeDtypeSt...]
where the time goes in v9:
time: 47.7 us; the launch traced here: 47.5 us
  Pallas kernels  21.5 us (45%)
  blocking collectives  10.6 us (22%)
  starting transfers between devices  9.64 us (20%)
  waiting for transfers between devices  5.67 us (12%)
    pallas_call x5, Pallas kernels, call(): pl.pallas_call(kernel if lay is None else functools.partial(kernel, lay),...  15.6 us
    all_gather x1, blocking collectives, per_device(): rho_all = lax.all_gather(rho, 'tm', axis=0)  10.6 us
    ppermute x1, waiting for transfers between devices, per_device(): passed = lax.ppermute(passed, 'tm', ring(blocks, 1))  5.66 us
    ppermute x1, starting transfers between devices, per_device(): far_high = in_vmem(lax.ppermute(head, 'space', ring(slabs, -1)))  3.81 us
    ppermute x1, starting transfers between devices, per_device(): low = in_vmem(lax.ppermute(tail, 'space', ring(slabs, 1)))  3.1 us
    pallas_call x2, Pallas kernels, call_from_hbm(): pl.pallas_call(kernel, out_shape=outs, in_specs=[pl.BlockSpec(memory_spac...  2.95 us
    pallas_call x1, Pallas kernels, per_device(): pl.pallas_call(functools.partial(kernel, lay), out_shape=jax.ShapeDtypeSt...  2.94 us
    ppermute x1, starting transfers between devices, per_device(): high = in_vmem(lax.ppermute(head, 'space', ring(slabs, -1)))  2.09 us
  transfers between devices with their start and end apart: 6, of which 1 were waited for; matrix products, arithmetic and copies ran while one was open for 0% of the time, Pallas kernels for 13%

profile of v9, /device:TPU:0, one launch (start us, length us, event | category | flops | bytes accessed | tf_op | source)
XLA Modules:
  0.0 47.5 jit_solution(12611792094567681385)
XLA Ops:
  0.0 1.3 %shard_map.64 = (bf16[152,512]{1,0:T(8,128)(2,1)S(1)}, bf16[152,512]{1,0:T(8,128)(2,1)S(1)}) custom-call(bf16[48,512]{1,0:T(8,128)(2,1)} %velocity.7, bf16[48,512]{1,0:T(8,128)(2,1)} %diffusion.7, bf16[8,48,512]{2,1,0:T(8,128)(2,1)} %forcing.7, f32[48,512]{1,0:T(8,128)} %start.7), custom_call_target="tpu_custom_call" | custom-call | tf_op jit(solution)/shard_map/pallas_call | solution.py:340
  1.3 3.1 %collective-permute-start = (bf16[152,512]{1,0:T(8,128)(2,1)S(1)}, bf16[152,512]{1,0:T(8,128)(2,1)S(1)}, u32[]{:S(2)}, u32[]{:S(2)}) collective-permute-start(bf16[152,512]{1,0:T(8,128)(2,1)S(1)} %get-tuple-element.20), channel_id=1, source_target_pairs={{0,1},{1,2},{2,3},{3,0},{4,5},{5,6},{6,7},{7,4},{8,9},{9,10},{10,1... | collective-permute-start | bytes 466952 | tf_op jit(solution)/shard_map/ppermute | solution.py:373
  4.4 2.1 %collective-permute-start.1 = (bf16[152,512]{1,0:T(8,128)(2,1)S(1)}, bf16[152,512]{1,0:T(8,128)(2,1)S(1)}, u32[]{:S(2)}, u32[]{:S(2)}) collective-permute-start(bf16[152,512]{1,0:T(8,128)(2,1)S(1)} %get-tuple-element.21), channel_id=1, source_target_pairs={{0,3},{1,0},{2,1},{3,2},{4,7},{5,4},{6,5},{7,6},{8,11},{9,8},{10,9... | collective-permute-start | bytes 466952 | tf_op jit(solution)/shard_map/ppermute | solution.py:374
  6.5 0.0 copy-start
  6.5 0.0 copy-start.1
  6.5 0.0 copy-start.2
  6.5 0.0 copy-start.3
  6.5 1.7 %shard_map.65 = (bf16[512,512]{1,0:T(8,128)(2,1)S(1)}, bf16[512,512]{1,0:T(8,128)(2,1)S(1)}, bf16[512,512]{1,0:T(8,128)(2,1)S(1)}) custom-call(f32[512,512]{1,0:T(8,128)} %implicit.1, f32[512,512]{1,0:T(8,128)} %coarse_implicit.1), custom_call_target="tpu_custom_call" | custom-call | tf_op jit(solution)/shard_map/pallas_call | solution.py:340
  8.2 0.0 copy-done
  8.2 0.0 copy-done.1
  8.2 0.0 copy-done.2
  8.2 0.0 copy-done.3
  8.2 2.3 %shard_map.66 = (f32[48,512]{1,0:T(8,128)S(1)}, bf16[56,512]{1,0:T(8,128)(2,1)S(1)}, bf16[56,512]{1,0:T(8,128)(2,1)S(1)}) custom-call(s32[1]{0:T(128)} %bitcast.place, bf16[8,48,512]{2,1,0:T(8,128)(2,1)S(1)} %copy-done, bf16[48,512]{1,0:T(8,128)(2,1)S(1)} %copy-done.2, bf16[48,512]{1,0:T(8,128)(2,1)S(1)} %copy-done.3, f32[48,512]{1,0:T(8,128)S(1)} %copy-done.1, ...), custom_call_target="tpu_custom_call" | custom-call | tf_op jit(solution)/shard_map/pallas_call | solution.py:329
  10.5 0.1 collective-permute-start.2
  10.5 3.8 %collective-permute-start.3 = (bf16[56,512]{1,0:T(8,128)(2,1)S(1)}, bf16[56,512]{1,0:T(8,128)(2,1)S(1)}, u32[]{:S(2)}, u32[]{:S(2)}) collective-permute-start(bf16[56,512]{1,0:T(8,128)(2,1)S(1)} %get-tuple-element.25), channel_id=1, source_target_pairs={{0,3},{1,0},{2,1},{3,2},{4,7},{5,4},{6,5},{7,6},{8,11},{9,8},{10,9... | collective-permute-start | bytes 172040 | tf_op jit(solution)/shard_map/ppermute | solution.py:390
  14.4 0.0 collective-permute-done.low
  14.4 0.0 collective-permute-done.1.high
  14.4 2.4 %shard_map.67.edges = f32[32,512]{1,0:T(8,128)S(1)} custom-call(s32[1]{0:T(128)} %bitcast.place, bf16[152,512]{1,0:T(8,128)(2,1)S(1)} %collective-permute-done.low, bf16[152,512]{1,0:T(8,128)(2,1)S(1)} %collective-permute-done.1.high, bf16[8,48,512]{2,1,0:T(8,128)(2,1)S(1)} %copy-done, bf16[48,512]{1,0:T(8,128)(2,1)S(1)} %copy-done.2, ...), custom_call_target="tpu_custom_call" | custom-call | tf_op jit(solution)/shard_map/pallas_call | solution.py:329
  16.8 0.0 collective-permute-done.2.far_low
  16.8 0.0 collective-permute-done.3.far_high
  16.8 2.8 %shard_map.68 = (bf16[96,512]{1,0:T(8,128)(2,1)S(1)}, bf16[48,512]{1,0:T(8,128)(2,1)S(1)}, f32[64,512]{1,0:T(8,128)S(1)}, f32[3,112,512]{2,1,0:T(8,128)S(1)}) custom-call(bf16[152,512]{1,0:T(8,128)(2,1)S(1)} %collective-permute-done.low, bf16[152,512]{1,0:T(8,128)(2,1)S(1)} %collective-permute-done.1.high, ...), custom_call_target="tpu_custom_call" | custom-call | tf_op jit(solution)/shard_map/pallas_call | solution.py:329
  19.6 10.6 %all-gather = bf16[768,512]{1,0:T(8,128)(2,1)S(1)} all-gather(bf16[96,512]{1,0:T(8,128)(2,1)S(1)} %get-tuple-element.27), channel_id=2, replica_groups=mesh['tm'=8,'space'=4] {'tm'}, dimensions={0}, use_global_device_ids=true | all-gather | bytes 884736 | tf_op jit(solution)/shard_map/all_gather | solution.py:410
  30.2 6.0 %shard_map.69 = (f32[3,80,512]{2,1,0:T(8,128)S(1)}, bf16[176,512]{1,0:T(8,128)(2,1)S(1)}, f32[48,512]{1,0:T(8,128)S(1)}) custom-call(s32[1]{0:T(128)} %bitcast.place, bf16[8,96,512]{2,1,0:T(8,128)(2,1)S(1)} %bitcast.2, bf16[48,512]{1,0:T(8,128)(2,1)S(1)} %get-tuple-element.28.rho_low, f32[64,512]{1,0:T(8,128)S(1)} %get-tuple-element.29.a_near, ...), custom_call_target="tpu_custom_call" | custom-call | tf_op jit(solution)/shard_map/pallas_call | solution.py:329
  36.2 2.2 %shard_map.70.psi = bf16[3,64,512]{2,1,0:T(8,128)(2,1)S(1)} custom-call(f32[3,80,512]{2,1,0:T(8,128)S(1)} %get-tuple-element.32.change, f32[3,112,512]{2,1,0:T(8,128)S(1)} %get-tuple-element.30.weights, bf16[512,512]{1,0:T(8,128)(2,1)S(1)} %get-tuple-element.22.high_m), custom_call_target="tpu_custom_call" | custom-call | tf_op jit(solution)/shard_map/pallas_call | solution.py:329
  38.3 0.4 collective-permute-start.4
  38.7 0.2 collective-permute-start.5
  38.9 5.7 %collective-permute-done.5.passed = bf16[176,512]{1,0:T(8,128)(2,1)S(1)} collective-permute-done((bf16[176,512]{1,0:T(8,128)(2,1)S(1)}, bf16[176,512]{1,0:T(8,128)(2,1)S(1)}, u32[]{:S(2)}, u32[]{:S(2)}) %collective-permute-start.5) | collective-permute-done | bytes 180256 | tf_op jit(solution)/shard_map/ppermute | solution.py:424
  44.6 0.0 collective-permute-done.4.psi_other
  44.6 2.9 %last_sweep.1 = f32[8,48,512]{2,1,0:T(8,128)} custom-call(s32[1]{0:T(128)} %bitcast.place, bf16[3,64,512]{2,1,0:T(8,128)(2,1)S(1)} %shard_map.70.psi, bf16[3,64,512]{2,1,0:T(8,128)(2,1)S(1)} %collective-permute-done.4.psi_other, bf16[176,512]{1,0:T(8,128)(2,1)S(1)} %collective-permute-done.5.passed, f32[48,512]{1,0:T(8,128)S(1)} %get-tuple-element.34.b_own, ...), custom_call_target="tpu_custom_call" | custom-call | tf_op jit(solution)/shard_map/last_sweep/pallas_call | solution.py:441
Async XLA Ops:
  1.3 13.1 %collective-permute-start = (bf16[152,512]{1,0:T(8,128)(2,1)S(1)}, bf16[152,512]{1,0:T(8,128)(2,1)S(1)}, u32[]{:S(2)}, u32[]{:S(2)}) collective-permute-start(bf16[152,512]{1,0:T(8,128)(2,1)S(1)} %get-tuple-element.20), channel_id=1, source_target_pairs={{0,1},{1,2},{2,3},{3,0},{4,5},{5,6},{6,7},{7,4},{8,9},{9,10},{10,1... | collective-permute-start | bytes 466952 | tf_op jit(solution)/shard_map/ppermute | solution.py:373
  4.4 10.0 %collective-permute-start.1 = (bf16[152,512]{1,0:T(8,128)(2,1)S(1)}, bf16[152,512]{1,0:T(8,128)(2,1)S(1)}, u32[]{:S(2)}, u32[]{:S(2)}) collective-permute-start(bf16[152,512]{1,0:T(8,128)(2,1)S(1)} %get-tuple-element.21), channel_id=1, source_target_pairs={{0,3},{1,0},{2,1},{3,2},{4,7},{5,4},{6,5},{7,6},{8,11},{9,8},{10,9... | collective-permute-start | bytes 466952 | tf_op jit(solution)/shard_map/ppermute | solution.py:374
  6.5 1.7 %copy-start = (bf16[8,48,512]{2,1,0:T(8,128)(2,1)S(1)}, bf16[8,48,512]{2,1,0:T(8,128)(2,1)}, u32[]{:S(2)}) copy-start(bf16[8,48,512]{2,1,0:T(8,128)(2,1)} %forcing.7) | copy-start | bytes 1179652
  6.5 1.7 %copy-start.1 = (f32[48,512]{1,0:T(8,128)S(1)}, f32[48,512]{1,0:T(8,128)}, u32[]{:S(2)}) copy-start(f32[48,512]{1,0:T(8,128)} %start.7) | copy-start | bytes 294916
  6.5 1.7 %copy-start.2 = (bf16[48,512]{1,0:T(8,128)(2,1)S(1)}, bf16[48,512]{1,0:T(8,128)(2,1)}, u32[]{:S(2)}) copy-start(bf16[48,512]{1,0:T(8,128)(2,1)} %velocity.7) | copy-start | bytes 147460
  6.5 1.7 %copy-start.3 = (bf16[48,512]{1,0:T(8,128)(2,1)S(1)}, bf16[48,512]{1,0:T(8,128)(2,1)}, u32[]{:S(2)}) copy-start(bf16[48,512]{1,0:T(8,128)(2,1)} %diffusion.7) | copy-start | bytes 147460
  10.5 6.3 %collective-permute-start.2 = (bf16[56,512]{1,0:T(8,128)(2,1)S(1)}, bf16[56,512]{1,0:T(8,128)(2,1)S(1)}, u32[]{:S(2)}, u32[]{:S(2)}) collective-permute-start(bf16[56,512]{1,0:T(8,128)(2,1)S(1)} %get-tuple-element.24), channel_id=1, source_target_pairs={{0,1},{1,2},{2,3},{3,0},{4,5},{5,6},{6,7},{7,4},{8,9},{9,10},{10,1... | collective-permute-start | bytes 172040 | tf_op jit(solution)/shard_map/ppermute | solution.py:389
  10.5 6.2 %collective-permute-start.3 = (bf16[56,512]{1,0:T(8,128)(2,1)S(1)}, bf16[56,512]{1,0:T(8,128)(2,1)S(1)}, u32[]{:S(2)}, u32[]{:S(2)}) collective-permute-start(bf16[56,512]{1,0:T(8,128)(2,1)S(1)} %get-tuple-element.25), channel_id=1, source_target_pairs={{0,3},{1,0},{2,1},{3,2},{4,7},{5,4},{6,5},{7,6},{8,11},{9,8},{10,9... | collective-permute-start | bytes 172040 | tf_op jit(solution)/shard_map/ppermute | solution.py:390
  38.3 6.2 %collective-permute-start.4 = (bf16[3,64,512]{2,1,0:T(8,128)(2,1)S(1)}, bf16[3,64,512]{2,1,0:T(8,128)(2,1)S(1)}, u32[]{:S(2)}, u32[]{:S(2)}) collective-permute-start(bf16[3,64,512]{2,1,0:T(8,128)(2,1)S(1)} %shard_map.70.psi), channel_id=1, source_target_pairs={{0,4},{4,0},{8,12},{12,8},{16,20},{20,16},{24,28},{28,24},{1,5},{5... | collective-permute-start | bytes 589832 | tf_op jit(solution)/shard_map/ppermute | solution.py:433
  38.7 5.8 %collective-permute-start.5 = (bf16[176,512]{1,0:T(8,128)(2,1)S(1)}, bf16[176,512]{1,0:T(8,128)(2,1)S(1)}, u32[]{:S(2)}, u32[]{:S(2)}) collective-permute-start(bf16[176,512]{1,0:T(8,128)(2,1)S(1)} %get-tuple-element.33), channel_id=1, source_target_pairs={{0,4},{4,8},{8,12},{12,16},{16,20},{20,24},{24,28},{28,0},{1,5},{5... | collective-permute-start | bytes 540680 | tf_op jit(solution)/shard_map/ppermute | solution.py:424

commit v10 on v9

--- a/solution.py
+++ b/solution.py
@@ -86,8 +86,8 @@
     for side, (out, first, inner, outer) in enumerate(sides):
         near = pl.ds(first, fine)
         copies.append((forcing.at[:, pl.ds(outer, steps)], outer_kept.at[side]))
-        for step in range(steps):
-            copies.append((forcing.at[step, pl.ds(inner, steps)], out.at[pl.ds(step * steps, steps)]))
+        target = out.at[pl.ds(0, steps * steps)].reshape(steps, steps, out.shape[1])
+        copies.append((forcing.at[:, pl.ds(inner, steps)], target))
         copies.append((velocity.at[near], out.at[pl.ds(lay.velocity, fine)]))
         copies.append((diffusion.at[near], out.at[pl.ds(lay.diffusion, fine)]))
     copies = [pltpu.make_async_copy(*pair, semaphores.at[i]) for i, pair in enumerate(copies)]
@@ -366,7 +366,7 @@
         [
             pltpu.VMEM((own, columns), F32),
             pltpu.VMEM((2, steps, steps, columns), BF16),
-            pltpu.SemaphoreType.DMA((1 + 2 * (steps + 3),)),
+            pltpu.SemaphoreType.DMA((1 + 2 * 4,)),
         ],
         velocity, diffusion, forcing, initial_state,
     )
@@ -421,7 +421,7 @@
         place, rho_all, in_vmem(rho_low), in_vmem(a_near), weights, high_m, low_m, coarse,
         field=count * (own + 2 * lay.keep),
     )
-    passed = lax.ppermute(passed, "tm", ring(blocks, 1))
+    passed = lax.ppermute(passed, "tm", ring(blocks, 1)[:-1])
     psi = call(
         fourth_sweep,
         lay,

time: 47.7 us -> 48.2 us (1.010)
  the two profiles are of different devices: /device:TPU:0 before, /device:TPU:4 now
where the time goes in v10:
time: 48.2 us; the launch traced here: 48 us
  Pallas kernels  21.6 us (45%)
  blocking collectives  10.4 us (22%)
  starting transfers between devices  10.2 us (21%)
  waiting for transfers between devices  5.66 us (12%)
    pallas_call x5, Pallas kernels, call(): pl.pallas_call(kernel if lay is None else functools.partial(kernel, lay),...  15.6 us
    all_gather x1, blocking collectives, per_device(): rho_all = lax.all_gather(rho, 'tm', axis=0)  10.4 us
    ppermute x1, waiting for transfers between devices, per_device(): passed = lax.ppermute(passed, 'tm', ring(blocks, 1)[:-1])  5.64 us
    ppermute x1, starting transfers between devices, per_device(): far_high = in_vmem(lax.ppermute(head, 'space', ring(slabs, -1)))  3.81 us
    pallas_call x1, Pallas kernels, per_device(): pl.pallas_call(functools.partial(kernel, lay), out_shape=jax.ShapeDtypeSt...  3.17 us
    pallas_call x2, Pallas kernels, call_from_hbm(): pl.pallas_call(kernel, out_shape=outs, in_specs=[pl.BlockSpec(memory_spac...  2.79 us
    ppermute x1, starting transfers between devices, per_device(): high = in_vmem(lax.ppermute(head, 'space', ring(slabs, -1)))  2.25 us
    ppermute x1, starting transfers between devices, per_device(): passed = lax.ppermute(passed, 'tm', ring(blocks, 1)[:-1])  2.05 us
  transfers between devices with their start and end apart: 6, of which 1 were waited for; matrix products, arithmetic and copies ran while one was open for 0% of the time, Pallas kernels for 13%

profile of v10, /device:TPU:4, one launch (start us, length us, event | category | flops | bytes accessed | tf_op | source)
XLA Modules:
  0.0 48.0 jit_solution(14006398907422754567)
XLA Ops:
  0.0 1.1 %shard_map.64 = (bf16[152,512]{1,0:T(8,128)(2,1)S(1)}, bf16[152,512]{1,0:T(8,128)(2,1)S(1)}) custom-call(bf16[48,512]{1,0:T(8,128)(2,1)} %velocity.7, bf16[48,512]{1,0:T(8,128)(2,1)} %diffusion.7, bf16[8,48,512]{2,1,0:T(8,128)(2,1)} %forcing.7, f32[48,512]{1,0:T(8,128)} %start.7), custom_call_target="tpu_custom_call" | custom-call | tf_op jit(solution)/shard_map/pallas_call | solution.py:340
  1.1 1.6 %collective-permute-start = (bf16[152,512]{1,0:T(8,128)(2,1)S(1)}, bf16[152,512]{1,0:T(8,128)(2,1)S(1)}, u32[]{:S(2)}, u32[]{:S(2)}) collective-permute-start(bf16[152,512]{1,0:T(8,128)(2,1)S(1)} %get-tuple-element.20), channel_id=1, source_target_pairs={{0,1},{1,2},{2,3},{3,0},{4,5},{5,6},{6,7},{7,4},{8,9},{9,10},{10,1... | collective-permute-start | bytes 466952 | tf_op jit(solution)/shard_map/ppermute | solution.py:373
  2.8 2.2 %collective-permute-start.1 = (bf16[152,512]{1,0:T(8,128)(2,1)S(1)}, bf16[152,512]{1,0:T(8,128)(2,1)S(1)}, u32[]{:S(2)}, u32[]{:S(2)}) collective-permute-start(bf16[152,512]{1,0:T(8,128)(2,1)S(1)} %get-tuple-element.21), channel_id=1, source_target_pairs={{0,3},{1,0},{2,1},{3,2},{4,7},{5,4},{6,5},{7,6},{8,11},{9,8},{10,9... | collective-permute-start | bytes 466952 | tf_op jit(solution)/shard_map/ppermute | solution.py:374
  5.0 0.0 copy-start
  5.0 0.0 copy-start.1
  5.0 0.0 copy-start.2
  5.0 0.0 copy-start.3
  5.0 1.7 %shard_map.65 = (bf16[512,512]{1,0:T(8,128)(2,1)S(1)}, bf16[512,512]{1,0:T(8,128)(2,1)S(1)}, bf16[512,512]{1,0:T(8,128)(2,1)S(1)}) custom-call(f32[512,512]{1,0:T(8,128)} %implicit.1, f32[512,512]{1,0:T(8,128)} %coarse_implicit.1), custom_call_target="tpu_custom_call" | custom-call | tf_op jit(solution)/shard_map/pallas_call | solution.py:340
  6.7 0.0 copy-done
  6.7 0.0 copy-done.1
  6.7 0.0 copy-done.2
  6.7 0.0 copy-done.3
  6.7 2.3 %shard_map.66 = (f32[48,512]{1,0:T(8,128)S(1)}, bf16[56,512]{1,0:T(8,128)(2,1)S(1)}, bf16[56,512]{1,0:T(8,128)(2,1)S(1)}) custom-call(s32[1]{0:T(128)} %bitcast.place, bf16[8,48,512]{2,1,0:T(8,128)(2,1)S(1)} %copy-done, bf16[48,512]{1,0:T(8,128)(2,1)S(1)} %copy-done.2, bf16[48,512]{1,0:T(8,128)(2,1)S(1)} %copy-done.3, f32[48,512]{1,0:T(8,128)S(1)} %copy-done.1, ...), custom_call_target="tpu_custom_call" | custom-call | tf_op jit(solution)/shard_map/pallas_call | solution.py:329
  9.0 0.1 collective-permute-start.2
  9.1 3.8 %collective-permute-start.3 = (bf16[56,512]{1,0:T(8,128)(2,1)S(1)}, bf16[56,512]{1,0:T(8,128)(2,1)S(1)}, u32[]{:S(2)}, u32[]{:S(2)}) collective-permute-start(bf16[56,512]{1,0:T(8,128)(2,1)S(1)} %get-tuple-element.25), channel_id=1, source_target_pairs={{0,3},{1,0},{2,1},{3,2},{4,7},{5,4},{6,5},{7,6},{8,11},{9,8},{10,9... | collective-permute-start | bytes 172040 | tf_op jit(solution)/shard_map/ppermute | solution.py:390
  12.9 0.0 collective-permute-done.low
  12.9 0.0 collective-permute-done.1.high
  12.9 2.4 %shard_map.67.edges = f32[32,512]{1,0:T(8,128)S(1)} custom-call(s32[1]{0:T(128)} %bitcast.place, bf16[152,512]{1,0:T(8,128)(2,1)S(1)} %collective-permute-done.low, bf16[152,512]{1,0:T(8,128)(2,1)S(1)} %collective-permute-done.1.high, bf16[8,48,512]{2,1,0:T(8,128)(2,1)S(1)} %copy-done, bf16[48,512]{1,0:T(8,128)(2,1)S(1)} %copy-done.2, ...), custom_call_target="tpu_custom_call" | custom-call | tf_op jit(solution)/shard_map/pallas_call | solution.py:329
  15.3 0.0 collective-permute-done.2.far_low
  15.3 0.0 collective-permute-done.3.far_high
  15.3 2.8 %shard_map.68 = (bf16[96,512]{1,0:T(8,128)(2,1)S(1)}, bf16[48,512]{1,0:T(8,128)(2,1)S(1)}, f32[64,512]{1,0:T(8,128)S(1)}, f32[3,112,512]{2,1,0:T(8,128)S(1)}) custom-call(bf16[152,512]{1,0:T(8,128)(2,1)S(1)} %collective-permute-done.low, bf16[152,512]{1,0:T(8,128)(2,1)S(1)} %collective-permute-done.1.high, ...), custom_call_target="tpu_custom_call" | custom-call | tf_op jit(solution)/shard_map/pallas_call | solution.py:329
  18.1 10.4 %all-gather = bf16[768,512]{1,0:T(8,128)(2,1)S(1)} all-gather(bf16[96,512]{1,0:T(8,128)(2,1)S(1)} %get-tuple-element.27), channel_id=2, replica_groups=mesh['tm'=8,'space'=4] {'tm'}, dimensions={0}, use_global_device_ids=true | all-gather | bytes 884736 | tf_op jit(solution)/shard_map/all_gather | solution.py:410
  28.5 6.0 %shard_map.69 = (f32[3,80,512]{2,1,0:T(8,128)S(1)}, bf16[176,512]{1,0:T(8,128)(2,1)S(1)}, f32[48,512]{1,0:T(8,128)S(1)}) custom-call(s32[1]{0:T(128)} %bitcast.place, bf16[8,96,512]{2,1,0:T(8,128)(2,1)S(1)} %bitcast.2, bf16[48,512]{1,0:T(8,128)(2,1)S(1)} %get-tuple-element.28.rho_low, f32[64,512]{1,0:T(8,128)S(1)} %get-tuple-element.29.a_near, ...), custom_call_target="tpu_custom_call" | custom-call | tf_op jit(solution)/shard_map/pallas_call | solution.py:329
  34.5 2.2 %shard_map.70.psi = bf16[3,64,512]{2,1,0:T(8,128)(2,1)S(1)} custom-call(f32[3,80,512]{2,1,0:T(8,128)S(1)} %get-tuple-element.32.change, f32[3,112,512]{2,1,0:T(8,128)S(1)} %get-tuple-element.30.weights, bf16[512,512]{1,0:T(8,128)(2,1)S(1)} %get-tuple-element.22.high_m), custom_call_target="tpu_custom_call" | custom-call | tf_op jit(solution)/shard_map/pallas_call | solution.py:329
  36.7 0.4 collective-permute-start.4
  37.1 2.0 %collective-permute-start.5 = (bf16[176,512]{1,0:T(8,128)(2,1)S(1)}, bf16[176,512]{1,0:T(8,128)(2,1)S(1)}, u32[]{:S(2)}, u32[]{:S(2)}) collective-permute-start(bf16[176,512]{1,0:T(8,128)(2,1)S(1)} %get-tuple-element.33), channel_id=1, source_target_pairs={{0,4},{4,8},{8,12},{12,16},{16,20},{20,24},{24,28},{1,5},{5,9},{9,... | collective-permute-start | bytes 540680 | tf_op jit(solution)/shard_map/ppermute | solution.py:424
  39.2 5.6 %collective-permute-done.5.passed = bf16[176,512]{1,0:T(8,128)(2,1)S(1)} collective-permute-done((bf16[176,512]{1,0:T(8,128)(2,1)S(1)}, bf16[176,512]{1,0:T(8,128)(2,1)S(1)}, u32[]{:S(2)}, u32[]{:S(2)}) %collective-permute-start.5) | collective-permute-done | bytes 180256 | tf_op jit(solution)/shard_map/ppermute | solution.py:424
  44.8 0.0 collective-permute-done.4.psi_other
  44.8 3.2 %last_sweep.1 = f32[8,48,512]{2,1,0:T(8,128)} custom-call(s32[1]{0:T(128)} %bitcast.place, bf16[3,64,512]{2,1,0:T(8,128)(2,1)S(1)} %shard_map.70.psi, bf16[3,64,512]{2,1,0:T(8,128)(2,1)S(1)} %collective-permute-done.4.psi_other, bf16[176,512]{1,0:T(8,128)(2,1)S(1)} %collective-permute-done.5.passed, f32[48,512]{1,0:T(8,128)S(1)} %get-tuple-element.34.b_own, ...), custom_call_target="tpu_custom_call" | custom-call | tf_op jit(solution)/shard_map/last_sweep/pallas_call | solution.py:441
Async XLA Ops:
  1.1 11.8 %collective-permute-start = (bf16[152,512]{1,0:T(8,128)(2,1)S(1)}, bf16[152,512]{1,0:T(8,128)(2,1)S(1)}, u32[]{:S(2)}, u32[]{:S(2)}) collective-permute-start(bf16[152,512]{1,0:T(8,128)(2,1)S(1)} %get-tuple-element.20), channel_id=1, source_target_pairs={{0,1},{1,2},{2,3},{3,0},{4,5},{5,6},{6,7},{7,4},{8,9},{9,10},{10,1... | collective-permute-start | bytes 466952 | tf_op jit(solution)/shard_map/ppermute | solution.py:373
  2.8 10.1 %collective-permute-start.1 = (bf16[152,512]{1,0:T(8,128)(2,1)S(1)}, bf16[152,512]{1,0:T(8,128)(2,1)S(1)}, u32[]{:S(2)}, u32[]{:S(2)}) collective-permute-start(bf16[152,512]{1,0:T(8,128)(2,1)S(1)} %get-tuple-element.21), channel_id=1, source_target_pairs={{0,3},{1,0},{2,1},{3,2},{4,7},{5,4},{6,5},{7,6},{8,11},{9,8},{10,9... | collective-permute-start | bytes 466952 | tf_op jit(solution)/shard_map/ppermute | solution.py:374
  5.0 1.7 %copy-start = (bf16[8,48,512]{2,1,0:T(8,128)(2,1)S(1)}, bf16[8,48,512]{2,1,0:T(8,128)(2,1)}, u32[]{:S(2)}) copy-start(bf16[8,48,512]{2,1,0:T(8,128)(2,1)} %forcing.7) | copy-start | bytes 1179652
  5.0 1.7 %copy-start.1 = (f32[48,512]{1,0:T(8,128)S(1)}, f32[48,512]{1,0:T(8,128)}, u32[]{:S(2)}) copy-start(f32[48,512]{1,0:T(8,128)} %start.7) | copy-start | bytes 294916
  5.0 1.7 %copy-start.2 = (bf16[48,512]{1,0:T(8,128)(2,1)S(1)}, bf16[48,512]{1,0:T(8,128)(2,1)}, u32[]{:S(2)}) copy-start(bf16[48,512]{1,0:T(8,128)(2,1)} %velocity.7) | copy-start | bytes 147460
  5.0 1.7 %copy-start.3 = (bf16[48,512]{1,0:T(8,128)(2,1)S(1)}, bf16[48,512]{1,0:T(8,128)(2,1)}, u32[]{:S(2)}) copy-start(bf16[48,512]{1,0:T(8,128)(2,1)} %diffusion.7) | copy-start | bytes 147460
  9.0 6.3 %collective-permute-start.2 = (bf16[56,512]{1,0:T(8,128)(2,1)S(1)}, bf16[56,512]{1,0:T(8,128)(2,1)S(1)}, u32[]{:S(2)}, u32[]{:S(2)}) collective-permute-start(bf16[56,512]{1,0:T(8,128)(2,1)S(1)} %get-tuple-element.24), channel_id=1, source_target_pairs={{0,1},{1,2},{2,3},{3,0},{4,5},{5,6},{6,7},{7,4},{8,9},{9,10},{10,1... | collective-permute-start | bytes 172040 | tf_op jit(solution)/shard_map/ppermute | solution.py:389
  9.1 6.2 %collective-permute-start.3 = (bf16[56,512]{1,0:T(8,128)(2,1)S(1)}, bf16[56,512]{1,0:T(8,128)(2,1)S(1)}, u32[]{:S(2)}, u32[]{:S(2)}) collective-permute-start(bf16[56,512]{1,0:T(8,128)(2,1)S(1)} %get-tuple-element.25), channel_id=1, source_target_pairs={{0,3},{1,0},{2,1},{3,2},{4,7},{5,4},{6,5},{7,6},{8,11},{9,8},{10,9... | collective-permute-start | bytes 172040 | tf_op jit(solution)/shard_map/ppermute | solution.py:390
  36.7 8.1 %collective-permute-start.4 = (bf16[3,64,512]{2,1,0:T(8,128)(2,1)S(1)}, bf16[3,64,512]{2,1,0:T(8,128)(2,1)S(1)}, u32[]{:S(2)}, u32[]{:S(2)}) collective-permute-start(bf16[3,64,512]{2,1,0:T(8,128)(2,1)S(1)} %shard_map.70.psi), channel_id=1, source_target_pairs={{0,4},{4,0},{8,12},{12,8},{16,20},{20,16},{24,28},{28,24},{1,5},{5... | collective-permute-start | bytes 589832 | tf_op jit(solution)/shard_map/ppermute | solution.py:433
  37.1 7.7 %collective-permute-start.5 = (bf16[176,512]{1,0:T(8,128)(2,1)S(1)}, bf16[176,512]{1,0:T(8,128)(2,1)S(1)}, u32[]{:S(2)}, u32[]{:S(2)}) collective-permute-start(bf16[176,512]{1,0:T(8,128)(2,1)S(1)} %get-tuple-element.33), channel_id=1, source_target_pairs={{0,4},{4,8},{8,12},{12,16},{16,20},{20,24},{24,28},{1,5},{5,9},{9,... | collective-permute-start | bytes 540680 | tf_op jit(solution)/shard_map/ppermute | solution.py:424

commit v11 on v9

--- a/solution.py
+++ b/solution.py
@@ -386,8 +386,9 @@
         [kept(own, columns), second_pack, second_pack],
         place, forcing, velocity, diffusion, initial_state, high_m, low_m,
     )
-    far_low = in_vmem(lax.ppermute(tail, "space", ring(slabs, 1)))
-    far_high = in_vmem(lax.ppermute(head, "space", ring(slabs, -1)))
+    far_low = lax.ppermute(tail, "space", ring(slabs, 1))
+    far_high = lax.ppermute(head, "space", ring(slabs, -1))
+    far_low, far_high = in_vmem(far_low), in_vmem(far_high)
     edges = call(
         edge_sweep,
         lay,

time: 47.7 us -> 47.7 us (level)
  no operation moved by 1% of the time
where the time goes in v11:
time: 47.7 us; the launch traced here: 47.5 us
  Pallas kernels  21.5 us (45%)
  blocking collectives  10.6 us (22%)
  starting transfers between devices  9.64 us (20%)
  waiting for transfers between devices  5.67 us (12%)
    pallas_call x5, Pallas kernels, call(): pl.pallas_call(kernel if lay is None else functools.partial(kernel, lay),...  15.6 us
    all_gather x1, blocking collectives, per_device(): rho_all = lax.all_gather(rho, 'tm', axis=0)  10.6 us
    ppermute x1, waiting for transfers between devices, per_device(): passed = lax.ppermute(passed, 'tm', ring(blocks, 1))  5.66 us
    ppermute x1, starting transfers between devices, per_device(): far_high = lax.ppermute(head, 'space', ring(slabs, -1))  3.81 us
    ppermute x1, starting transfers between devices, per_device(): low = in_vmem(lax.ppermute(tail, 'space', ring(slabs, 1)))  3.1 us
    pallas_call x2, Pallas kernels, call_from_hbm(): pl.pallas_call(kernel, out_shape=outs, in_specs=[pl.BlockSpec(memory_spac...  2.95 us
    pallas_call x1, Pallas kernels, per_device(): pl.pallas_call(functools.partial(kernel, lay), out_shape=jax.ShapeDtypeSt...  2.94 us
    ppermute x1, starting transfers between devices, per_device(): high = in_vmem(lax.ppermute(head, 'space', ring(slabs, -1)))  2.09 us
  transfers between devices with their start and end apart: 6, of which 1 were waited for; matrix products, arithmetic and copies ran while one was open for 0% of the time, Pallas kernels for 13%

profile of v11, /device:TPU:0, one launch (start us, length us, event | category | flops | bytes accessed | tf_op | source)
XLA Modules:
  0.0 47.5 jit_solution(12611792094567681385)
XLA Ops:
  0.0 1.3 %shard_map.64 = (bf16[152,512]{1,0:T(8,128)(2,1)S(1)}, bf16[152,512]{1,0:T(8,128)(2,1)S(1)}) custom-call(bf16[48,512]{1,0:T(8,128)(2,1)} %velocity.7, bf16[48,512]{1,0:T(8,128)(2,1)} %diffusion.7, bf16[8,48,512]{2,1,0:T(8,128)(2,1)} %forcing.7, f32[48,512]{1,0:T(8,128)} %start.7), custom_call_target="tpu_custom_call" | custom-call | tf_op jit(solution)/shard_map/pallas_call | solution.py:340
  1.3 3.1 %collective-permute-start = (bf16[152,512]{1,0:T(8,128)(2,1)S(1)}, bf16[152,512]{1,0:T(8,128)(2,1)S(1)}, u32[]{:S(2)}, u32[]{:S(2)}) collective-permute-start(bf16[152,512]{1,0:T(8,128)(2,1)S(1)} %get-tuple-element.20), channel_id=1, source_target_pairs={{0,1},{1,2},{2,3},{3,0},{4,5},{5,6},{6,7},{7,4},{8,9},{9,10},{10,1... | collective-permute-start | bytes 466952 | tf_op jit(solution)/shard_map/ppermute | solution.py:373
  4.4 2.1 %collective-permute-start.1 = (bf16[152,512]{1,0:T(8,128)(2,1)S(1)}, bf16[152,512]{1,0:T(8,128)(2,1)S(1)}, u32[]{:S(2)}, u32[]{:S(2)}) collective-permute-start(bf16[152,512]{1,0:T(8,128)(2,1)S(1)} %get-tuple-element.21), channel_id=1, source_target_pairs={{0,3},{1,0},{2,1},{3,2},{4,7},{5,4},{6,5},{7,6},{8,11},{9,8},{10,9... | collective-permute-start | bytes 466952 | tf_op jit(solution)/shard_map/ppermute | solution.py:374
  6.5 0.0 copy-start
  6.5 0.0 copy-start.1
  6.5 0.0 copy-start.2
  6.5 0.0 copy-start.3
  6.5 1.7 %shard_map.65 = (bf16[512,512]{1,0:T(8,128)(2,1)S(1)}, bf16[512,512]{1,0:T(8,128)(2,1)S(1)}, bf16[512,512]{1,0:T(8,128)(2,1)S(1)}) custom-call(f32[512,512]{1,0:T(8,128)} %implicit.1, f32[512,512]{1,0:T(8,128)} %coarse_implicit.1), custom_call_target="tpu_custom_call" | custom-call | tf_op jit(solution)/shard_map/pallas_call | solution.py:340
  8.2 0.0 copy-done
  8.2 0.0 copy-done.1
  8.2 0.0 copy-done.2
  8.2 0.0 copy-done.3
  8.2 2.3 %shard_map.66 = (f32[48,512]{1,0:T(8,128)S(1)}, bf16[56,512]{1,0:T(8,128)(2,1)S(1)}, bf16[56,512]{1,0:T(8,128)(2,1)S(1)}) custom-call(s32[1]{0:T(128)} %bitcast.place, bf16[8,48,512]{2,1,0:T(8,128)(2,1)S(1)} %copy-done, bf16[48,512]{1,0:T(8,128)(2,1)S(1)} %copy-done.2, bf16[48,512]{1,0:T(8,128)(2,1)S(1)} %copy-done.3, f32[48,512]{1,0:T(8,128)S(1)} %copy-done.1, ...), custom_call_target="tpu_custom_call" | custom-call | tf_op jit(solution)/shard_map/pallas_call | solution.py:329
  10.5 0.1 collective-permute-start.2
  10.5 3.8 %collective-permute-start.3 = (bf16[56,512]{1,0:T(8,128)(2,1)S(1)}, bf16[56,512]{1,0:T(8,128)(2,1)S(1)}, u32[]{:S(2)}, u32[]{:S(2)}) collective-permute-start(bf16[56,512]{1,0:T(8,128)(2,1)S(1)} %get-tuple-element.25), channel_id=1, source_target_pairs={{0,3},{1,0},{2,1},{3,2},{4,7},{5,4},{6,5},{7,6},{8,11},{9,8},{10,9... | collective-permute-start | bytes 172040 | tf_op jit(solution)/shard_map/ppermute | solution.py:390
  14.4 0.0 collective-permute-done.low
  14.4 0.0 collective-permute-done.1.high
  14.4 2.4 %shard_map.67.edges = f32[32,512]{1,0:T(8,128)S(1)} custom-call(s32[1]{0:T(128)} %bitcast.place, bf16[152,512]{1,0:T(8,128)(2,1)S(1)} %collective-permute-done.low, bf16[152,512]{1,0:T(8,128)(2,1)S(1)} %collective-permute-done.1.high, bf16[8,48,512]{2,1,0:T(8,128)(2,1)S(1)} %copy-done, bf16[48,512]{1,0:T(8,128)(2,1)S(1)} %copy-done.2, ...), custom_call_target="tpu_custom_call" | custom-call | tf_op jit(solution)/shard_map/pallas_call | solution.py:329
  16.8 0.0 collective-permute-done.2.far_low
  16.8 0.0 collective-permute-done.3.far_high
  16.8 2.8 %shard_map.68 = (bf16[96,512]{1,0:T(8,128)(2,1)S(1)}, bf16[48,512]{1,0:T(8,128)(2,1)S(1)}, f32[64,512]{1,0:T(8,128)S(1)}, f32[3,112,512]{2,1,0:T(8,128)S(1)}) custom-call(bf16[152,512]{1,0:T(8,128)(2,1)S(1)} %collective-permute-done.low, bf16[152,512]{1,0:T(8,128)(2,1)S(1)} %collective-permute-done.1.high, ...), custom_call_target="tpu_custom_call" | custom-call | tf_op jit(solution)/shard_map/pallas_call | solution.py:329
  19.6 10.6 %all-gather = bf16[768,512]{1,0:T(8,128)(2,1)S(1)} all-gather(bf16[96,512]{1,0:T(8,128)(2,1)S(1)} %get-tuple-element.27), channel_id=2, replica_groups=mesh['tm'=8,'space'=4] {'tm'}, dimensions={0}, use_global_device_ids=true | all-gather | bytes 884736 | tf_op jit(solution)/shard_map/all_gather | solution.py:411
  30.2 6.0 %shard_map.69 = (f32[3,80,512]{2,1,0:T(8,128)S(1)}, bf16[176,512]{1,0:T(8,128)(2,1)S(1)}, f32[48,512]{1,0:T(8,128)S(1)}) custom-call(s32[1]{0:T(128)} %bitcast.place, bf16[8,96,512]{2,1,0:T(8,128)(2,1)S(1)} %bitcast.2, bf16[48,512]{1,0:T(8,128)(2,1)S(1)} %get-tuple-element.28.rho_low, f32[64,512]{1,0:T(8,128)S(1)} %get-tuple-element.29.a_near, ...), custom_call_target="tpu_custom_call" | custom-call | tf_op jit(solution)/shard_map/pallas_call | solution.py:329
  36.2 2.2 %shard_map.70.psi = bf16[3,64,512]{2,1,0:T(8,128)(2,1)S(1)} custom-call(f32[3,80,512]{2,1,0:T(8,128)S(1)} %get-tuple-element.32.change, f32[3,112,512]{2,1,0:T(8,128)S(1)} %get-tuple-element.30.weights, bf16[512,512]{1,0:T(8,128)(2,1)S(1)} %get-tuple-element.22.high_m), custom_call_target="tpu_custom_call" | custom-call | tf_op jit(solution)/shard_map/pallas_call | solution.py:329
  38.3 0.4 collective-permute-start.4
  38.7 0.2 collective-permute-start.5
  38.9 5.7 %collective-permute-done.5.passed = bf16[176,512]{1,0:T(8,128)(2,1)S(1)} collective-permute-done((bf16[176,512]{1,0:T(8,128)(2,1)S(1)}, bf16[176,512]{1,0:T(8,128)(2,1)S(1)}, u32[]{:S(2)}, u32[]{:S(2)}) %collective-permute-start.5) | collective-permute-done | bytes 180256 | tf_op jit(solution)/shard_map/ppermute | solution.py:425
  44.6 0.0 collective-permute-done.4.psi_other
  44.6 2.9 %last_sweep.1 = f32[8,48,512]{2,1,0:T(8,128)} custom-call(s32[1]{0:T(128)} %bitcast.place, bf16[3,64,512]{2,1,0:T(8,128)(2,1)S(1)} %shard_map.70.psi, bf16[3,64,512]{2,1,0:T(8,128)(2,1)S(1)} %collective-permute-done.4.psi_other, bf16[176,512]{1,0:T(8,128)(2,1)S(1)} %collective-permute-done.5.passed, f32[48,512]{1,0:T(8,128)S(1)} %get-tuple-element.34.b_own, ...), custom_call_target="tpu_custom_call" | custom-call | tf_op jit(solution)/shard_map/last_sweep/pallas_call | solution.py:442
Async XLA Ops:
  1.3 13.1 %collective-permute-start = (bf16[152,512]{1,0:T(8,128)(2,1)S(1)}, bf16[152,512]{1,0:T(8,128)(2,1)S(1)}, u32[]{:S(2)}, u32[]{:S(2)}) collective-permute-start(bf16[152,512]{1,0:T(8,128)(2,1)S(1)} %get-tuple-element.20), channel_id=1, source_target_pairs={{0,1},{1,2},{2,3},{3,0},{4,5},{5,6},{6,7},{7,4},{8,9},{9,10},{10,1... | collective-permute-start | bytes 466952 | tf_op jit(solution)/shard_map/ppermute | solution.py:373
  4.4 10.0 %collective-permute-start.1 = (bf16[152,512]{1,0:T(8,128)(2,1)S(1)}, bf16[152,512]{1,0:T(8,128)(2,1)S(1)}, u32[]{:S(2)}, u32[]{:S(2)}) collective-permute-start(bf16[152,512]{1,0:T(8,128)(2,1)S(1)} %get-tuple-element.21), channel_id=1, source_target_pairs={{0,3},{1,0},{2,1},{3,2},{4,7},{5,4},{6,5},{7,6},{8,11},{9,8},{10,9... | collective-permute-start | bytes 466952 | tf_op jit(solution)/shard_map/ppermute | solution.py:374
  6.5 1.7 %copy-start = (bf16[8,48,512]{2,1,0:T(8,128)(2,1)S(1)}, bf16[8,48,512]{2,1,0:T(8,128)(2,1)}, u32[]{:S(2)}) copy-start(bf16[8,48,512]{2,1,0:T(8,128)(2,1)} %forcing.7) | copy-start | bytes 1179652
  6.5 1.7 %copy-start.1 = (f32[48,512]{1,0:T(8,128)S(1)}, f32[48,512]{1,0:T(8,128)}, u32[]{:S(2)}) copy-start(f32[48,512]{1,0:T(8,128)} %start.7) | copy-start | bytes 294916
  6.5 1.7 %copy-start.2 = (bf16[48,512]{1,0:T(8,128)(2,1)S(1)}, bf16[48,512]{1,0:T(8,128)(2,1)}, u32[]{:S(2)}) copy-start(bf16[48,512]{1,0:T(8,128)(2,1)} %velocity.7) | copy-start | bytes 147460
  6.5 1.7 %copy-start.3 = (bf16[48,512]{1,0:T(8,128)(2,1)S(1)}, bf16[48,512]{1,0:T(8,128)(2,1)}, u32[]{:S(2)}) copy-start(bf16[48,512]{1,0:T(8,128)(2,1)} %diffusion.7) | copy-start | bytes 147460
  10.5 6.3 %collective-permute-start.2 = (bf16[56,512]{1,0:T(8,128)(2,1)S(1)}, bf16[56,512]{1,0:T(8,128)(2,1)S(1)}, u32[]{:S(2)}, u32[]{:S(2)}) collective-permute-start(bf16[56,512]{1,0:T(8,128)(2,1)S(1)} %get-tuple-element.24), channel_id=1, source_target_pairs={{0,1},{1,2},{2,3},{3,0},{4,5},{5,6},{6,7},{7,4},{8,9},{9,10},{10,1... | collective-permute-start | bytes 172040 | tf_op jit(solution)/shard_map/ppermute | solution.py:389
  10.5 6.2 %collective-permute-start.3 = (bf16[56,512]{1,0:T(8,128)(2,1)S(1)}, bf16[56,512]{1,0:T(8,128)(2,1)S(1)}, u32[]{:S(2)}, u32[]{:S(2)}) collective-permute-start(bf16[56,512]{1,0:T(8,128)(2,1)S(1)} %get-tuple-element.25), channel_id=1, source_target_pairs={{0,3},{1,0},{2,1},{3,2},{4,7},{5,4},{6,5},{7,6},{8,11},{9,8},{10,9... | collective-permute-start | bytes 172040 | tf_op jit(solution)/shard_map/ppermute | solution.py:390
  38.3 6.2 %collective-permute-start.4 = (bf16[3,64,512]{2,1,0:T(8,128)(2,1)S(1)}, bf16[3,64,512]{2,1,0:T(8,128)(2,1)S(1)}, u32[]{:S(2)}, u32[]{:S(2)}) collective-permute-start(bf16[3,64,512]{2,1,0:T(8,128)(2,1)S(1)} %shard_map.70.psi), channel_id=1, source_target_pairs={{0,4},{4,0},{8,12},{12,8},{16,20},{20,16},{24,28},{28,24},{1,5},{5... | collective-permute-start | bytes 589832 | tf_op jit(solution)/shard_map/ppermute | solution.py:434
  38.7 5.8 %collective-permute-start.5 = (bf16[176,512]{1,0:T(8,128)(2,1)S(1)}, bf16[176,512]{1,0:T(8,128)(2,1)S(1)}, u32[]{:S(2)}, u32[]{:S(2)}) collective-permute-start(bf16[176,512]{1,0:T(8,128)(2,1)S(1)} %get-tuple-element.33), channel_id=1, source_target_pairs={{0,4},{4,8},{8,12},{12,16},{16,20},{20,24},{24,28},{28,0},{1,5},{5... | collective-permute-start | bytes 540680 | tf_op jit(solution)/shard_map/ppermute | solution.py:425

commit v12 on v9

--- a/solution.py
+++ b/solution.py
@@ -370,8 +370,9 @@
         ],
         velocity, diffusion, forcing, initial_state,
     )
-    low = in_vmem(lax.ppermute(tail, "space", ring(slabs, 1)))
-    high = in_vmem(lax.ppermute(head, "space", ring(slabs, -1)))
+    low = lax.ppermute(tail, "space", ring(slabs, 1))
+    high = lax.ppermute(head, "space", ring(slabs, -1))
+    low, high = in_vmem(low), in_vmem(high)
     high_m, low_m, coarse = call_from_hbm(
         split_matrices,
         [kept(*implicit.shape, dtype=BF16)] * 3,

time: 47.7 us -> 47.7 us (level)
  no operation moved by 1% of the time
where the time goes in v12:
time: 47.7 us; the launch traced here: 47.5 us
  Pallas kernels  21.5 us (45%)
  blocking collectives  10.6 us (22%)
  starting transfers between devices  9.64 us (20%)
  waiting for transfers between devices  5.67 us (12%)
    pallas_call x5, Pallas kernels, call(): pl.pallas_call(kernel if lay is None else functools.partial(kernel, lay),...  15.6 us
    all_gather x1, blocking collectives, per_device(): rho_all = lax.all_gather(rho, 'tm', axis=0)  10.6 us
    ppermute x1, waiting for transfers between devices, per_device(): passed = lax.ppermute(passed, 'tm', ring(blocks, 1))  5.66 us
    ppermute x1, starting transfers between devices, per_device(): far_high = in_vmem(lax.ppermute(head, 'space', ring(slabs, -1)))  3.81 us
    ppermute x1, starting transfers between devices, per_device(): low = lax.ppermute(tail, 'space', ring(slabs, 1))  3.1 us
    pallas_call x2, Pallas kernels, call_from_hbm(): pl.pallas_call(kernel, out_shape=outs, in_specs=[pl.BlockSpec(memory_spac...  2.95 us
    pallas_call x1, Pallas kernels, per_device(): pl.pallas_call(functools.partial(kernel, lay), out_shape=jax.ShapeDtypeSt...  2.94 us
    ppermute x1, starting transfers between devices, per_device(): high = lax.ppermute(head, 'space', ring(slabs, -1))  2.09 us
  transfers between devices with their start and end apart: 6, of which 1 were waited for; matrix products, arithmetic and copies ran while one was open for 0% of the time, Pallas kernels for 13%

profile of v12, /device:TPU:0, one launch (start us, length us, event | category | flops | bytes accessed | tf_op | source)
XLA Modules:
  0.0 47.5 jit_solution(12611792094567681385)
XLA Ops:
  0.0 1.3 %shard_map.64 = (bf16[152,512]{1,0:T(8,128)(2,1)S(1)}, bf16[152,512]{1,0:T(8,128)(2,1)S(1)}) custom-call(bf16[48,512]{1,0:T(8,128)(2,1)} %velocity.7, bf16[48,512]{1,0:T(8,128)(2,1)} %diffusion.7, bf16[8,48,512]{2,1,0:T(8,128)(2,1)} %forcing.7, f32[48,512]{1,0:T(8,128)} %start.7), custom_call_target="tpu_custom_call" | custom-call | tf_op jit(solution)/shard_map/pallas_call | solution.py:340
  1.3 3.1 %collective-permute-start = (bf16[152,512]{1,0:T(8,128)(2,1)S(1)}, bf16[152,512]{1,0:T(8,128)(2,1)S(1)}, u32[]{:S(2)}, u32[]{:S(2)}) collective-permute-start(bf16[152,512]{1,0:T(8,128)(2,1)S(1)} %get-tuple-element.20), channel_id=1, source_target_pairs={{0,1},{1,2},{2,3},{3,0},{4,5},{5,6},{6,7},{7,4},{8,9},{9,10},{10,1... | collective-permute-start | bytes 466952 | tf_op jit(solution)/shard_map/ppermute | solution.py:373
  4.4 2.1 %collective-permute-start.1 = (bf16[152,512]{1,0:T(8,128)(2,1)S(1)}, bf16[152,512]{1,0:T(8,128)(2,1)S(1)}, u32[]{:S(2)}, u32[]{:S(2)}) collective-permute-start(bf16[152,512]{1,0:T(8,128)(2,1)S(1)} %get-tuple-element.21), channel_id=1, source_target_pairs={{0,3},{1,0},{2,1},{3,2},{4,7},{5,4},{6,5},{7,6},{8,11},{9,8},{10,9... | collective-permute-start | bytes 466952 | tf_op jit(solution)/shard_map/ppermute | solution.py:374
  6.5 0.0 copy-start
  6.5 0.0 copy-start.1
  6.5 0.0 copy-start.2
  6.5 0.0 copy-start.3
  6.5 1.7 %shard_map.65 = (bf16[512,512]{1,0:T(8,128)(2,1)S(1)}, bf16[512,512]{1,0:T(8,128)(2,1)S(1)}, bf16[512,512]{1,0:T(8,128)(2,1)S(1)}) custom-call(f32[512,512]{1,0:T(8,128)} %implicit.1, f32[512,512]{1,0:T(8,128)} %coarse_implicit.1), custom_call_target="tpu_custom_call" | custom-call | tf_op jit(solution)/shard_map/pallas_call | solution.py:340
  8.2 0.0 copy-done
  8.2 0.0 copy-done.1
  8.2 0.0 copy-done.2
  8.2 0.0 copy-done.3
  8.2 2.3 %shard_map.66 = (f32[48,512]{1,0:T(8,128)S(1)}, bf16[56,512]{1,0:T(8,128)(2,1)S(1)}, bf16[56,512]{1,0:T(8,128)(2,1)S(1)}) custom-call(s32[1]{0:T(128)} %bitcast.place, bf16[8,48,512]{2,1,0:T(8,128)(2,1)S(1)} %copy-done, bf16[48,512]{1,0:T(8,128)(2,1)S(1)} %copy-done.2, bf16[48,512]{1,0:T(8,128)(2,1)S(1)} %copy-done.3, f32[48,512]{1,0:T(8,128)S(1)} %copy-done.1, ...), custom_call_target="tpu_custom_call" | custom-call | tf_op jit(solution)/shard_map/pallas_call | solution.py:329
  10.5 0.1 collective-permute-start.2
  10.5 3.8 %collective-permute-start.3 = (bf16[56,512]{1,0:T(8,128)(2,1)S(1)}, bf16[56,512]{1,0:T(8,128)(2,1)S(1)}, u32[]{:S(2)}, u32[]{:S(2)}) collective-permute-start(bf16[56,512]{1,0:T(8,128)(2,1)S(1)} %get-tuple-element.25), channel_id=1, source_target_pairs={{0,3},{1,0},{2,1},{3,2},{4,7},{5,4},{6,5},{7,6},{8,11},{9,8},{10,9... | collective-permute-start | bytes 172040 | tf_op jit(solution)/shard_map/ppermute | solution.py:391
  14.4 0.0 collective-permute-done.low
  14.4 0.0 collective-permute-done.1.high
  14.4 2.4 %shard_map.67.edges = f32[32,512]{1,0:T(8,128)S(1)} custom-call(s32[1]{0:T(128)} %bitcast.place, bf16[152,512]{1,0:T(8,128)(2,1)S(1)} %collective-permute-done.low, bf16[152,512]{1,0:T(8,128)(2,1)S(1)} %collective-permute-done.1.high, bf16[8,48,512]{2,1,0:T(8,128)(2,1)S(1)} %copy-done, bf16[48,512]{1,0:T(8,128)(2,1)S(1)} %copy-done.2, ...), custom_call_target="tpu_custom_call" | custom-call | tf_op jit(solution)/shard_map/pallas_call | solution.py:329
  16.8 0.0 collective-permute-done.2.far_low
  16.8 0.0 collective-permute-done.3.far_high
  16.8 2.8 %shard_map.68 = (bf16[96,512]{1,0:T(8,128)(2,1)S(1)}, bf16[48,512]{1,0:T(8,128)(2,1)S(1)}, f32[64,512]{1,0:T(8,128)S(1)}, f32[3,112,512]{2,1,0:T(8,128)S(1)}) custom-call(bf16[152,512]{1,0:T(8,128)(2,1)S(1)} %collective-permute-done.low, bf16[152,512]{1,0:T(8,128)(2,1)S(1)} %collective-permute-done.1.high, ...), custom_call_target="tpu_custom_call" | custom-call | tf_op jit(solution)/shard_map/pallas_call | solution.py:329
  19.6 10.6 %all-gather = bf16[768,512]{1,0:T(8,128)(2,1)S(1)} all-gather(bf16[96,512]{1,0:T(8,128)(2,1)S(1)} %get-tuple-element.27), channel_id=2, replica_groups=mesh['tm'=8,'space'=4] {'tm'}, dimensions={0}, use_global_device_ids=true | all-gather | bytes 884736 | tf_op jit(solution)/shard_map/all_gather | solution.py:411
  30.2 6.0 %shard_map.69 = (f32[3,80,512]{2,1,0:T(8,128)S(1)}, bf16[176,512]{1,0:T(8,128)(2,1)S(1)}, f32[48,512]{1,0:T(8,128)S(1)}) custom-call(s32[1]{0:T(128)} %bitcast.place, bf16[8,96,512]{2,1,0:T(8,128)(2,1)S(1)} %bitcast.2, bf16[48,512]{1,0:T(8,128)(2,1)S(1)} %get-tuple-element.28.rho_low, f32[64,512]{1,0:T(8,128)S(1)} %get-tuple-element.29.a_near, ...), custom_call_target="tpu_custom_call" | custom-call | tf_op jit(solution)/shard_map/pallas_call | solution.py:329
  36.2 2.2 %shard_map.70.psi = bf16[3,64,512]{2,1,0:T(8,128)(2,1)S(1)} custom-call(f32[3,80,512]{2,1,0:T(8,128)S(1)} %get-tuple-element.32.change, f32[3,112,512]{2,1,0:T(8,128)S(1)} %get-tuple-element.30.weights, bf16[512,512]{1,0:T(8,128)(2,1)S(1)} %get-tuple-element.22.high_m), custom_call_target="tpu_custom_call" | custom-call | tf_op jit(solution)/shard_map/pallas_call | solution.py:329
  38.3 0.4 collective-permute-start.4
  38.7 0.2 collective-permute-start.5
  38.9 5.7 %collective-permute-done.5.passed = bf16[176,512]{1,0:T(8,128)(2,1)S(1)} collective-permute-done((bf16[176,512]{1,0:T(8,128)(2,1)S(1)}, bf16[176,512]{1,0:T(8,128)(2,1)S(1)}, u32[]{:S(2)}, u32[]{:S(2)}) %collective-permute-start.5) | collective-permute-done | bytes 180256 | tf_op jit(solution)/shard_map/ppermute | solution.py:425
  44.6 0.0 collective-permute-done.4.psi_other
  44.6 2.9 %last_sweep.1 = f32[8,48,512]{2,1,0:T(8,128)} custom-call(s32[1]{0:T(128)} %bitcast.place, bf16[3,64,512]{2,1,0:T(8,128)(2,1)S(1)} %shard_map.70.psi, bf16[3,64,512]{2,1,0:T(8,128)(2,1)S(1)} %collective-permute-done.4.psi_other, bf16[176,512]{1,0:T(8,128)(2,1)S(1)} %collective-permute-done.5.passed, f32[48,512]{1,0:T(8,128)S(1)} %get-tuple-element.34.b_own, ...), custom_call_target="tpu_custom_call" | custom-call | tf_op jit(solution)/shard_map/last_sweep/pallas_call | solution.py:442
Async XLA Ops:
  1.3 13.1 %collective-permute-start = (bf16[152,512]{1,0:T(8,128)(2,1)S(1)}, bf16[152,512]{1,0:T(8,128)(2,1)S(1)}, u32[]{:S(2)}, u32[]{:S(2)}) collective-permute-start(bf16[152,512]{1,0:T(8,128)(2,1)S(1)} %get-tuple-element.20), channel_id=1, source_target_pairs={{0,1},{1,2},{2,3},{3,0},{4,5},{5,6},{6,7},{7,4},{8,9},{9,10},{10,1... | collective-permute-start | bytes 466952 | tf_op jit(solution)/shard_map/ppermute | solution.py:373
  4.4 10.0 %collective-permute-start.1 = (bf16[152,512]{1,0:T(8,128)(2,1)S(1)}, bf16[152,512]{1,0:T(8,128)(2,1)S(1)}, u32[]{:S(2)}, u32[]{:S(2)}) collective-permute-start(bf16[152,512]{1,0:T(8,128)(2,1)S(1)} %get-tuple-element.21), channel_id=1, source_target_pairs={{0,3},{1,0},{2,1},{3,2},{4,7},{5,4},{6,5},{7,6},{8,11},{9,8},{10,9... | collective-permute-start | bytes 466952 | tf_op jit(solution)/shard_map/ppermute | solution.py:374
  6.5 1.7 %copy-start = (bf16[8,48,512]{2,1,0:T(8,128)(2,1)S(1)}, bf16[8,48,512]{2,1,0:T(8,128)(2,1)}, u32[]{:S(2)}) copy-start(bf16[8,48,512]{2,1,0:T(8,128)(2,1)} %forcing.7) | copy-start | bytes 1179652
  6.5 1.7 %copy-start.1 = (f32[48,512]{1,0:T(8,128)S(1)}, f32[48,512]{1,0:T(8,128)}, u32[]{:S(2)}) copy-start(f32[48,512]{1,0:T(8,128)} %start.7) | copy-start | bytes 294916
  6.5 1.7 %copy-start.2 = (bf16[48,512]{1,0:T(8,128)(2,1)S(1)}, bf16[48,512]{1,0:T(8,128)(2,1)}, u32[]{:S(2)}) copy-start(bf16[48,512]{1,0:T(8,128)(2,1)} %velocity.7) | copy-start | bytes 147460
  6.5 1.7 %copy-start.3 = (bf16[48,512]{1,0:T(8,128)(2,1)S(1)}, bf16[48,512]{1,0:T(8,128)(2,1)}, u32[]{:S(2)}) copy-start(bf16[48,512]{1,0:T(8,128)(2,1)} %diffusion.7) | copy-start | bytes 147460
  10.5 6.3 %collective-permute-start.2 = (bf16[56,512]{1,0:T(8,128)(2,1)S(1)}, bf16[56,512]{1,0:T(8,128)(2,1)S(1)}, u32[]{:S(2)}, u32[]{:S(2)}) collective-permute-start(bf16[56,512]{1,0:T(8,128)(2,1)S(1)} %get-tuple-element.24), channel_id=1, source_target_pairs={{0,1},{1,2},{2,3},{3,0},{4,5},{5,6},{6,7},{7,4},{8,9},{9,10},{10,1... | collective-permute-start | bytes 172040 | tf_op jit(solution)/shard_map/ppermute | solution.py:390
  10.5 6.2 %collective-permute-start.3 = (bf16[56,512]{1,0:T(8,128)(2,1)S(1)}, bf16[56,512]{1,0:T(8,128)(2,1)S(1)}, u32[]{:S(2)}, u32[]{:S(2)}) collective-permute-start(bf16[56,512]{1,0:T(8,128)(2,1)S(1)} %get-tuple-element.25), channel_id=1, source_target_pairs={{0,3},{1,0},{2,1},{3,2},{4,7},{5,4},{6,5},{7,6},{8,11},{9,8},{10,9... | collective-permute-start | bytes 172040 | tf_op jit(solution)/shard_map/ppermute | solution.py:391
  38.3 6.2 %collective-permute-start.4 = (bf16[3,64,512]{2,1,0:T(8,128)(2,1)S(1)}, bf16[3,64,512]{2,1,0:T(8,128)(2,1)S(1)}, u32[]{:S(2)}, u32[]{:S(2)}) collective-permute-start(bf16[3,64,512]{2,1,0:T(8,128)(2,1)S(1)} %shard_map.70.psi), channel_id=1, source_target_pairs={{0,4},{4,0},{8,12},{12,8},{16,20},{20,16},{24,28},{28,24},{1,5},{5... | collective-permute-start | bytes 589832 | tf_op jit(solution)/shard_map/ppermute | solution.py:434
  38.7 5.8 %collective-permute-start.5 = (bf16[176,512]{1,0:T(8,128)(2,1)S(1)}, bf16[176,512]{1,0:T(8,128)(2,1)S(1)}, u32[]{:S(2)}, u32[]{:S(2)}) collective-permute-start(bf16[176,512]{1,0:T(8,128)(2,1)S(1)} %get-tuple-element.33), channel_id=1, source_target_pairs={{0,4},{4,8},{8,12},{12,16},{16,20},{20,24},{24,28},{28,0},{1,5},{5... | collective-permute-start | bytes 540680 | tf_op jit(solution)/shard_map/ppermute | solution.py:425

commit v13 on v9

--- a/solution.py
+++ b/solution.py
@@ -111,15 +111,18 @@
             out[at : at + steps] = both.astype(BF16)
 
 
-def split_matrices(implicit, coarse_implicit, high_m, low_m, coarse, fine_kept, coarse_kept, semaphores):
-    fine_copy = pltpu.make_async_copy(implicit, fine_kept, semaphores.at[0])
-    coarse_copy = pltpu.make_async_copy(coarse_implicit, coarse_kept, semaphores.at[1])
-    fine_copy.start()
-    coarse_copy.start()
-    fine_copy.wait()
-    high_m[...], low_m[...] = split(fine_kept[...])
-    coarse_copy.wait()
-    coarse[...] = coarse_kept[...].astype(BF16)
+def split_matrix(implicit, high_m, low_m, kept, semaphore):
+    copy = pltpu.make_async_copy(implicit, kept, semaphore.at[0])
+    copy.start()
+    copy.wait()
+    high_m[...], low_m[...] = split(kept[...])
+
+
+def round_matrix(coarse_implicit, coarse, kept, semaphore):
+    copy = pltpu.make_async_copy(coarse_implicit, kept, semaphore.at[0])
+    copy.start()
+    copy.wait()
+    coarse[...] = kept[...].astype(BF16)
 
 
 def joined(low, own, high):
@@ -372,12 +375,9 @@
     )
     low = in_vmem(lax.ppermute(tail, "space", ring(slabs, 1)))
     high = in_vmem(lax.ppermute(head, "space", ring(slabs, -1)))
-    high_m, low_m, coarse = call_from_hbm(
-        split_matrices,
-        [kept(*implicit.shape, dtype=BF16)] * 3,
-        [pltpu.VMEM(implicit.shape, F32), pltpu.VMEM(implicit.shape, F32), pltpu.SemaphoreType.DMA((2,))],
-        implicit, coarse_implicit,
-    )
+    matrix, scratch = kept(*implicit.shape, dtype=BF16), [pltpu.VMEM(implicit.shape, F32), pltpu.SemaphoreType.DMA((1,))]
+    high_m, low_m = call_from_hbm(split_matrix, [matrix] * 2, scratch, implicit)
+    (coarse,) = call_from_hbm(round_matrix, [matrix], scratch, coarse_implicit)
     high_m, low_m, coarse = in_vmem(high_m), in_vmem(low_m), in_vmem(coarse)
     second_pack = kept(lay.second_rows, columns, dtype=BF16)
     a, head, tail = call(
@@ -387,7 +387,8 @@
         place, forcing, velocity, diffusion, initial_state, high_m, low_m,
     )
     far_low = in_vmem(lax.ppermute(tail, "space", ring(slabs, 1)))
-    far_high = in_vmem(lax.ppermute(head, "space", ring(slabs, -1)))
+    far_high = lax.ppermute(head, "space", ring(slabs, -1))
+    far_high = in_vmem(far_high)
     edges = call(
         edge_sweep,
         lay,

time: 47.7 us -> 48.8 us (1.023)
  Pallas kernels: 21.5 us -> 22.6 us
    pallas_call x2 -> x3, Pallas kernels: 2.95 us -> 3.99 us  [call_from_hbm(): pl.pallas_call(kernel, out_shape=outs, in_specs=[pl.BlockSpec(memory_spac...]
  transfers between devices with their start and end apart: 6 -> 6, of which waited for: 1 -> 1; matrix products, arithmetic and copies ran while one was open for 0% -> 0% of each run, Pallas kernels for 13% -> 15%
where the time goes in v13:
time: 48.8 us; the launch traced here: 48.6 us
  Pallas kernels  22.6 us (46%)
  blocking collectives  10.6 us (22%)
  starting transfers between devices  9.64 us (20%)
  waiting for transfers between devices  5.67 us (12%)
    pallas_call x5, Pallas kernels, call(): pl.pallas_call(kernel if lay is None else functools.partial(kernel, lay),...  15.6 us
    all_gather x1, blocking collectives, per_device(): rho_all = lax.all_gather(rho, 'tm', axis=0)  10.6 us
    ppermute x1, waiting for transfers between devices, per_device(): passed = lax.ppermute(passed, 'tm', ring(blocks, 1))  5.66 us
    pallas_call x3, Pallas kernels, call_from_hbm(): pl.pallas_call(kernel, out_shape=outs, in_specs=[pl.BlockSpec(memory_spac...  3.99 us
    ppermute x1, starting transfers between devices, per_device(): far_high = lax.ppermute(head, 'space', ring(slabs, -1))  3.81 us
    ppermute x1, starting transfers between devices, per_device(): low = in_vmem(lax.ppermute(tail, 'space', ring(slabs, 1)))  3.1 us
    pallas_call x1, Pallas kernels, per_device(): pl.pallas_call(functools.partial(kernel, lay), out_shape=jax.ShapeDtypeSt...  2.94 us
    ppermute x1, starting transfers between devices, per_device(): high = in_vmem(lax.ppermute(head, 'space', ring(slabs, -1)))  2.09 us
  transfers between devices with their start and end apart: 6, of which 1 were waited for; matrix products, arithmetic and copies ran while one was open for 0% of the time, Pallas kernels for 15%

profile of v13, /device:TPU:0, one launch (start us, length us, event | category | flops | bytes accessed | tf_op | source)
XLA Modules:
  0.0 48.6 jit_solution(7438786969505715846)
XLA Ops:
  0.0 1.3 %shard_map.64 = (bf16[152,512]{1,0:T(8,128)(2,1)S(1)}, bf16[152,512]{1,0:T(8,128)(2,1)S(1)}) custom-call(bf16[48,512]{1,0:T(8,128)(2,1)} %velocity.7, bf16[48,512]{1,0:T(8,128)(2,1)} %diffusion.7, bf16[8,48,512]{2,1,0:T(8,128)(2,1)} %forcing.7, f32[48,512]{1,0:T(8,128)} %start.7), custom_call_target="tpu_custom_call" | custom-call | tf_op jit(solution)/shard_map/pallas_call | solution.py:343
  1.3 3.1 %collective-permute-start = (bf16[152,512]{1,0:T(8,128)(2,1)S(1)}, bf16[152,512]{1,0:T(8,128)(2,1)S(1)}, u32[]{:S(2)}, u32[]{:S(2)}) collective-permute-start(bf16[152,512]{1,0:T(8,128)(2,1)S(1)} %get-tuple-element.19), channel_id=1, source_target_pairs={{0,1},{1,2},{2,3},{3,0},{4,5},{5,6},{6,7},{7,4},{8,9},{9,10},{10,1... | collective-permute-start | bytes 466952 | tf_op jit(solution)/shard_map/ppermute | solution.py:376
  4.4 2.1 %collective-permute-start.1 = (bf16[152,512]{1,0:T(8,128)(2,1)S(1)}, bf16[152,512]{1,0:T(8,128)(2,1)S(1)}, u32[]{:S(2)}, u32[]{:S(2)}) collective-permute-start(bf16[152,512]{1,0:T(8,128)(2,1)S(1)} %get-tuple-element.20), channel_id=1, source_target_pairs={{0,3},{1,0},{2,1},{3,2},{4,7},{5,4},{6,5},{7,6},{8,11},{9,8},{10,9... | collective-permute-start | bytes 466952 | tf_op jit(solution)/shard_map/ppermute | solution.py:377
  6.5 0.0 copy-start
  6.5 0.0 copy-start.1
  6.5 0.0 copy-start.2
  6.5 0.0 copy-start.3
  6.5 1.4 %shard_map.65 = (bf16[512,512]{1,0:T(8,128)(2,1)S(1)}, bf16[512,512]{1,0:T(8,128)(2,1)S(1)}) custom-call(f32[512,512]{1,0:T(8,128)} %implicit.1), custom_call_target="tpu_custom_call" | custom-call | tf_op jit(solution)/shard_map/pallas_call | solution.py:343
  7.9 0.0 copy-done
  7.9 0.0 copy-done.1
  8.0 0.0 copy-done.2
  8.0 0.0 copy-done.3
  8.0 2.3 %shard_map.66 = (f32[48,512]{1,0:T(8,128)S(1)}, bf16[56,512]{1,0:T(8,128)(2,1)S(1)}, bf16[56,512]{1,0:T(8,128)(2,1)S(1)}) custom-call(s32[1]{0:T(128)} %bitcast.place, bf16[8,48,512]{2,1,0:T(8,128)(2,1)S(1)} %copy-done, bf16[48,512]{1,0:T(8,128)(2,1)S(1)} %copy-done.2, bf16[48,512]{1,0:T(8,128)(2,1)S(1)} %copy-done.3, f32[48,512]{1,0:T(8,128)S(1)} %copy-done.1, ...), custom_call_target="tpu_custom_call" | custom-call | tf_op jit(solution)/shard_map/pallas_call | solution.py:332
  10.2 0.1 collective-permute-start.2
  10.3 3.8 %collective-permute-start.3 = (bf16[56,512]{1,0:T(8,128)(2,1)S(1)}, bf16[56,512]{1,0:T(8,128)(2,1)S(1)}, u32[]{:S(2)}, u32[]{:S(2)}) collective-permute-start(bf16[56,512]{1,0:T(8,128)(2,1)S(1)} %get-tuple-element.24), channel_id=1, source_target_pairs={{0,3},{1,0},{2,1},{3,2},{4,7},{5,4},{6,5},{7,6},{8,11},{9,8},{10,9... | collective-permute-start | bytes 172040 | tf_op jit(solution)/shard_map/ppermute | solution.py:390
  14.1 1.3 %shard_map.69.coarse = bf16[512,512]{1,0:T(8,128)(2,1)S(1)} custom-call(f32[512,512]{1,0:T(8,128)} %coarse_implicit.1), custom_call_target="tpu_custom_call" | custom-call | tf_op jit(solution)/shard_map/pallas_call | solution.py:343
  15.4 0.0 collective-permute-done.low
  15.4 0.0 collective-permute-done.1.high
  15.4 2.4 %shard_map.67.edges = f32[32,512]{1,0:T(8,128)S(1)} custom-call(s32[1]{0:T(128)} %bitcast.place, bf16[152,512]{1,0:T(8,128)(2,1)S(1)} %collective-permute-done.low, bf16[152,512]{1,0:T(8,128)(2,1)S(1)} %collective-permute-done.1.high, bf16[8,48,512]{2,1,0:T(8,128)(2,1)S(1)} %copy-done, bf16[48,512]{1,0:T(8,128)(2,1)S(1)} %copy-done.2, ...), custom_call_target="tpu_custom_call" | custom-call | tf_op jit(solution)/shard_map/pallas_call | solution.py:332
  17.8 0.0 collective-permute-done.2.far_low
  17.9 0.0 collective-permute-done.3.far_high
  17.9 2.8 %shard_map.68 = (bf16[96,512]{1,0:T(8,128)(2,1)S(1)}, bf16[48,512]{1,0:T(8,128)(2,1)S(1)}, f32[64,512]{1,0:T(8,128)S(1)}, f32[3,112,512]{2,1,0:T(8,128)S(1)}) custom-call(bf16[152,512]{1,0:T(8,128)(2,1)S(1)} %collective-permute-done.low, bf16[152,512]{1,0:T(8,128)(2,1)S(1)} %collective-permute-done.1.high, ...), custom_call_target="tpu_custom_call" | custom-call | tf_op jit(solution)/shard_map/pallas_call | solution.py:332
  20.7 10.6 %all-gather = bf16[768,512]{1,0:T(8,128)(2,1)S(1)} all-gather(bf16[96,512]{1,0:T(8,128)(2,1)S(1)} %get-tuple-element.26), channel_id=2, replica_groups=mesh['tm'=8,'space'=4] {'tm'}, dimensions={0}, use_global_device_ids=true | all-gather | bytes 884736 | tf_op jit(solution)/shard_map/all_gather | solution.py:411
  31.3 6.0 %shard_map.70 = (f32[3,80,512]{2,1,0:T(8,128)S(1)}, bf16[176,512]{1,0:T(8,128)(2,1)S(1)}, f32[48,512]{1,0:T(8,128)S(1)}) custom-call(s32[1]{0:T(128)} %bitcast.place, bf16[8,96,512]{2,1,0:T(8,128)(2,1)S(1)} %bitcast.2, bf16[48,512]{1,0:T(8,128)(2,1)S(1)} %get-tuple-element.27.rho_low, f32[64,512]{1,0:T(8,128)S(1)} %get-tuple-element.28.a_near, ...), custom_call_target="tpu_custom_call" | custom-call | tf_op jit(solution)/shard_map/pallas_call | solution.py:332
  37.2 2.2 %shard_map.71.psi = bf16[3,64,512]{2,1,0:T(8,128)(2,1)S(1)} custom-call(f32[3,80,512]{2,1,0:T(8,128)S(1)} %get-tuple-element.30.change, f32[3,112,512]{2,1,0:T(8,128)S(1)} %get-tuple-element.29.weights, bf16[512,512]{1,0:T(8,128)(2,1)S(1)} %get-tuple-element.21.high_m), custom_call_target="tpu_custom_call" | custom-call | tf_op jit(solution)/shard_map/pallas_call | solution.py:332
  39.4 0.4 collective-permute-start.4
  39.8 0.2 collective-permute-start.5
  40.0 5.7 %collective-permute-done.5.passed = bf16[176,512]{1,0:T(8,128)(2,1)S(1)} collective-permute-done((bf16[176,512]{1,0:T(8,128)(2,1)S(1)}, bf16[176,512]{1,0:T(8,128)(2,1)S(1)}, u32[]{:S(2)}, u32[]{:S(2)}) %collective-permute-start.5) | collective-permute-done | bytes 180256 | tf_op jit(solution)/shard_map/ppermute | solution.py:425
  45.6 0.0 collective-permute-done.4.psi_other
  45.6 2.9 %last_sweep.1 = f32[8,48,512]{2,1,0:T(8,128)} custom-call(s32[1]{0:T(128)} %bitcast.place, bf16[3,64,512]{2,1,0:T(8,128)(2,1)S(1)} %shard_map.71.psi, bf16[3,64,512]{2,1,0:T(8,128)(2,1)S(1)} %collective-permute-done.4.psi_other, bf16[176,512]{1,0:T(8,128)(2,1)S(1)} %collective-permute-done.5.passed, f32[48,512]{1,0:T(8,128)S(1)} %get-tuple-element.32.b_own, ...), custom_call_target="tpu_custom_call" | custom-call | tf_op jit(solution)/shard_map/last_sweep/pallas_call | solution.py:442
Async XLA Ops:
  1.3 14.1 %collective-permute-start = (bf16[152,512]{1,0:T(8,128)(2,1)S(1)}, bf16[152,512]{1,0:T(8,128)(2,1)S(1)}, u32[]{:S(2)}, u32[]{:S(2)}) collective-permute-start(bf16[152,512]{1,0:T(8,128)(2,1)S(1)} %get-tuple-element.19), channel_id=1, source_target_pairs={{0,1},{1,2},{2,3},{3,0},{4,5},{5,6},{6,7},{7,4},{8,9},{9,10},{10,1... | collective-permute-start | bytes 466952 | tf_op jit(solution)/shard_map/ppermute | solution.py:376
  4.4 11.0 %collective-permute-start.1 = (bf16[152,512]{1,0:T(8,128)(2,1)S(1)}, bf16[152,512]{1,0:T(8,128)(2,1)S(1)}, u32[]{:S(2)}, u32[]{:S(2)}) collective-permute-start(bf16[152,512]{1,0:T(8,128)(2,1)S(1)} %get-tuple-element.20), channel_id=1, source_target_pairs={{0,3},{1,0},{2,1},{3,2},{4,7},{5,4},{6,5},{7,6},{8,11},{9,8},{10,9... | collective-permute-start | bytes 466952 | tf_op jit(solution)/shard_map/ppermute | solution.py:377
  6.5 1.4 %copy-start = (bf16[8,48,512]{2,1,0:T(8,128)(2,1)S(1)}, bf16[8,48,512]{2,1,0:T(8,128)(2,1)}, u32[]{:S(2)}) copy-start(bf16[8,48,512]{2,1,0:T(8,128)(2,1)} %forcing.7) | copy-start | bytes 1179652
  6.5 1.5 %copy-start.1 = (f32[48,512]{1,0:T(8,128)S(1)}, f32[48,512]{1,0:T(8,128)}, u32[]{:S(2)}) copy-start(f32[48,512]{1,0:T(8,128)} %start.7) | copy-start | bytes 294916
  6.5 1.5 %copy-start.2 = (bf16[48,512]{1,0:T(8,128)(2,1)S(1)}, bf16[48,512]{1,0:T(8,128)(2,1)}, u32[]{:S(2)}) copy-start(bf16[48,512]{1,0:T(8,128)(2,1)} %velocity.7) | copy-start | bytes 147460
  6.5 1.5 %copy-start.3 = (bf16[48,512]{1,0:T(8,128)(2,1)S(1)}, bf16[48,512]{1,0:T(8,128)(2,1)}, u32[]{:S(2)}) copy-start(bf16[48,512]{1,0:T(8,128)(2,1)} %diffusion.7) | copy-start | bytes 147460
  10.2 7.6 %collective-permute-start.2 = (bf16[56,512]{1,0:T(8,128)(2,1)S(1)}, bf16[56,512]{1,0:T(8,128)(2,1)S(1)}, u32[]{:S(2)}, u32[]{:S(2)}) collective-permute-start(bf16[56,512]{1,0:T(8,128)(2,1)S(1)} %get-tuple-element.23), channel_id=1, source_target_pairs={{0,1},{1,2},{2,3},{3,0},{4,5},{5,6},{6,7},{7,4},{8,9},{9,10},{10,1... | collective-permute-start | bytes 172040 | tf_op jit(solution)/shard_map/ppermute | solution.py:389
  10.3 7.5 %collective-permute-start.3 = (bf16[56,512]{1,0:T(8,128)(2,1)S(1)}, bf16[56,512]{1,0:T(8,128)(2,1)S(1)}, u32[]{:S(2)}, u32[]{:S(2)}) collective-permute-start(bf16[56,512]{1,0:T(8,128)(2,1)S(1)} %get-tuple-element.24), channel_id=1, source_target_pairs={{0,3},{1,0},{2,1},{3,2},{4,7},{5,4},{6,5},{7,6},{8,11},{9,8},{10,9... | collective-permute-start | bytes 172040 | tf_op jit(solution)/shard_map/ppermute | solution.py:390
  39.4 6.2 %collective-permute-start.4 = (bf16[3,64,512]{2,1,0:T(8,128)(2,1)S(1)}, bf16[3,64,512]{2,1,0:T(8,128)(2,1)S(1)}, u32[]{:S(2)}, u32[]{:S(2)}) collective-permute-start(bf16[3,64,512]{2,1,0:T(8,128)(2,1)S(1)} %shard_map.71.psi), channel_id=1, source_target_pairs={{0,4},{4,0},{8,12},{12,8},{16,20},{20,16},{24,28},{28,24},{1,5},{5... | collective-permute-start | bytes 589832 | tf_op jit(solution)/shard_map/ppermute | solution.py:434
  39.8 5.8 %collective-permute-start.5 = (bf16[176,512]{1,0:T(8,128)(2,1)S(1)}, bf16[176,512]{1,0:T(8,128)(2,1)S(1)}, u32[]{:S(2)}, u32[]{:S(2)}) collective-permute-start(bf16[176,512]{1,0:T(8,128)(2,1)S(1)} %get-tuple-element.31), channel_id=1, source_target_pairs={{0,4},{4,8},{8,12},{12,16},{16,20},{20,24},{24,28},{28,0},{1,5},{5... | collective-permute-start | bytes 540680 | tf_op jit(solution)/shard_map/ppermute | solution.py:425
